TPU v7x, 256 devices: a whole 4x4x8 slice. The times are simulated.
256 devices in a mesh: pipe: 4 (over y), expert: 64 (over z, x, core).
Axes of the slice: x: 4, y: 4, z: 8, core: 2. Of those that a mesh axis runs over, the one named last changes fastest.
Arguments:
- upstream: bfloat16 [4, 8192, 3584], P('pipe', 'expert'), may hold values from -6 to 6
- routes: int32 [4, 8192, 8], P('pipe', 'expert'), may hold values from 0 to 63, all different within a row; in each aligned block of 128 rows (0 to 127, 128 to 255, ..., all dimensions but the last counted through in order) at most 20 rows name the same one
- affinity: float32 [4, 8192, 8], P('pipe', 'expert'), may hold values from 0.02 to 0.98
- w_down: bfloat16 [4, 64, 1024, 3584], P('pipe', 'expert'), may hold values from -0.1875 to 0.1875
- saved_hidden: bfloat16 [4, 64, 1280, 1024], P('pipe', 'expert'), may hold values from -0.29882812 to 0.29882812
Outputs:
- hidden_grad: bfloat16 [4, 64, 1280, 1024], P('pipe', 'expert')
- affinity_grad: float32 [4, 8192, 8], P('pipe', 'expert')
Inputs may be any that keep to these rules, and one draw needn't show every extreme that they name: `routes`: each token names 8 different experts. Within one device's block of 128 tokens of a section no expert is named by more than 20 tokens, and in some block one expert is named by exactly 20.
All inputs are finite; a program needn't handle non-finite values.
Results may differ from a plain program's by a relative error of at most 0.0049.
Values may be sent and summed in bfloat16 or wider, within the bound.
No kernel may reach another device: no remote copies, remote signals or barrier semaphores. Data moves between devices by JAX's collectives and lax.ppermute only.
A program may use at most 128 MiB of HBM per device.

v0:
```python
import jax
import jax.numpy as jnp
from jax import lax
from jax.sharding import PartitionSpec as P

SCALE_ROUTED = 2.5


def passed_along(block, axis, distance):
    devices = range(lax.axis_size(axis))
    route = [(i - distance, i) for i in devices if i - distance in devices]
    return lax.ppermute(block, axis, route)


def rank_slots(token_routes, experts_count):
    labels = jnp.arange(experts_count, dtype=jnp.int32)
    onehot = jnp.sum((token_routes[:, :, None] == labels).astype(jnp.int32), axis=1)
    before = jnp.cumsum(onehot, axis=0) - onehot
    return jnp.take_along_axis(before, token_routes, axis=1)


def on_device(upstream, routes, affinity, w_down, saved_hidden):
    sections = lax.axis_size("pipe")
    expert_count = lax.axis_size("expert")
    token_count = routes.shape[1]
    top_count = routes.shape[2]
    slot_total = saved_hidden.shape[2]
    capacity = slot_total // expert_count
    shifted = passed_along(upstream, "pipe", -1)
    incoming = jnp.where(lax.axis_index("pipe") == sections - 1, upstream, shifted)[0]
    token_routes = routes[0]
    weights_raw = affinity[0]
    totals = jnp.sum(weights_raw, axis=1)
    gate_weights = (SCALE_ROUTED * weights_raw / totals[:, None]).astype(jnp.bfloat16)
    rank_list = rank_slots(token_routes, expert_count)
    slot_flat = (token_routes * capacity + rank_list).reshape(-1)
    feature_count = incoming.shape[1]
    positions = jnp.arange(token_count * top_count, dtype=jnp.int32)
    source = (
        jnp.full((expert_count * capacity,), token_count * top_count, jnp.int32)
        .at[slot_flat]
        .set(positions)
    )
    padded_rows = jnp.concatenate([incoming, jnp.zeros((1, feature_count), jnp.bfloat16)], axis=0)
    padded_gains = jnp.concatenate(
        [gate_weights.reshape(-1), jnp.zeros((1,), jnp.bfloat16)], axis=0
    )
    send_rows = padded_rows[source // top_count].reshape(expert_count, capacity, feature_count)
    send_gains = padded_gains[source].reshape(expert_count, capacity)
    weight_one = w_down[0, 0]
    received, recv_gains = (
        lax.all_to_all(send_rows, "expert", split_axis=0, concat_axis=0, tiled=True),
        lax.all_to_all(send_gains, "expert", split_axis=0, concat_axis=0, tiled=True),
    )
    flat_rows = received.reshape(slot_total, feature_count)
    projected = lax.dot_general(
        flat_rows, weight_one, (((1,), (1,)), ((), ())), preferred_element_type=jnp.float32
    )
    hidden_grad = (recv_gains.reshape(-1).astype(jnp.float32)[:, None] * projected).astype(
        jnp.bfloat16
    )
    slot_scores = jnp.sum(projected * saved_hidden[0, 0].astype(jnp.float32), axis=1).reshape(
        expert_count, capacity
    )
    returned = lax.all_to_all(slot_scores, "expert", split_axis=0, concat_axis=0, tiled=True)
    gate_grad = returned.reshape(-1)[slot_flat].reshape(token_count, top_count)
    weighted_sum = jnp.sum(gate_weights.astype(jnp.float32) * gate_grad, axis=1)
    affinity_grad = (SCALE_ROUTED / totals)[:, None] * gate_grad - (weighted_sum / totals)[:, None]
    return (hidden_grad[None, None], affinity_grad[None])


def solution(mesh):
    return jax.shard_map(
        on_device,
        mesh=mesh,
        in_specs=(
            P("pipe", "expert", None),
            P("pipe", "expert", None),
            P("pipe", "expert", None),
            P("pipe", "expert", None, None),
            P("pipe", "expert", None, None),
        ),
        out_specs=(P("pipe", "expert", None, None), P("pipe", "expert", None)),
        check_vma=False,
    )
```

profile of v0, /device:TPU:1, one launch (start us, length us, event | category | flops | bytes accessed | tf_op | source)
XLA Modules:
  0.0 370.1 jit_solution(3213314655542548543)
XLA Ops:
  0.6 1.3 collective-permute-start
  1.9 0.7 fusion.9
  2.6 0.8 copy.27
  3.4 0.7 convert_reduce_fusion
  4.2 0.2 reduce_window_sum.11
  4.4 0.1 copy.30
  4.6 0.1 squeeze.13
  4.7 0.8 copy.26
  5.5 0.7 reduce_sum.36
  6.5 7.1 %gather_fusion.3 = s32[1024]{0:T(1024)S(1)} fusion(s32[128,64]{1,0:T(8,128)S(1)} %sub.24, s32[1024]{0:T(1024)S(1)} %reshape.246), kind=kCustom, calls=%fused_computation.3 | custom fusion | bytes 16384 | tf_op jit(solution)/shard_map/jit(take_along_axis)/gather | solution.py:19
  13.6 4.3 %scatter_custom_fusion = s32[1280]{0:T(1024)S(1)} fusion(s32[1024]{0:T(1024)S(1)} %bitcast.29, s32[1024]{0:T(1024)S(1)} %iota.7, s32[]{:T(128)} %constant.22.clone.1), kind=kCustom, calls=%fused_computation.40 | custom fusion | bytes 5124 | tf_op jit(solution)/shard_map/scatter | solution.py:42
  18.0 8.0 %gather_fusion = bf16[1280]{0:T(1024)(128)(2,1)S(1)} fusion(bf16[1025]{0:T(1024)(128)(2,1)S(1)} %pad_maximum_fusion, s32[2048]{0:T(1024)S(1)} %pad_clamp_fusion.1), kind=kCustom, calls=%fused_computation | custom fusion | bytes 10240 | tf_op jit(solution)/shard_map/gather | solution.py:49
  26.0 0.7 all_to_all.20
  26.7 13.0 %all-to-all-start = ((bf16[64,1,20]{2,1,0:T(2,128)(2,1)}), bf16[64,1,20]{2,1,0:T(2,128)(2,1)S(1)}, u32[]{:S(2)}, u32[]{:S(2)}) async-start(bf16[64,1,20]{2,1,0:T(2,128)(2,1)} %all_to_all.20), calls=%async_computation | async-start | bytes 65536 | tf_op jit(solution)/shard_map/all_to_all | solution.py:53
  39.8 0.1 select_bitcast_fusion
  39.9 7.9 %gather_fusion.1 = bf16[1280,3584]{1,0:T(8,128)(2,1)} fusion(bf16[129,3584]{1,0:T(8,128)(2,1)S(1)} %concatenate.7, s32[2048]{0:T(1024)S(1)} %pad_clamp_fusion), kind=kCustom, calls=%fused_computation.1 | custom fusion | bytes 18355200 | tf_op jit(solution)/shard_map/gather | solution.py:48
  47.9 13.1 %reshape.215 = bf16[64,20,3584]{2,1,0:T(8,128)(2,1)} reshape(bf16[1280,3584]{1,0:T(8,128)(2,1)} %gather_fusion.1) | data formatting | bytes 18350080 | tf_op jit(solution)/shard_map/reshape | solution.py:48
  61.0 10.6 %all-to-all-start.1 = ((bf16[64,20,3584]{2,1,0:T(8,128)(2,1)}), bf16[64,20,3584]{2,1,0:T(8,128)(2,1)}, u32[]{:S(2)}, u32[]{:S(2)}) async-start(bf16[64,20,3584]{2,1,0:T(8,128)(2,1)} %reshape.215), calls=%async_computation.1 | async-start | bytes 22020096 | tf_op jit(solution)/shard_map/all_to_all | solution.py:52
  71.6 2.7 copy.32
  74.5 236.5 %all-to-all-done.1 = bf16[64,20,3584]{2,1,0:T(8,128)(2,1)} async-done(((bf16[64,20,3584]{2,1,0:T(8,128)(2,1)}), bf16[64,20,3584]{2,1,0:T(8,128)(2,1)}, u32[]{:S(2)}, u32[]{:S(2)}) %all-to-all-start.1) | async-done | bytes 9175072 | tf_op jit(solution)/shard_map/all_to_all | solution.py:52
  311.0 13.2 %reshape.216 = bf16[1280,3584]{1,0:T(8,128)(2,1)} reshape(bf16[64,20,3584]{2,1,0:T(8,128)(2,1)} %all-to-all-done.1) | data formatting | bytes 18350080 | tf_op jit(solution)/shard_map/reshape | solution.py:55
  324.3 15.8 %fusion.2 = (f32[1280]{0:T(1024)S(1)}, bf16[1,1,1280,1024]{2,3,1,0:T(8,128)(2,1)}) fusion(bf16[1,1,1280,1024]{2,3,1,0:T(8,128)(2,1)S(1)} %copy-done.1, f32[1280]{0:T(1024)S(1)} %reshape.220, bf16[1280,3584]{1,0:T(8,128)(2,1)} %reshape.216, bf16[1,1,1024,3584]{3,2,1,0:T(8,128)(2,1)} %param.8), kind=kOutput, calls=%fused_computation.8 | convolution fusion | flops 9401793536 | bytes 21768192 | tf_op jit(solution)/shard_map/dot_general | solution.py:56
  340.0 0.7 all_to_all.18
  340.7 11.3 %all-to-all-start.2 = ((f32[64,1,20]{2,1,0:T(1,128)}), f32[64,1,20]{2,1,0:T(1,128)S(1)}, u32[]{:S(2)}, u32[]{:S(2)}) async-start(f32[64,1,20]{2,1,0:T(1,128)} %bitcast.8), calls=%async_computation.2 | async-start | bytes 65536 | tf_op jit(solution)/shard_map/all_to_all | solution.py:65
  352.1 4.4 %copy.34 = bf16[1,1,1280,1024]{3,2,1,0:T(8,128)(2,1)} copy(bf16[1,1,1280,1024]{2,3,1,0:T(8,128)(2,1)} %get-tuple-element.11) | data formatting | bytes 5242880
  356.5 5.0 %all-to-all-done.2 = f32[64,1,20]{2,1,0:T(1,128)S(1)} async-done(((f32[64,1,20]{2,1,0:T(1,128)}), f32[64,1,20]{2,1,0:T(1,128)S(1)}, u32[]{:S(2)}, u32[]{:S(2)}) %all-to-all-start.2) | async-done | bytes 5152 | tf_op jit(solution)/shard_map/all_to_all | solution.py:65
  361.5 0.5 broadcast.181
  362.0 0.7 reduce.8
  362.8 6.2 %gather_fusion.2 = f32[1024]{0:T(1024)S(1)} fusion(f32[1280]{0:T(1024)S(1)} %reshape.217, s32[1024]{0:T(1024)S(1)} %broadcast_clamp_fusion), kind=kCustom, calls=%fused_computation.2 | custom fusion | bytes 12288 | tf_op jit(solution)/shard_map/gather | solution.py:66
  369.1 0.2 multiply_reduce_fusion
  369.3 0.1 multiply_subtract_fusion
  369.5 0.7 copy.35
  (30 shorter events, 1.1 us)
Async XLA Ops:
  0.6 39.1 %collective-permute-start = (bf16[1,128,3584]{2,1,0:T(8,128)(2,1)}, bf16[1,128,3584]{2,1,0:T(8,128)(2,1)S(1)}, u32[]{:S(2)}, u32[]{:S(2)}) collective-permute-start(bf16[1,128,3584]{2,1,0:T(8,128)(2,1)} %param.5), channel_id=1, source_target_pairs={{64,0},{128,64},{192,128},{65,1},{129,65},{193,129},{66,2},{130,66... | collective-permute-start | bytes 2752520 | tf_op jit(solution)/shard_map/ppermute | solution.py:12
  6.5 33.3 %copy-start.2 = (bf16[1,128,3584]{2,1,0:T(8,128)(2,1)S(1)}, bf16[1,128,3584]{2,1,0:T(8,128)(2,1)}, u32[]{:S(2)}) copy-start(bf16[1,128,3584]{2,1,0:T(8,128)(2,1)} %param.5) | copy-start | bytes 2752516
  26.7 34.3 %all-to-all-start = ((bf16[64,1,20]{2,1,0:T(2,128)(2,1)}), bf16[64,1,20]{2,1,0:T(2,128)(2,1)S(1)}, u32[]{:S(2)}, u32[]{:S(2)}) async-start(bf16[64,1,20]{2,1,0:T(2,128)(2,1)} %all_to_all.20), calls=%async_computation | async-start | bytes 65536 | tf_op jit(solution)/shard_map/all_to_all | solution.py:53
  61.0 10.6 %copy-start = (bf16[1,1,1280,1024]{3,2,1,0:T(8,128)(2,1)S(1)}, bf16[1,1,1280,1024]{3,2,1,0:T(8,128)(2,1)}, u32[]{:S(2)}) copy-start(bf16[1,1,1280,1024]{3,2,1,0:T(8,128)(2,1)} %param.9) | copy-start | bytes 7864324
  61.0 250.0 %all-to-all-start.1 = ((bf16[64,20,3584]{2,1,0:T(8,128)(2,1)}), bf16[64,20,3584]{2,1,0:T(8,128)(2,1)}, u32[]{:S(2)}, u32[]{:S(2)}) async-start(bf16[64,20,3584]{2,1,0:T(8,128)(2,1)} %reshape.215), calls=%async_computation.1 | async-start | bytes 22020096 | tf_op jit(solution)/shard_map/all_to_all | solution.py:52
  74.5 249.7 %copy-start.1 = (bf16[1,1,1280,1024]{2,3,1,0:T(8,128)(2,1)S(1)}, bf16[1,1,1280,1024]{2,3,1,0:T(8,128)(2,1)}, u32[]{:S(2)}) copy-start(bf16[1,1,1280,1024]{2,3,1,0:T(8,128)(2,1)} %copy.32) | copy-start | bytes 7864324
  340.7 20.7 %all-to-all-start.2 = ((f32[64,1,20]{2,1,0:T(1,128)}), f32[64,1,20]{2,1,0:T(1,128)S(1)}, u32[]{:S(2)}, u32[]{:S(2)}) async-start(f32[64,1,20]{2,1,0:T(1,128)} %bitcast.8), calls=%async_computation.2 | async-start | bytes 65536 | tf_op jit(solution)/shard_map/all_to_all | solution.py:65
where the time goes:
time: 372 us; the launch traced here: 370 us
  waiting for transfers between devices  241 us (65%)
  local copies, waits for them, and re-layouts  72.1 us (19%)
  starting transfers between devices  36.2 us (10%)
  matrix products  15.8 us (4%)
    all_to_all x1, waiting for transfers between devices, on_device(): lax.all_to_all(send_rows, 'expert', split_axis=0, concat_axis=0, tiled=True)  237 us
    dot_general x1, matrix products, on_device(): lax.dot_general(flat_rows, weight_one, (((1,), (1,)), ((), ())), preferre...  15.8 us
    reshape x1, local copies, waits for them, and re-layouts, on_device(): flat_rows = received.reshape(slot_total, feature_count)  13.2 us
    reshape x1, local copies, waits for them, and re-layouts, on_device(): padded_rows[source // top_count]  13.1 us
    all_to_all x1, starting transfers between devices, on_device(): lax.all_to_all(send_gains, 'expert', split_axis=0, concat_axis=0, tiled=T...  13 us
    all_to_all x1, starting transfers between devices, on_device(): lax.all_to_all(slot_scores, 'expert', split_axis=0, concat_axis=0, tiled=...  11.3 us
    all_to_all x1, starting transfers between devices, on_device(): lax.all_to_all(send_rows, 'expert', split_axis=0, concat_axis=0, tiled=True)  10.6 us
    unnamed x11, local copies, waits for them, and re-layouts  9.33 us
  transfers between devices with their start and end apart: 4, of which 2 were waited for; matrix products, arithmetic and copies ran while one was open for 14% of the time, Pallas kernels for 0%

commit v1 on v0

v1 whole, which is shorter than its diff:
```python
from functools import partial

import jax
import jax.numpy as jnp
from jax import lax
from jax.experimental import pallas as pl
from jax.experimental.pallas import tpu as pltpu
from jax.sharding import Mesh, PartitionSpec as P

SCALE_ROUTED = 2.5
CORES = 2
COLUMNS = 4
LANES = 128
VMEM_BYTES = 48 * 2**20


def iota(shape, dim):
    return lax.broadcasted_iota(jnp.int32, shape, dim)


def call(body, out_shape, cost, **kwargs):
    return pl.pallas_call(
        body,
        out_shape=out_shape,
        cost_estimate=pl.CostEstimate(flops=cost[0], bytes_accessed=cost[1], transcendentals=0),
        compiler_params=pltpu.CompilerParams(vmem_limit_bytes=VMEM_BYTES),
        **kwargs,
    )


def ranks_before(hits):
    tokens = hits.shape[1]
    first, second = iota((tokens, tokens), 0), iota((tokens, tokens), 1)
    ahead = (first < second) & (first // LANES == second // LANES)
    ahead = jnp.where(ahead, 1.0, 0.0).astype(jnp.bfloat16)
    return jnp.dot(hits.astype(jnp.bfloat16), ahead, preferred_element_type=jnp.float32)


def gate_rows(affinity):
    total = jnp.sum(affinity, axis=0, keepdims=True)
    weights = (SCALE_ROUTED * affinity / total).astype(jnp.bfloat16).astype(jnp.float32)
    return total, weights


def routing_kernel(capacity, routes_ref, affinity_ref, gains_ref, slot_ref):
    experts = slot_ref.shape[0]
    _, weights = gate_rows(affinity_ref[...])
    labels = iota((experts, LANES), 0)
    hits = jnp.zeros((experts, LANES), jnp.float32)
    gains = jnp.zeros((experts, LANES), jnp.float32)
    for k in range(routes_ref.shape[0]):
        same = routes_ref[k : k + 1, :] == labels
        hits += jnp.where(same, 1.0, 0.0)
        gains += jnp.where(same, weights[k : k + 1, :], 0.0)
    slot = jnp.where(hits > 0, ranks_before(hits), -1.0).astype(jnp.int32)
    slot_ref[...] = slot
    lane = iota((experts, LANES), 1)
    table = jnp.zeros((experts, LANES), jnp.float32)
    for r in range(capacity):
        column = jnp.sum(jnp.where(slot == r, gains, 0.0), axis=1, keepdims=True)
        table = jnp.where(lane == r, column, table)
    gains_ref[...] = table


def select_kernel(parts, capacity, place_ref, *refs):
    routes = refs[: max(parts) + 1]
    blocks = refs[len(routes) : len(routes) + len(parts)]
    out_ref, onehot_ref = refs[-2:]
    rows, tokens = onehot_ref.shape[1:]
    experts = rows // (CORES * capacity)
    part = pl.program_id(0)

    @pl.when((part == 0) & (pl.program_id(1) == 0))
    def _():
        for i, routes_ref in enumerate(routes):
            labels = place_ref[0] * experts + iota((16, tokens), 0)
            hits = jnp.zeros((16, tokens), jnp.float32)
            for k in range(routes_ref.shape[0]):
                hits += jnp.where(routes_ref[k : k + 1, :] == labels, 1.0, 0.0)
            slot = ranks_before(hits).astype(jnp.int32) + (iota((16, tokens), 1) // LANES) * capacity
            slot = jnp.where(hits > 0, slot, -1)
            each = CORES * capacity
            order = iota((each, tokens), 0)
            for s in range(experts):
                mine = jnp.where(order == slot[s : s + 1, :], 1.0, 0.0)
                onehot_ref[i, s * each : (s + 1) * each, :] = mine

    for j, block_ref in enumerate(blocks):

        @pl.when(part == j)
        def _(j=j, block_ref=block_ref):
            out_ref[...] = jnp.dot(
                onehot_ref[parts[j]].astype(jnp.bfloat16),
                block_ref[...],
                preferred_element_type=jnp.float32,
            ).astype(jnp.bfloat16)


def select_rows(place, routes, blocks, parts, experts, capacity):
    tokens, width = blocks[0].shape
    rows = experts * CORES * capacity
    tile = width // 2
    count = len(blocks)

    def held(j):
        def index(h, n, place):
            return 0, jnp.where(h == j, n, jnp.where(h < j, 0, 1))

        return index

    def target(h, n, place):
        if count == 1:
            return 0, n
        return 0, jnp.where(h < 2, jnp.bitwise_xor(h, place[1]), h) * 2 + n

    whole = [pl.BlockSpec(r.shape, lambda h, n, place: (0, 0)) for r in routes]
    return call(
        partial(select_kernel, parts, capacity),
        jax.ShapeDtypeStruct((rows, width * count), jnp.bfloat16),
        (2 * rows * tokens * width * count, 2 * (rows + tokens) * width * count),
        grid_spec=pltpu.PrefetchScalarGridSpec(
            num_scalar_prefetch=1,
            grid=(count, 2),
            in_specs=whole + [pl.BlockSpec((tokens, tile), held(j)) for j in range(count)],
            out_specs=pl.BlockSpec((rows, tile), target),
            scratch_shapes=[pltpu.VMEM((len(routes), rows, tokens), jnp.float32)],
        ),
    )(place, *routes, *blocks)


def project_kernel(full, half, capacity, zs_ref, x_ref, w_ref, saved_ref, gains_ref, scores_in, *refs):
    hidden_ref, scores_ref, acc_ref, gain_ref, part_ref = refs[-5:]
    n, j = pl.program_id(0), pl.program_id(1)
    slots, width = acc_ref.shape[1:]
    each = CORES * capacity
    features = w_ref.shape[1]
    middle = features // 2
    dims = (((1,), (1,)), ((), ()))

    def times(x, w):
        return lax.dot_general(x, w, dims, preferred_element_type=jnp.float32)

    @pl.when(j == 0)
    def _():
        at = 0
        if full:
            y = times(x_ref[:, :features], w_ref[...])
            for c in range(CORES):
                for x in range(COLUMNS):
                    top = (x * CORES + c) * each
                    acc_ref[c, x * each : (x + 1) * each, :] = y[top : top + each]
            at = features
        if half:
            low = times(x_ref[:, at : at + middle], w_ref[:, :middle])
            high = times(x_ref[:, at : at + middle], w_ref[:, middle:])
            for x in range(COLUMNS):
                top = x * CORES * each
                acc_ref[CORES * full, x * each : (x + 1) * each, :] = (
                    low[top : top + each] + high[top + each : top + 2 * each]
                )

    @pl.when((n == 0) & (j == 0))
    def _():
        scores_ref[...] = scores_in[...]

    row = iota((slots, LANES), 0)
    lane = iota((slots, LANES), 1)
    sources = slots // capacity
    first = pl.multiple_of(zs_ref[j] * sources, sources)
    own_lane = lane == row % capacity

    @pl.when(n == 0)
    def _():
        table = gains_ref[pl.ds(first, sources), :]
        spread = jnp.zeros((slots, LANES), jnp.float32)
        for s in range(sources):
            spread = jnp.where(row // capacity == s, table[s : s + 1, :], spread)
        column = jnp.sum(jnp.where(own_lane, spread, 0.0), axis=1, keepdims=True)
        gain_ref[j] = jnp.broadcast_to(column, (slots, LANES))
        part_ref[j] = jnp.zeros((slots, LANES), jnp.float32)

    gain = gain_ref[j]
    total = part_ref[j]
    for i in range(width // LANES):
        lanes = slice(i * LANES, (i + 1) * LANES)
        projected = acc_ref[j, :, lanes]
        hidden_ref[0, :, lanes] = (gain * projected).astype(jnp.bfloat16)
        total += projected * saved_ref[0, :, lanes].astype(jnp.float32)
    part_ref[j] = total

    @pl.when(n == pl.num_programs(0) - 1)
    def _():
        column = jnp.sum(total, axis=1, keepdims=True)
        spread = jnp.where(own_lane, column, 0.0)
        place = iota((sources, LANES), 0)
        table = jnp.zeros((sources, LANES), jnp.float32)
        for s in range(sources):
            line = jnp.sum(jnp.where(row // capacity == s, spread, 0.0), axis=0, keepdims=True)
            table = jnp.where(place == s, line, table)
        scores_ref[pl.ds(first, sources), :] = table


def project(zs, rows, weight, saved, gains, scores, hidden, full, half, capacity):
    count = CORES * full + half
    blocks, slots, units = saved.shape
    features = weight.shape[1]
    width = 256
    constant = lambda n, j, zs: (0, 0)
    by_block = lambda n, j, zs: (zs[j], 0, n)
    in_specs = [
        pl.BlockSpec(rows.shape, constant),
        pl.BlockSpec((width, features), lambda n, j, zs: (n, 0)),
        pl.BlockSpec((1, slots, width), by_block),
        pl.BlockSpec(gains.shape, constant),
        pl.BlockSpec(scores.shape, constant),
    ]
    operands = [zs, rows, weight, saved, gains, scores]
    aliases = {}
    if hidden is not None:
        in_specs.append(pl.BlockSpec(memory_space=pl.ANY))
        aliases = {len(operands): 0}
        operands.append(hidden)
    return call(
        partial(project_kernel, full, half, capacity),
        (
            jax.ShapeDtypeStruct(saved.shape, jnp.bfloat16),
            jax.ShapeDtypeStruct(scores.shape, jnp.float32),
        ),
        (2 * rows.size * units, 2 * (rows.size + weight.size + 2 * count * slots * units)),
        grid_spec=pltpu.PrefetchScalarGridSpec(
            num_scalar_prefetch=1,
            grid=(units // width, count),
            in_specs=in_specs,
            out_specs=(pl.BlockSpec((1, slots, width), by_block), pl.BlockSpec(scores.shape, constant)),
            scratch_shapes=[
                pltpu.VMEM((count, slots, width), jnp.float32),
                pltpu.VMEM((count, slots, LANES), jnp.float32),
                pltpu.VMEM((count, slots, LANES), jnp.float32),
            ],
        ),
        input_output_aliases=aliases,
    )(*operands)


def gate_kernel(capacity, scores_ref, slot_ref, routes_ref, affinity_ref, out_ref):
    top = routes_ref.shape[0]
    total, weights = gate_rows(affinity_ref[...])
    slot = slot_ref[...]
    found = jnp.zeros(slot.shape, jnp.float32)
    for r in range(capacity):
        found = jnp.where(slot == r, scores_ref[:, r : r + 1], found)
    labels = iota(slot.shape, 0)
    place = iota((top, LANES), 0)
    grad = jnp.zeros((top, LANES), jnp.float32)
    for k in range(top):
        line = jnp.sum(jnp.where(routes_ref[k : k + 1, :] == labels, found, 0.0), axis=0, keepdims=True)
        grad = jnp.where(place == k, line, grad)
    weighted = jnp.sum(weights * grad, axis=0, keepdims=True)
    out_ref[...] = (SCALE_ROUTED / total) * grad - weighted / total


def on_device(upstream, routes, affinity, w_down, saved_hidden):
    sections, depth = lax.axis_size("pipe"), lax.axis_size("z")
    section, z, core = lax.axis_index("pipe"), lax.axis_index("z"), lax.axis_index("core")
    everyone = ("z", "x", "core")
    expert_count = depth * COLUMNS * CORES
    local = COLUMNS * CORES
    slot_total, units = saved_hidden.shape[2:]
    capacity = slot_total // expert_count
    tokens, features = upstream.shape[1:]
    half = features // 2
    cores = range(CORES)

    mine = lax.dynamic_slice(upstream[0], (0, core * half), (tokens, half))
    other = lax.dynamic_slice(upstream[0], (0, (1 - core) * half), (tokens, half))
    hop = range(1, sections)
    last = sections - 1
    near = lax.ppermute(mine, ("pipe", "core"), [(i * CORES + c, (i - 1) * CORES + c) for i in hop for c in cores])
    far = lax.ppermute(other, ("pipe", "core"), [(i * CORES + c, (i - 1) * CORES + 1 - c) for i in hop for c in cores])
    stay = lax.ppermute(other, ("pipe", "core"), [(last * CORES + c, last * CORES + 1 - c) for c in cores])

    routes_own = routes[0].T
    affinity_own = affinity[0].T
    routes_mate = lax.ppermute(routes_own, "core", [(c, 1 - c) for c in cores])

    def in_order(a, b, axis):
        return jnp.where(core == 0, jnp.concatenate([a, b], axis), jnp.concatenate([b, a], axis))

    def along(block, distance, cross=False):
        pairs = []
        for i in range(depth):
            pairs.append((i * CORES + (1 if cross else 0), (i + distance) % depth * CORES))
            pairs.append((i * CORES + (0 if cross else 1), (i - distance) % depth * CORES + 1))
        return lax.ppermute(block, ("z", "core"), pairs)

    reach = depth // 2
    routes_at = [in_order(routes_own, routes_mate, 1)]
    routes_at += [along(routes_at[0], k) for k in range(1, reach + 1)]

    gains, slot_of = call(
        partial(routing_kernel, capacity),
        (
            jax.ShapeDtypeStruct((expert_count, LANES), jnp.float32),
            jax.ShapeDtypeStruct((expert_count, LANES), jnp.int32),
        ),
        (10**6, 10**5),
    )(routes_own, affinity_own)

    def exchange(block, axes, parts):
        shape = block.shape
        block = block.reshape(parts, shape[0] // parts, shape[1])
        return lax.all_to_all(block, axes, split_axis=0, concat_axis=0, tiled=True).reshape(shape)

    gains = exchange(gains, everyone, expert_count)

    is_last = section == last
    held = in_order(jnp.where(is_last, mine, near), jnp.where(is_last, stay, far), 0)
    same, cross = [along(held, 1)], [along(held, 1, cross=True)]
    for k in range(1, reach):
        same.append(along(same[-1], 1))
        if k < reach - 1:
            cross.append(along(cross[-1], 1))

    place = jnp.stack([z, core])

    def columns(group_routes, blocks, parts):
        rows = select_rows(place, group_routes, blocks, parts, local, capacity)
        return exchange(rows, ("x", "core"), local)

    def at(*distances):
        return jnp.stack([(z + d) % depth for d in distances])

    weight = w_down[0, 0]
    saved = saved_hidden[0, 0].reshape(depth, slot_total // depth, units)
    scores = jnp.zeros((expert_count, LANES), jnp.float32)

    got = columns(routes_at[:1], [held], (0,))
    hidden, scores = project(at(0), got, weight, saved, gains, scores, None, 0, 1, capacity)
    for k in range(1, reach - 1):
        got = columns([routes_at[k]], [same[k - 1], cross[k - 1]], (0, 0))
        hidden, scores = project(at(-k, k), got, weight, saved, gains, scores, hidden, 1, 0, capacity)
    k = reach - 1
    got = columns(routes_at[k:], [same[k - 1], cross[k - 1], same[k]], (0, 0, 1))
    hidden, scores = project(at(-k, k, reach), got, weight, saved, gains, scores, hidden, 1, 1, capacity)

    returned = exchange(scores, everyone, expert_count)
    affinity_grad = call(
        partial(gate_kernel, capacity),
        jax.ShapeDtypeStruct(affinity_own.shape, jnp.float32),
        (10**6, 10**5),
    )(returned, slot_of, routes_own, affinity_own)
    return hidden.reshape(1, 1, slot_total, units), affinity_grad.T[None]


def solution(mesh):
    sections, experts = mesh.devices.shape
    grid = mesh.devices.reshape(sections, experts // (COLUMNS * CORES), COLUMNS, CORES)
    rows = ("z", "x", "core")
    return jax.shard_map(
        on_device,
        mesh=Mesh(grid, ("pipe",) + rows),
        in_specs=(
            P("pipe", rows, None),
            P("pipe", rows, None),
            P("pipe", rows, None),
            P("pipe", rows, None, None),
            P("pipe", rows, None, None),
        ),
        out_specs=(P("pipe", rows, None, None), P("pipe", rows, None)),
        check_vma=False,
    )
```

time: 372 us -> 229 us (0.62)
  waiting for transfers between devices: 241 us -> 78.1 us
  local copies, waits for them, and re-layouts: 72.1 us -> 7.22 us
  Pallas kernels: 0 us -> 64 us
  starting transfers between devices: 36.2 us -> 62 us
  matrix products: 15.8 us -> 0 us
  blocking collectives: 0 us -> 14.3 us
    all_to_all x3 -> x5, waiting for transfers between devices: 241 us -> 11.5 us  [exchange(): lax.all_to_all(block, axes, split_axis=0, concat_axis=0, tiled=True)]
    ppermute x1 -> x15, waiting for transfers between devices: 0.01 us -> 66.7 us  [the longest x11 60.8 us: along(): return lax.ppermute(block, ('z', 'core'), pairs)]
    pallas_call x0 -> x10, Pallas kernels: none -> 64 us  [the longest x4 48.6 us: project(): call(partial(project_kernel, full, half, capacity), (jax.ShapeDtypeStruct...]
    gather x6 -> x0, local copies, waits for them, and re-layouts: 29.3 us -> none  [the longest x1 7.97 us: on_device(): send_gains = padded_gains[source].reshape(expert_count, capacity)]
    reshape x5 -> x0, local copies, waits for them, and re-layouts: 26.6 us -> none  [the longest x1 13.2 us: on_device(): flat_rows = received.reshape(slot_total, feature_count)]
    ppermute x1 -> x15, starting transfers between devices: 1.29 us -> 24.3 us  [the longest x11 17.7 us: along(): return lax.ppermute(block, ('z', 'core'), pairs)]
    dot_general x1 -> x0, matrix products: 15.8 us -> none  [on_device(): lax.dot_general(flat_rows, weight_one, (((1,), (1,)), ((), ())), preferre...]
    all_to_all x0 -> x1, blocking collectives: none -> 14.3 us  [exchange(): lax.all_to_all(block, axes, split_axis=0, concat_axis=0, tiled=True)]
  transfers between devices with their start and end apart: 4 -> 20, of which waited for: 2 -> 9; matrix products, arithmetic and copies ran while one was open for 14% -> 0% of each run, Pallas kernels for 0% -> 20%
where the time goes in v1:
time: 229 us; the launch traced here: 227 us
  waiting for transfers between devices  78.1 us (34%)
  Pallas kernels  64 us (28%)
  starting transfers between devices  62 us (27%)
  blocking collectives  14.3 us (6%)
  local copies, waits for them, and re-layouts  7.22 us (3%)
    ppermute x11, waiting for transfers between devices, along(): return lax.ppermute(block, ('z', 'core'), pairs)  60.8 us
    pallas_call x4, Pallas kernels, project(): call(partial(project_kernel, full, half, capacity), (jax.ShapeDtypeStruct...  48.6 us
    all_to_all x5, starting transfers between devices, exchange(): lax.all_to_all(block, axes, split_axis=0, concat_axis=0, tiled=True)  37.7 us
    ppermute x11, starting transfers between devices, along(): return lax.ppermute(block, ('z', 'core'), pairs)  17.7 us
    all_to_all x1, blocking collectives, exchange(): lax.all_to_all(block, axes, split_axis=0, concat_axis=0, tiled=True)  14.3 us
    pallas_call x4, Pallas kernels, select_rows(): call(partial(select_kernel, parts, capacity), jax.ShapeDtypeStruct((rows,...  13.5 us
    all_to_all x5, waiting for transfers between devices, exchange(): lax.all_to_all(block, axes, split_axis=0, concat_axis=0, tiled=True)  11.5 us
    unnamed x32, local copies, waits for them, and re-layouts  6 us
  transfers between devices with their start and end apart: 20, of which 9 were waited for; matrix products, arithmetic and copies ran while one was open for 0% of the time, Pallas kernels for 20%

profile of v1, /device:TPU:1, one launch (start us, length us, event | category | flops | bytes accessed | tf_op | source)
XLA Modules:
  0.0 227.0 jit_solution(7801111080663298254)
XLA Ops:
  0.6 1.2 dynamic-slice_bitcast_fusion.1
  1.9 1.3 collective-permute-start.3
  3.9 1.3 collective-permute-start.5
  5.2 3.3 %collective-permute-start = (s32[8,128]{1,0:T(8,128)}, s32[8,128]{1,0:T(8,128)S(1)}, u32[]{:S(2)}, u32[]{:S(2)}) collective-permute-start(s32[8,128]{1,0:T(8,128)} %bitcast.52), channel_id=1, source_target_pairs={{0,1},{1,0},{2,3},{3,2},{4,5},{5,4},{6,7},{7,6},{8,9},{9,8},{10,11... | collective-permute-start | bytes 12296 | tf_op jit(solution)/shard_map/ppermute | solution.py:284
  10.9 9.9 %all-to-all-start.1 = ((f32[64,1,128]{2,1,0:T(1,128)}), f32[64,1,128]{2,1,0:T(1,128)S(1)}, u32[]{:S(2)}, u32[]{:S(2)}) async-start(f32[64,1,128]{2,1,0:T(1,128)} %bitcast.17), calls=%async_computation.1 | async-start | bytes 65536 | tf_op jit(solution)/shard_map/all_to_all | solution.py:312
  20.9 5.9 %collective-permute-done.5 = bf16[128,1792]{1,0:T(8,128)(2,1)S(1)} collective-permute-done((bf16[128,1792]{1,0:T(8,128)(2,1)S(1)}, bf16[128,1792]{1,0:T(8,128)(2,1)S(1)}, u32[]{:S(2)}, u32[]{:S(2)}) %collective-permute-start.5) | collective-permute-done | bytes 458784 | tf_op jit(solution)/shard_map/ppermute | solution.py:279
  27.1 2.3 %shard_map.72 = bf16[320,1792]{1,0:T(8,128)(2,1)} custom-call(s32[2]{0:T(128)S(1)} %pad_add_fusion.1.place_ref, s32[8,256]{1,0:T(8,128)S(1)} %add_select_fusion.refs_0_, bf16[256,1792]{1,0:T(8,128)(2,1)S(1)} %maximum_select_fusion.refs_1_), custom_call_target="tpu_custom_call" | custom-call | flops 293601280 | bytes 2064384 | tf_op jit(solution)/shard_map/pallas_call | solution.py:117
  30.1 4.8 %all-to-all-start.4 = ((bf16[8,40,1792]{2,1,0:T(8,128)(2,1)}), bf16[8,40,1792]{2,1,0:T(8,128)(2,1)}, u32[]{:S(2)}, u32[]{:S(2)}) async-start(bf16[8,40,1792]{2,1,0:T(8,128)(2,1)} %bitcast.28), calls=%async_computation.4 | async-start | bytes 2293760 | tf_op jit(solution)/shard_map/all_to_all | solution.py:312
  35.0 4.3 %collective-permute-start.6 = (bf16[256,1792]{1,0:T(8,128)(2,1)S(1)}, bf16[256,1792]{1,0:T(8,128)(2,1)S(1)}, u32[]{:S(2)}, u32[]{:S(2)}) collective-permute-start(bf16[256,1792]{1,0:T(8,128)(2,1)S(1)} %maximum_select_fusion.refs_1_), channel_id=1, source_target_pairs={{0,8},{1,57},{8,16},{9,1},{16,24},{17,9},{24,32},{25,17},{32,40},{... | collective-permute-start | bytes 2752520 | tf_op jit(solution)/shard_map/ppermute | solution.py:294
  40.0 18.2 %collective-permute-done.14.refs_0_ = s32[8,256]{1,0:T(8,128)S(1)} collective-permute-done((s32[8,256]{1,0:T(8,128)S(1)}, s32[8,256]{1,0:T(8,128)S(1)}, u32[]{:S(2)}, u32[]{:S(2)}) %collective-permute-start.14) | collective-permute-done | bytes 8224 | tf_op jit(solution)/shard_map/ppermute | solution.py:294
  58.3 3.7 %shard_map.71 = bf16[320,3584]{1,0:T(8,128)(2,1)} custom-call(s32[2]{0:T(128)S(1)} %pad_add_fusion.1.place_ref, s32[8,256]{1,0:T(8,128)S(1)} %collective-permute-done.14.refs_0_, bf16[256,1792]{1,0:T(8,128)(2,1)S(1)} %collective-permute-done.6.refs_1_, bf16[256,1792]{1,0:T(8,128)(2,1)S(1)} %collective-permute-done.9.refs_2_), custom_call_target="tpu_custom_call" | custom-call | flops 587202560 | bytes 4128768 | tf_op jit(solution)/shard_map/pallas_call | solution.py:117
  63.9 7.5 %all-to-all-start.3 = ((bf16[8,40,3584]{2,1,0:T(8,128)(2,1)}), bf16[8,40,3584]{2,1,0:T(8,128)(2,1)}, u32[]{:S(2)}, u32[]{:S(2)}) async-start(bf16[8,40,3584]{2,1,0:T(8,128)(2,1)} %bitcast.25), calls=%async_computation.3 | async-start | bytes 4587520 | tf_op jit(solution)/shard_map/all_to_all | solution.py:312
  71.4 1.5 collective-permute-start.10
  73.8 2.4 %collective-permute-start.13 = (s32[8,256]{1,0:T(8,128)S(1)}, s32[8,256]{1,0:T(8,128)S(1)}, u32[]{:S(2)}, u32[]{:S(2)}) collective-permute-start(s32[8,256]{1,0:T(8,128)S(1)} %add_select_fusion.refs_0_), channel_id=1, source_target_pairs={{0,16},{1,49},{8,24},{9,57},{16,32},{17,1},{24,40},{25,9},{32,48},... | collective-permute-start | bytes 24584 | tf_op jit(solution)/shard_map/ppermute | solution.py:294
  76.2 17.0 %collective-permute-done.13.refs_0_ = s32[8,256]{1,0:T(8,128)S(1)} collective-permute-done((s32[8,256]{1,0:T(8,128)S(1)}, s32[8,256]{1,0:T(8,128)S(1)}, u32[]{:S(2)}, u32[]{:S(2)}) %collective-permute-start.13) | collective-permute-done | bytes 8224 | tf_op jit(solution)/shard_map/ppermute | solution.py:294
  93.8 3.7 %shard_map.70 = bf16[320,3584]{1,0:T(8,128)(2,1)} custom-call(s32[2]{0:T(128)S(1)} %pad_add_fusion.1.place_ref, s32[8,256]{1,0:T(8,128)S(1)} %collective-permute-done.13.refs_0_, bf16[256,1792]{1,0:T(8,128)(2,1)S(1)} %collective-permute-done.7.refs_1_, bf16[256,1792]{1,0:T(8,128)(2,1)S(1)} %collective-permute-done.10.refs_2_), custom_call_target="tpu_custom_call" | custom-call | flops 587202560 | bytes 4128768 | tf_op jit(solution)/shard_map/pallas_call | solution.py:117
  98.4 1.5 all-to-all-done.3
  99.9 5.6 %all-to-all-start.2 = ((bf16[8,40,3584]{2,1,0:T(8,128)(2,1)}), bf16[8,40,3584]{2,1,0:T(8,128)(2,1)}, u32[]{:S(2)}, u32[]{:S(2)}) async-start(bf16[8,40,3584]{2,1,0:T(8,128)(2,1)} %bitcast.21), calls=%async_computation.2 | async-start | bytes 4587520 | tf_op jit(solution)/shard_map/all_to_all | solution.py:312
  105.5 1.2 collective-permute-start.8
  107.7 10.5 %collective-permute-done.8.refs_2_ = bf16[256,1792]{1,0:T(8,128)(2,1)S(1)} collective-permute-done((bf16[256,1792]{1,0:T(8,128)(2,1)S(1)}, bf16[256,1792]{1,0:T(8,128)(2,1)S(1)}, u32[]{:S(2)}, u32[]{:S(2)}) %collective-permute-start.8) | collective-permute-done | bytes 917536 | tf_op jit(solution)/shard_map/ppermute | solution.py:294
  118.2 2.4 %collective-permute-start.12 = (bf16[256,1792]{1,0:T(8,128)(2,1)S(1)}, bf16[256,1792]{1,0:T(8,128)(2,1)S(1)}, u32[]{:S(2)}, u32[]{:S(2)}) collective-permute-start(bf16[256,1792]{1,0:T(8,128)(2,1)S(1)} %collective-permute-done.8.refs_2_), channel_id=1, source_target_pairs={{0,8},{1,57},{8,16},{9,1},{16,24},{17,9},{24,32},{25,17},{32,40},{... | collective-permute-start | bytes 2752520 | tf_op jit(solution)/shard_map/ppermute | solution.py:294
  120.6 2.1 collective-permute-start.1
  123.8 14.4 %collective-permute-done.1.refs_0_ = s32[8,256]{1,0:T(8,128)S(1)} collective-permute-done((s32[8,256]{1,0:T(8,128)S(1)}, s32[8,256]{1,0:T(8,128)S(1)}, u32[]{:S(2)}, u32[]{:S(2)}) %collective-permute-start.1) | collective-permute-done | bytes 8224 | tf_op jit(solution)/shard_map/ppermute | solution.py:294
  138.3 3.8 %shard_map.68 = bf16[320,5376]{1,0:T(8,128)(2,1)S(1)} custom-call(s32[2]{0:T(128)S(1)} %pad_add_fusion.1.place_ref, s32[8,256]{1,0:T(8,128)S(1)} %collective-permute-done.1.refs_0_, s32[8,256]{1,0:T(8,128)S(1)} %collective-permute-done.2.refs_1_, bf16[256,1792]{1,0:T(8,128)(2,1)S(1)} %collective-permute-done.8.refs_2_, ...), custom_call_target="tpu_custom_call" | custom-call | flops 880803840 | bytes 6193152 | tf_op jit(solution)/shard_map/pallas_call | solution.py:117
  142.1 1.8 copy-done.1
  143.9 9.9 %all-to-all-start = ((bf16[8,40,5376]{2,1,0:T(8,128)(2,1)}), bf16[8,40,5376]{2,1,0:T(8,128)(2,1)}, u32[]{:S(2)}, u32[]{:S(2)}) async-start(bf16[8,40,5376]{2,1,0:T(8,128)(2,1)} %bitcast.46), calls=%async_computation | async-start | bytes 6881280 | tf_op jit(solution)/shard_map/all_to_all | solution.py:312
  154.0 7.1 %shard_map.73 = (bf16[8,160,1024]{2,1,0:T(8,128)(2,1)}, f32[64,128]{1,0:T(8,128)S(1)}) custom-call(s32[1]{0:T(128)} %bitcast.27.zs_ref, bf16[320,1792]{1,0:T(8,128)(2,1)} %bitcast.29.x_ref, bf16[1024,3584]{1,0:T(8,128)(2,1)} %bitcast.59, bf16[8,160,1024]{2,1,0:T(8,128)(2,1)S(1)} %bitcast.42, f32[64,128]{1,0:T(8,128)S(1)} %bitcast.47, ...), custom_call_target="tpu_custom_call" | custom-call | flops 1174405120 | bytes 9142272 | tf_op jit(solution)/shard_map/pallas_call | solution.py:223
  161.1 12.2 %shard_map.74 = (bf16[8,160,1024]{2,1,0:T(8,128)(2,1)}, f32[64,128]{1,0:T(8,128)S(1)}) custom-call(s32[2]{0:T(128)S(1)} %pad_add_fusion.3.zs_ref, bf16[320,3584]{1,0:T(8,128)(2,1)} %bitcast.26.x_ref, bf16[1024,3584]{1,0:T(8,128)(2,1)} %bitcast.60, bf16[8,160,1024]{2,1,0:T(8,128)(2,1)S(1)} %bitcast.43, ...), custom_call_target="tpu_custom_call", output_to_operand_aliasing={{0}: (6, {})} | custom-call | flops 2348810240 | bytes 10944512 | tf_op jit(solution)/shard_map/pallas_call | solution.py:223
  173.2 12.2 %shard_map.75 = (bf16[8,160,1024]{2,1,0:T(8,128)(2,1)}, f32[64,128]{1,0:T(8,128)S(1)}) custom-call(s32[2]{0:T(128)S(1)} %pad_add_fusion.2.zs_ref, bf16[320,3584]{1,0:T(8,128)(2,1)} %bitcast.22.x_ref, bf16[1024,3584]{1,0:T(8,128)(2,1)} %bitcast.61, bf16[8,160,1024]{2,1,0:T(8,128)(2,1)S(1)} %bitcast.44, ...), custom_call_target="tpu_custom_call", output_to_operand_aliasing={{0}: (6, {})} | custom-call | flops 2348810240 | bytes 10944512 | tf_op jit(solution)/shard_map/pallas_call | solution.py:223
  185.4 9.2 %all-to-all-done = bf16[8,40,5376]{2,1,0:T(8,128)(2,1)} async-done(((bf16[8,40,5376]{2,1,0:T(8,128)(2,1)}), bf16[8,40,5376]{2,1,0:T(8,128)(2,1)}, u32[]{:S(2)}, u32[]{:S(2)}) %all-to-all-start) | async-done | bytes 3440672 | tf_op jit(solution)/shard_map/all_to_all | solution.py:312
  194.6 17.2 %shard_map.76 = (bf16[8,160,1024]{2,1,0:T(8,128)(2,1)}, f32[64,128]{1,0:T(8,128)S(1)}) custom-call(s32[3]{0:T(128)S(1)} %pad_add_fusion.zs_ref, bf16[320,5376]{1,0:T(8,128)(2,1)} %bitcast.11.x_ref, bf16[1024,3584]{1,0:T(8,128)(2,1)} %bitcast.62, bf16[8,160,1024]{2,1,0:T(8,128)(2,1)S(1)} %bitcast.45, ...), custom_call_target="tpu_custom_call", output_to_operand_aliasing={{0}: (6, {})} | custom-call | flops 3523215360 | bytes 12746752 | tf_op jit(solution)/shard_map/pallas_call | solution.py:223
  211.8 14.3 %all_to_all.30 = f32[64,1,128]{2,1,0:T(1,128)S(1)} all-to-all(f32[64,1,128]{2,1,0:T(1,128)S(1)} %bitcast.56), channel_id=1, replica_groups=mesh['pipe'=4,'z'=8,'x'=4,'core'=2] {'z','x','core'}, dimensions={0} | all-to-all | bytes 65536 | tf_op jit(solution)/shard_map/all_to_all | solution.py:312
  (61 shorter events, 12.6 us)
Async XLA Ops:
  1.9 19.0 %collective-permute-start.3 = (bf16[128,1792]{1,0:T(8,128)(2,1)S(1)}, bf16[128,1792]{1,0:T(8,128)(2,1)S(1)}, u32[]{:S(2)}, u32[]{:S(2)}) collective-permute-start(bf16[128,1792]{1,0:T(8,128)(2,1)S(1)} %get-tuple-element.22), channel_id=1, source_target_pairs={{64,0},{65,1},{128,64},{129,65},{192,128},{193,129},{66,2},{67,3},... | collective-permute-start | bytes 1376264 | tf_op jit(solution)/shard_map/ppermute | solution.py:278
  3.2 17.8 %collective-permute-start.4 = (bf16[128,1792]{1,0:T(8,128)(2,1)S(1)}, bf16[128,1792]{1,0:T(8,128)(2,1)S(1)}, u32[]{:S(2)}, u32[]{:S(2)}) collective-permute-start(bf16[128,1792]{1,0:T(8,128)(2,1)S(1)} %get-tuple-element.23), channel_id=1, source_target_pairs={{192,193},{193,192},{194,195},{195,194},{196,197},{197,196},{198,1... | collective-permute-start | bytes 1376264 | tf_op jit(solution)/shard_map/ppermute | solution.py:280
  3.9 22.9 %collective-permute-start.5 = (bf16[128,1792]{1,0:T(8,128)(2,1)S(1)}, bf16[128,1792]{1,0:T(8,128)(2,1)S(1)}, u32[]{:S(2)}, u32[]{:S(2)}) collective-permute-start(bf16[128,1792]{1,0:T(8,128)(2,1)S(1)} %get-tuple-element.23), channel_id=1, source_target_pairs={{64,1},{65,0},{128,65},{129,64},{192,129},{193,128},{66,3},{67,2},... | collective-permute-start | bytes 1376264 | tf_op jit(solution)/shard_map/ppermute | solution.py:279
  5.2 15.7 %collective-permute-start = (s32[8,128]{1,0:T(8,128)}, s32[8,128]{1,0:T(8,128)S(1)}, u32[]{:S(2)}, u32[]{:S(2)}) collective-permute-start(s32[8,128]{1,0:T(8,128)} %bitcast.52), channel_id=1, source_target_pairs={{0,1},{1,0},{2,3},{3,2},{4,5},{5,4},{6,7},{7,6},{8,9},{9,8},{10,11... | collective-permute-start | bytes 12296 | tf_op jit(solution)/shard_map/ppermute | solution.py:284
  10.9 15.9 %copy-start.12 = (s32[64,128]{1,0:T(8,128)}, s32[64,128]{1,0:T(8,128)S(1)}, u32[]{:S(2)}) copy-start(s32[64,128]{1,0:T(8,128)S(1)} %get-tuple-element.21.slot_ref) | copy-start | bytes 98308
  10.9 19.3 %all-to-all-start.1 = ((f32[64,1,128]{2,1,0:T(1,128)}), f32[64,1,128]{2,1,0:T(1,128)S(1)}, u32[]{:S(2)}, u32[]{:S(2)}) async-start(f32[64,1,128]{2,1,0:T(1,128)} %bitcast.17), calls=%async_computation.1 | async-start | bytes 65536 | tf_op jit(solution)/shard_map/all_to_all | solution.py:312
  30.1 28.1 %copy-start.8 = (f32[64,1,128]{2,1,0:T(1,128)}, f32[64,1,128]{2,1,0:T(1,128)S(1)}, u32[]{:S(2)}) copy-start(f32[64,1,128]{2,1,0:T(1,128)S(1)} %all-to-all-done.1) | copy-start | bytes 98308
  30.1 33.7 %all-to-all-start.4 = ((bf16[8,40,1792]{2,1,0:T(8,128)(2,1)}), bf16[8,40,1792]{2,1,0:T(8,128)(2,1)}, u32[]{:S(2)}, u32[]{:S(2)}) async-start(bf16[8,40,1792]{2,1,0:T(8,128)(2,1)} %bitcast.28), calls=%async_computation.4 | async-start | bytes 2293760 | tf_op jit(solution)/shard_map/all_to_all | solution.py:312
  35.0 23.3 %collective-permute-start.6 = (bf16[256,1792]{1,0:T(8,128)(2,1)S(1)}, bf16[256,1792]{1,0:T(8,128)(2,1)S(1)}, u32[]{:S(2)}, u32[]{:S(2)}) collective-permute-start(bf16[256,1792]{1,0:T(8,128)(2,1)S(1)} %maximum_select_fusion.refs_1_), channel_id=1, source_target_pairs={{0,8},{1,57},{8,16},{9,1},{16,24},{17,9},{24,32},{25,17},{32,40},{... | collective-permute-start | bytes 2752520 | tf_op jit(solution)/shard_map/ppermute | solution.py:294
  39.3 19.0 %collective-permute-start.9 = (bf16[256,1792]{1,0:T(8,128)(2,1)S(1)}, bf16[256,1792]{1,0:T(8,128)(2,1)S(1)}, u32[]{:S(2)}, u32[]{:S(2)}) collective-permute-start(bf16[256,1792]{1,0:T(8,128)(2,1)S(1)} %maximum_select_fusion.refs_1_), channel_id=1, source_target_pairs={{1,8},{0,57},{9,16},{8,1},{17,24},{16,9},{25,32},{24,17},{33,40},{... | collective-permute-start | bytes 2752520 | tf_op jit(solution)/shard_map/ppermute | solution.py:294
  39.3 19.0 %collective-permute-start.14 = (s32[8,256]{1,0:T(8,128)S(1)}, s32[8,256]{1,0:T(8,128)S(1)}, u32[]{:S(2)}, u32[]{:S(2)}) collective-permute-start(s32[8,256]{1,0:T(8,128)S(1)} %add_select_fusion.refs_0_), channel_id=1, source_target_pairs={{0,8},{1,57},{8,16},{9,1},{16,24},{17,9},{24,32},{25,17},{32,40},{... | collective-permute-start | bytes 24584 | tf_op jit(solution)/shard_map/ppermute | solution.py:294
  62.0 0.9 copy-start.2
  63.9 7.5 %copy-start.5 = (bf16[256,1792]{1,0:T(8,128)(2,1)S(1)}, bf16[256,1792]{1,0:T(8,128)(2,1)}, u32[]{:S(2)}) copy-start(bf16[256,1792]{1,0:T(8,128)(2,1)} %copy-done.4) | copy-start | bytes 2752516
  63.9 9.1 %copy-start.3 = (bf16[256,1792]{1,0:T(8,128)(2,1)S(1)}, bf16[256,1792]{1,0:T(8,128)(2,1)}, u32[]{:S(2)}) copy-start(bf16[256,1792]{1,0:T(8,128)(2,1)} %copy-done.2) | copy-start | bytes 2752516
  63.9 36.1 %all-to-all-start.3 = ((bf16[8,40,3584]{2,1,0:T(8,128)(2,1)}), bf16[8,40,3584]{2,1,0:T(8,128)(2,1)}, u32[]{:S(2)}, u32[]{:S(2)}) async-start(bf16[8,40,3584]{2,1,0:T(8,128)(2,1)} %bitcast.25), calls=%async_computation.3 | async-start | bytes 4587520 | tf_op jit(solution)/shard_map/all_to_all | solution.py:312
  71.4 21.9 %collective-permute-start.10 = (bf16[256,1792]{1,0:T(8,128)(2,1)S(1)}, bf16[256,1792]{1,0:T(8,128)(2,1)S(1)}, u32[]{:S(2)}, u32[]{:S(2)}) collective-permute-start(bf16[256,1792]{1,0:T(8,128)(2,1)S(1)} %copy-done.5), channel_id=1, source_target_pairs={{0,8},{1,57},{8,16},{9,1},{16,24},{17,9},{24,32},{25,17},{32,40},{... | collective-permute-start | bytes 2752520 | tf_op jit(solution)/shard_map/ppermute | solution.py:294
  72.9 20.9 %collective-permute-start.7 = (bf16[256,1792]{1,0:T(8,128)(2,1)S(1)}, bf16[256,1792]{1,0:T(8,128)(2,1)S(1)}, u32[]{:S(2)}, u32[]{:S(2)}) collective-permute-start(bf16[256,1792]{1,0:T(8,128)(2,1)S(1)} %copy-done.3), channel_id=1, source_target_pairs={{0,8},{1,57},{8,16},{9,1},{16,24},{17,9},{24,32},{25,17},{32,40},{... | collective-permute-start | bytes 2752520 | tf_op jit(solution)/shard_map/ppermute | solution.py:294
  73.8 19.4 %collective-permute-start.13 = (s32[8,256]{1,0:T(8,128)S(1)}, s32[8,256]{1,0:T(8,128)S(1)}, u32[]{:S(2)}, u32[]{:S(2)}) collective-permute-start(s32[8,256]{1,0:T(8,128)S(1)} %add_select_fusion.refs_0_), channel_id=1, source_target_pairs={{0,16},{1,49},{8,24},{9,57},{16,32},{17,1},{24,40},{25,9},{32,48},... | collective-permute-start | bytes 24584 | tf_op jit(solution)/shard_map/ppermute | solution.py:294
  99.9 5.6 %copy-start.7 = (bf16[256,1792]{1,0:T(8,128)(2,1)S(1)}, bf16[256,1792]{1,0:T(8,128)(2,1)}, u32[]{:S(2)}) copy-start(bf16[256,1792]{1,0:T(8,128)(2,1)} %copy-done.6) | copy-start | bytes 2752516
  99.9 43.9 %all-to-all-start.2 = ((bf16[8,40,3584]{2,1,0:T(8,128)(2,1)}), bf16[8,40,3584]{2,1,0:T(8,128)(2,1)}, u32[]{:S(2)}, u32[]{:S(2)}) async-start(bf16[8,40,3584]{2,1,0:T(8,128)(2,1)} %bitcast.21), calls=%async_computation.2 | async-start | bytes 4587520 | tf_op jit(solution)/shard_map/all_to_all | solution.py:312
  105.5 12.6 %collective-permute-start.8 = (bf16[256,1792]{1,0:T(8,128)(2,1)S(1)}, bf16[256,1792]{1,0:T(8,128)(2,1)S(1)}, u32[]{:S(2)}, u32[]{:S(2)}) collective-permute-start(bf16[256,1792]{1,0:T(8,128)(2,1)S(1)} %copy-done.7), channel_id=1, source_target_pairs={{0,8},{1,57},{8,16},{9,1},{16,24},{17,9},{24,32},{25,17},{32,40},{... | collective-permute-start | bytes 2752520 | tf_op jit(solution)/shard_map/ppermute | solution.py:294
  106.7 31.6 %collective-permute-start.11 = (bf16[256,1792]{1,0:T(8,128)(2,1)S(1)}, bf16[256,1792]{1,0:T(8,128)(2,1)S(1)}, u32[]{:S(2)}, u32[]{:S(2)}) collective-permute-start(bf16[256,1792]{1,0:T(8,128)(2,1)S(1)} %collective-permute-done.10.refs_2_), channel_id=1, source_target_pairs={{0,8},{1,57},{8,16},{9,1},{16,24},{17,9},{24,32},{25,17},{32,40},{... | collective-permute-start | bytes 2752520 | tf_op jit(solution)/shard_map/ppermute | solution.py:294
  118.2 20.1 %collective-permute-start.12 = (bf16[256,1792]{1,0:T(8,128)(2,1)S(1)}, bf16[256,1792]{1,0:T(8,128)(2,1)S(1)}, u32[]{:S(2)}, u32[]{:S(2)}) collective-permute-start(bf16[256,1792]{1,0:T(8,128)(2,1)S(1)} %collective-permute-done.8.refs_2_), channel_id=1, source_target_pairs={{0,8},{1,57},{8,16},{9,1},{16,24},{17,9},{24,32},{25,17},{32,40},{... | collective-permute-start | bytes 2752520 | tf_op jit(solution)/shard_map/ppermute | solution.py:294
  120.6 17.7 %collective-permute-start.1 = (s32[8,256]{1,0:T(8,128)S(1)}, s32[8,256]{1,0:T(8,128)S(1)}, u32[]{:S(2)}, u32[]{:S(2)}) collective-permute-start(s32[8,256]{1,0:T(8,128)S(1)} %add_select_fusion.refs_0_), channel_id=1, source_target_pairs={{0,24},{1,41},{8,32},{9,49},{16,40},{17,57},{24,48},{25,1},{32,56}... | collective-permute-start | bytes 24584 | tf_op jit(solution)/shard_map/ppermute | solution.py:294
  122.6 15.6 %collective-permute-start.2 = (s32[8,256]{1,0:T(8,128)S(1)}, s32[8,256]{1,0:T(8,128)S(1)}, u32[]{:S(2)}, u32[]{:S(2)}) collective-permute-start(s32[8,256]{1,0:T(8,128)S(1)} %add_select_fusion.refs_0_), channel_id=1, source_target_pairs={{0,32},{1,33},{8,40},{9,41},{16,48},{17,49},{24,56},{25,57},{32,0}... | collective-permute-start | bytes 24584 | tf_op jit(solution)/shard_map/ppermute | solution.py:294
  142.1 1.8 copy-start.1
  143.9 10.1 %copy-start = (bf16[1,1,1280,1024]{3,2,1,0:T(8,128)(2,1)S(1)}, bf16[1,1,1280,1024]{3,2,1,0:T(8,128)(2,1)}, u32[]{:S(2)}) copy-start(bf16[1,1,1280,1024]{3,2,1,0:T(8,128)(2,1)} %param.9) | copy-start | bytes 7864324
  143.9 10.1 %copy-start.9 = (f32[64,1,128]{2,1,0:T(1,128)S(1)}, f32[64,1,128]{2,1,0:T(1,128)}, u32[]{:S(2)}) copy-start(f32[64,1,128]{2,1,0:T(1,128)} %copy-done.8) | copy-start | bytes 98308
  143.9 50.7 %all-to-all-start = ((bf16[8,40,5376]{2,1,0:T(8,128)(2,1)}), bf16[8,40,5376]{2,1,0:T(8,128)(2,1)}, u32[]{:S(2)}, u32[]{:S(2)}) async-start(bf16[8,40,5376]{2,1,0:T(8,128)(2,1)} %bitcast.46), calls=%async_computation | async-start | bytes 6881280 | tf_op jit(solution)/shard_map/all_to_all | solution.py:312
  194.6 31.5 %copy-start.11 = (s32[1,128,8]{1,2,0:T(8,128)S(1)}, s32[1,128,8]{1,2,0:T(8,128)}, u32[]{:S(2)}) copy-start(s32[1,128,8]{1,2,0:T(8,128)} %param.6) | copy-start | bytes 12292
  194.6 31.5 %copy-start.13 = (s32[64,128]{1,0:T(8,128)S(1)}, s32[64,128]{1,0:T(8,128)}, u32[]{:S(2)}) copy-start(s32[64,128]{1,0:T(8,128)} %copy-done.12) | copy-start | bytes 98308
  194.6 31.5 %copy-start.15 = (f32[1,128,8]{1,2,0:T(8,128)S(1)}, f32[1,128,8]{1,2,0:T(8,128)}, u32[]{:S(2)}) copy-start(f32[1,128,8]{1,2,0:T(8,128)} %param.7) | copy-start | bytes 12292
  (4 other events, 3.2 us)

commit v2 on v1

v2 whole, which is shorter than its diff:
```python
from functools import partial

import jax
import jax.numpy as jnp
from jax import lax
from jax.experimental import pallas as pl
from jax.experimental.pallas import tpu as pltpu
from jax.sharding import Mesh, PartitionSpec as P

SCALE_ROUTED = 2.5
CORES = 2
COSTS = 3.0, 3.0, 14.0, 8.0
COLUMNS = 4
LANES = 128
SMALL_VMEM = 60 * 2**20
PROJECT_VMEM = 57 * 2**20


def iota(shape, dim):
    return lax.broadcasted_iota(jnp.int32, shape, dim)


def call(body, out_shape, cost, vmem=SMALL_VMEM, **kwargs):
    return pl.pallas_call(
        body,
        out_shape=out_shape,
        cost_estimate=pl.CostEstimate(flops=cost[0], bytes_accessed=cost[1], transcendentals=0),
        compiler_params=pltpu.CompilerParams(vmem_limit_bytes=vmem),
        **kwargs,
    )


def ranks_before(hits):
    tokens = hits.shape[1]
    first, second = iota((tokens, tokens), 0), iota((tokens, tokens), 1)
    ahead = (first < second) & (first // LANES == second // LANES)
    ahead = jnp.where(ahead, 1.0, 0.0).astype(jnp.bfloat16)
    return jnp.dot(hits.astype(jnp.bfloat16), ahead, preferred_element_type=jnp.float32)


def gate_rows(affinity):
    total = jnp.sum(affinity, axis=0, keepdims=True)
    weights = (SCALE_ROUTED * affinity / total).astype(jnp.bfloat16).astype(jnp.float32)
    return total, weights


def match_kernel(capacity, place_ref, *refs):
    groups = refs[:-3]
    onehot_ref, gain_ref, token_ref = refs[-3:]
    rows, tokens = onehot_ref.shape[1:]
    each = CORES * capacity
    experts = rows // each
    token_ref[...] = jnp.zeros(token_ref.shape, jnp.float32)
    lane = iota((each, LANES), 1)
    last = gain_ref.shape[0] - 1
    for i, group_ref in enumerate(groups):
        top = group_ref.shape[0] // 2
        _, weights = gate_rows(group_ref[top:])
        labels = (place_ref[0] * experts + iota((16, tokens), 0)).astype(jnp.float32)
        hits = jnp.zeros((16, tokens), jnp.float32)
        gains = jnp.zeros((16, tokens), jnp.float32)
        for k in range(top):
            named = group_ref[k : k + 1, :] == labels
            hits += jnp.where(named, 1.0, 0.0)
            gains += jnp.where(named, weights[k : k + 1, :], 0.0)
        slot = ranks_before(hits).astype(jnp.int32) + (iota((16, tokens), 1) // LANES) * capacity
        slot = jnp.where(hits > 0, slot, -1)
        order = iota((each, tokens), 0)
        for at in range(experts):
            s = (at % COLUMNS) * CORES + at // COLUMNS
            found = order == slot[s : s + 1, :]
            here = slice(at * each, (at + 1) * each)
            onehot_ref[i, here] = jnp.where(found, 1.0, 0.0)
            column = jnp.sum(jnp.where(found, gains[s : s + 1, :], 0.0), axis=1, keepdims=True)
            if i <= last:
                gain_ref[i, here] = jnp.where(lane == 0, column, 0.0)
            else:
                gain_ref[last, here] += jnp.where(lane == 1, column, 0.0)


def select_kernel(parts, place_ref, onehot_hbm, gain_hbm, token_ref, *refs):
    blocks = refs[: len(parts)]
    out_hbm, token_out, onehot_ref, gain_in, gain_ref, in_ref, out_ref, sems, in_sems, out_sems = refs[len(parts) :]
    count, tokens, width = in_ref.shape
    tile = width // 2
    token_out[...] = token_ref[...]
    first = parts[0]
    tables = [
        pltpu.make_async_copy(onehot_hbm.at[pl.ds(first, onehot_ref.shape[0])], onehot_ref, sems.at[0]),
        pltpu.make_async_copy(gain_hbm.at[first], gain_in, sems.at[1]),
    ]
    loads, targets = [], []
    for j in range(count):
        half = j if count == 1 or j == 2 else jnp.bitwise_xor(j, place_ref[1])
        for h in range(2):
            lanes = slice(h * tile, (h + 1) * tile)
            loads.append(pltpu.make_async_copy(blocks[j].at[:, lanes], in_ref.at[j, :, lanes], in_sems.at[len(loads)]))
            at = pl.multiple_of(half * width + h * tile, LANES)
            targets.append(out_hbm.at[:, pl.ds(at, tile)])
    for load in tables[:1] + loads + tables[1:]:
        load.start()
    tables[0].wait()
    onehots = [onehot_ref[i].astype(jnp.bfloat16) for i in range(onehot_ref.shape[0])]
    stores = []
    for i, load in enumerate(loads):
        j, lanes = i // 2, slice(i % 2 * tile, (i % 2 + 1) * tile)
        load.wait()
        rows = jnp.dot(onehots[parts[j] - first], in_ref[j, :, lanes], preferred_element_type=jnp.float32)
        out_ref[j, :, lanes] = rows.astype(jnp.bfloat16)
        stores.append(pltpu.make_async_copy(out_ref.at[j, :, lanes], targets[i], out_sems.at[i]))
        stores[-1].start()
    tables[1].wait()
    gain_ref[...] = gain_in[...].astype(jnp.bfloat16)
    stores.append(pltpu.make_async_copy(gain_ref, out_hbm.at[:, count * width :], out_sems.at[len(loads)]))
    stores[-1].start()
    for store in stores:
        store.wait()


def select_rows(place, onehots, gains, token, blocks, parts, micros):
    tokens, width = blocks[0].shape
    rows = onehots.shape[1]
    count = len(blocks)
    groups = max(parts) - parts[0] + 1
    outside = pl.BlockSpec(memory_space=pltpu.HBM)
    inside = pl.BlockSpec(memory_space=pltpu.VMEM)
    return call(
        partial(select_kernel, parts),
        (
            jax.ShapeDtypeStruct((rows, width * count + LANES), jnp.bfloat16),
            jax.ShapeDtypeStruct(token.shape, token.dtype),
        ),
        (int(micros * 1.1e9), 2 * (rows + tokens) * width * count),
        grid_spec=pltpu.PrefetchScalarGridSpec(
            num_scalar_prefetch=1,
            in_specs=[outside, outside, inside] + [outside] * count,
            out_specs=(outside, inside),
            scratch_shapes=[
                pltpu.VMEM((groups, rows, tokens), jnp.float32),
                pltpu.VMEM((rows, LANES), jnp.float32),
                pltpu.VMEM((rows, LANES), jnp.bfloat16),
                pltpu.VMEM((count, tokens, width), jnp.bfloat16),
                pltpu.VMEM((count, rows, width), jnp.bfloat16),
                pltpu.SemaphoreType.DMA((2,)),
                pltpu.SemaphoreType.DMA((2 * count,)),
                pltpu.SemaphoreType.DMA((2 * count + 1,)),
            ],
        ),
    )(place, onehots, gains, token, *blocks)


def project_kernel(full, half, capacity, zs_ref, x_hbm, w_hbm, saved_hbm, scores_in, *refs):
    hidden_hbm, scores_ref = refs[-12:-10]
    x_ref, gain_ref, w_ref, saved_ref, y_ref, out_ref, x_sems, w_sems, saved_sems, out_sems = refs[-10:]
    blocks, slots, units = out_ref.shape
    middle = x_ref.shape[2]
    width = y_ref.shape[1]
    chunks = units // width
    dims = (((1,), (1,)), ((), ()))
    pieces = []
    if full:
        for c in range(2):
            pieces.append((x_hbm.at[:, c * middle : (c + 1) * middle], x_ref.at[c, : 2 * slots]))
    if half:
        at = 2 * middle * full
        for c in range(2):
            pieces.append(
                (x_hbm.at[c * slots : (c + 1) * slots, at : at + middle], x_ref.at[c, 2 * slots * full :])
            )
    at = middle * (2 * full + half)
    pieces.append((x_hbm.at[:, at : at + LANES], gain_ref))
    loads = [pltpu.make_async_copy(a, b, x_sems.at[i]) for i, (a, b) in enumerate(pieces)]
    w_loads = [
        pltpu.make_async_copy(
            w_hbm.at[n * width : (n + 1) * width], w_ref.at[n * width : (n + 1) * width], w_sems.at[n]
        )
        for n in range(chunks)
    ]
    saved_loads = [
        pltpu.make_async_copy(saved_hbm.at[zs_ref[j]], saved_ref.at[j], saved_sems.at[j]) for j in range(blocks)
    ]
    for load in loads + w_loads[:1] + saved_loads + w_loads[1:]:
        load.start()

    def times(x, w):
        return lax.dot_general(x, w, dims, preferred_element_type=jnp.float32)

    row = iota((slots, LANES), 0)
    own_lane = iota((slots, LANES), 1) == row % capacity
    sources = slots // capacity
    scores_ref[...] = scores_in[...]
    for load in loads:
        load.wait()
    gains, totals = [], []
    for j in range(blocks):
        whole = full and j < CORES
        top = j * slots if whole else 0
        lane = 0 if whole or not full else 1
        column = gain_ref[top : top + slots, lane : lane + 1].astype(jnp.float32)
        gains.append(jnp.broadcast_to(column, (slots, LANES)))
        totals.append(jnp.zeros((slots, LANES), jnp.float32))

    stores = []
    for n in range(chunks):
        here = slice(n * width, (n + 1) * width)
        w_loads[n].wait()
        y_ref[...] = times(x_ref[0], w_ref[here, :middle]) + times(x_ref[1], w_ref[here, middle:])
        for j in range(blocks):
            if n == 0:
                saved_loads[j].wait()
            for i in range(0, width, LANES):
                lanes = slice(n * width + i, n * width + i + LANES)
                projected = y_ref[j * slots : (j + 1) * slots, i : i + LANES]
                out_ref[j, :, lanes] = (gains[j] * projected).astype(jnp.bfloat16)
                totals[j] += projected * saved_ref[j, :, lanes].astype(jnp.float32)
            store = pltpu.make_async_copy(
                out_ref.at[j, :, here], hidden_hbm.at[zs_ref[j], :, here], out_sems.at[n * blocks + j]
            )
            store.start()
            stores.append(store)

    for j in range(blocks):
        column = jnp.sum(totals[j], axis=1, keepdims=True)
        spread = jnp.where(own_lane, column, 0.0)
        place = iota((sources, LANES), 0)
        table = jnp.zeros((sources, LANES), jnp.float32)
        for s in range(sources):
            line = jnp.sum(jnp.where(row // capacity == s, spread, 0.0), axis=0, keepdims=True)
            table = jnp.where(place == s, line, table)
        scores_ref[pl.ds(pl.multiple_of(zs_ref[j] * sources, sources), sources), :] = table
    for store in stores:
        store.wait()


def project(zs, rows, weight, saved, scores, hidden, full, half, capacity):
    count = CORES * full + half
    blocks, slots, units = saved.shape
    features = weight.shape[1]
    width = 256
    inside = pl.BlockSpec(memory_space=pltpu.VMEM)
    outside = pl.BlockSpec(memory_space=pltpu.HBM)
    in_specs = [outside] * 3 + [inside]
    operands = [zs, rows, weight, saved, scores]
    aliases = {}
    if hidden is not None:
        in_specs.append(outside)
        aliases = {len(operands): 0}
        operands.append(hidden)
    return call(
        partial(project_kernel, full, half, capacity),
        (
            jax.ShapeDtypeStruct(saved.shape, jnp.bfloat16),
            jax.ShapeDtypeStruct(scores.shape, jnp.float32),
        ),
        (2 * rows.size * units, 2 * (rows.size + weight.size + 2 * count * slots * units)),
        vmem=PROJECT_VMEM,
        grid_spec=pltpu.PrefetchScalarGridSpec(
            num_scalar_prefetch=1,
            in_specs=in_specs,
            out_specs=(outside, inside),
            scratch_shapes=[
                pltpu.VMEM((2, count * slots, features // 2), jnp.bfloat16),
                pltpu.VMEM((2 * slots, LANES), jnp.bfloat16),
                pltpu.VMEM(weight.shape, weight.dtype),
                pltpu.VMEM((count, slots, units), saved.dtype),
                pltpu.VMEM((count * slots, width), jnp.float32),
                pltpu.VMEM((count, slots, units), jnp.bfloat16),
                pltpu.SemaphoreType.DMA((2 * full + 2 * half + 1,)),
                pltpu.SemaphoreType.DMA((units // width,)),
                pltpu.SemaphoreType.DMA((count,)),
                pltpu.SemaphoreType.DMA((units // width * count,)),
            ],
        ),
        input_output_aliases=aliases,
    )(*operands)


def gate_kernel(capacity, scores_ref, routes_ref, affinity_ref, out_ref):
    top = routes_ref.shape[0]
    total, weights = gate_rows(affinity_ref[...])
    labels = iota(scores_ref.shape, 0)
    hits = jnp.zeros(labels.shape, jnp.float32)
    for k in range(top):
        hits += jnp.where(routes_ref[k : k + 1, :] == labels, 1.0, 0.0)
    slot = jnp.where(hits > 0, ranks_before(hits), -1.0).astype(jnp.int32)
    found = jnp.zeros(labels.shape, jnp.float32)
    for r in range(capacity):
        found = jnp.where(slot == r, scores_ref[:, r : r + 1], found)
    place = iota((top, LANES), 0)
    grad = jnp.zeros((top, LANES), jnp.float32)
    for k in range(top):
        line = jnp.sum(jnp.where(routes_ref[k : k + 1, :] == labels, found, 0.0), axis=0, keepdims=True)
        grad = jnp.where(place == k, line, grad)
    weighted = jnp.sum(weights * grad, axis=0, keepdims=True)
    out_ref[...] = (SCALE_ROUTED / total) * grad - weighted / total


def on_device(upstream, routes, affinity, w_down, saved_hidden):
    sections, depth = lax.axis_size("pipe"), lax.axis_size("z")
    section, z, core = lax.axis_index("pipe"), lax.axis_index("z"), lax.axis_index("core")
    everyone = ("z", "x", "core")
    expert_count = depth * COLUMNS * CORES
    local = COLUMNS * CORES
    slot_total, units = saved_hidden.shape[2:]
    capacity = slot_total // expert_count
    tokens, features = upstream.shape[1:]
    half = features // 2
    cores = range(CORES)

    mine = lax.dynamic_slice(upstream[0], (0, core * half), (tokens, half))
    other = lax.dynamic_slice(upstream[0], (0, (1 - core) * half), (tokens, half))
    hop = range(1, sections)
    last = sections - 1
    near = lax.ppermute(mine, ("pipe", "core"), [(i * CORES + c, (i - 1) * CORES + c) for i in hop for c in cores])
    far = lax.ppermute(other, ("pipe", "core"), [(i * CORES + c, (i - 1) * CORES + 1 - c) for i in hop for c in cores])
    stay = lax.ppermute(other, ("pipe", "core"), [(last * CORES + c, last * CORES + 1 - c) for c in cores])

    routes_own = routes[0].T
    affinity_own = affinity[0].T
    choices = jnp.concatenate([routes_own.astype(jnp.float32), affinity_own], 0)
    choices_mate = lax.ppermute(choices, "core", [(c, 1 - c) for c in cores])

    def in_order(a, b, axis):
        return jnp.where(core == 0, jnp.concatenate([a, b], axis), jnp.concatenate([b, a], axis))

    def along(block, distance, cross=False):
        pairs = []
        for i in range(depth):
            pairs.append((i * CORES + (1 if cross else 0), (i + distance) % depth * CORES))
            pairs.append((i * CORES + (0 if cross else 1), (i - distance) % depth * CORES + 1))
        return lax.ppermute(block, ("z", "core"), pairs)

    reach = depth // 2
    choices_at = [in_order(choices, choices_mate, 1)]
    choices_at += [along(choices_at[0], k) for k in range(1, reach + 1)]
    place = jnp.stack([z, core])
    rows = local * CORES * capacity
    inside = pl.BlockSpec(memory_space=pltpu.VMEM)
    onehots, gains, token = call(
        partial(match_kernel, capacity),
        (
            jax.ShapeDtypeStruct((reach + 1, rows, CORES * tokens), jnp.float32),
            jax.ShapeDtypeStruct((reach, rows, LANES), jnp.float32),
            jax.ShapeDtypeStruct((8, LANES), jnp.float32),
        ),
        (10**6, 10**5),
        grid_spec=pltpu.PrefetchScalarGridSpec(
            num_scalar_prefetch=1, in_specs=[inside] * (reach + 1), out_specs=(inside,) * 3
        ),
    )(place, *choices_at)

    def exchange(block, axes, parts):
        shape = block.shape
        block = block.reshape(parts, shape[0] // parts, shape[1])
        return lax.all_to_all(block, axes, split_axis=0, concat_axis=0, tiled=True).reshape(shape)

    near, far, stay, token = lax.optimization_barrier((near, far, stay, token))
    is_last = section == last
    held = in_order(jnp.where(is_last, mine, near), jnp.where(is_last, stay, far), 0)
    weight = w_down[0, 0]
    saved = saved_hidden[0, 0].reshape(depth, slot_total // depth, units)
    scores = jnp.zeros((expert_count, LANES), jnp.float32)

    def at(*distances):
        return jnp.stack([(z + d) % depth for d in distances])

    def columns(blocks, parts, micros):
        rows, after = select_rows(place, onehots, gains, token, blocks, parts, micros)
        return exchange(rows, ("core", "x"), local), after

    groups = []
    same, cross = along(held, 1), along(held, 1, cross=True)
    got, token = columns([held], (0,), COSTS[0])
    groups.append((got, at(0), 0, 1))
    for k in range(1, reach - 1):
        same, cross, token = lax.optimization_barrier((same, cross, token))
        ahead = along(same, 1), along(cross, 1)
        got, token = columns([same, cross], (k, k), COSTS[k])
        groups.append((got, at(-k, k), 1, 0))
        same, cross = ahead
    k = reach - 1
    same, cross, token = lax.optimization_barrier((same, cross, token))
    got, token = columns([same, cross, along(same, 1)], (k, k, k + 1), COSTS[k])
    groups.append((got, at(-k, k, reach), 1, 1))

    hidden = None
    for got, zs, full, part in groups:
        hidden, scores = project(zs, got, weight, saved, scores, hidden, full, part, capacity)

    returned = exchange(scores, everyone, expert_count)
    affinity_grad = call(
        partial(gate_kernel, capacity),
        jax.ShapeDtypeStruct(affinity_own.shape, jnp.float32),
        (10**6, 10**5),
    )(returned, routes_own, affinity_own)
    return hidden.reshape(1, 1, slot_total, units), affinity_grad.T[None]


def solution(mesh):
    sections, experts = mesh.devices.shape
    grid = mesh.devices.reshape(sections, experts // (COLUMNS * CORES), COLUMNS, CORES)
    rows = ("z", "x", "core")
    return jax.shard_map(
        on_device,
        mesh=Mesh(grid, ("pipe",) + rows),
        in_specs=(
            P("pipe", rows, None),
            P("pipe", rows, None),
            P("pipe", rows, None),
            P("pipe", rows, None, None),
            P("pipe", rows, None, None),
        ),
        out_specs=(P("pipe", rows, None, None), P("pipe", rows, None)),
        check_vma=False,
    )
```

time: 229 us -> 218 us (0.952)
  waiting for transfers between devices: 78.1 us -> 60.6 us
  starting transfers between devices: 62 us -> 48.6 us
  Pallas kernels: 64 us -> 75 us
  other arithmetic: 0.62 us -> 4.9 us
  blocking collectives: 14.3 us -> 16.8 us
    ppermute x11, waiting for transfers between devices: 60.8 us -> 32.8 us  [along(): return lax.ppermute(block, ('z', 'core'), pairs)]
    all_to_all x5 -> x4, starting transfers between devices: 37.7 us -> 18.8 us  [exchange(): lax.all_to_all(block, axes, split_axis=0, concat_axis=0, tiled=True)]
    all_to_all x5 -> x4, waiting for transfers between devices: 11.5 us -> 27 us  [exchange(): lax.all_to_all(block, axes, split_axis=0, concat_axis=0, tiled=True)]
    pallas_call x5, Pallas kernels: 14.5 us -> 25.6 us  [the longest x4 22.3 us: select_rows(): call(partial(select_kernel, parts), (jax.ShapeDtypeStruct((rows, width *...]
    ppermute x1, waiting for transfers between devices: 5.87 us -> 0.01 us  [on_device(): lax.ppermute(other, ('pipe', 'core'), [(i * CORES + c, (i - 1) * CORES +...]
    ppermute x11, starting transfers between devices: 17.7 us -> 23.2 us  [along(): return lax.ppermute(block, ('z', 'core'), pairs)]
    all_to_all x1, blocking collectives: 14.3 us -> 16.8 us  [exchange(): lax.all_to_all(block, axes, split_axis=0, concat_axis=0, tiled=True)]
    unnamed x32 -> x24, local copies, waits for them, and re-layouts: 6 us -> 5.82 us
  transfers between devices with their start and end apart: 20 -> 19, of which waited for: 9 -> 9; matrix products, arithmetic and copies ran while one was open for 0% -> 2% of each run, Pallas kernels for 20% -> 27%
where the time goes in v2:
time: 218 us; the launch traced here: 214 us
  Pallas kernels  75 us (34%)
  waiting for transfers between devices  60.6 us (28%)
  starting transfers between devices  48.6 us (22%)
  blocking collectives  16.8 us (8%)
  local copies, waits for them, and re-layouts  7.65 us (4%)
  other arithmetic  4.9 us (2%)
    pallas_call x4, Pallas kernels, project(): call(partial(project_kernel, full, half, capacity), (jax.ShapeDtypeStruct...  47.7 us
    ppermute x11, waiting for transfers between devices, along(): return lax.ppermute(block, ('z', 'core'), pairs)  32.8 us
    all_to_all x4, waiting for transfers between devices, exchange(): lax.all_to_all(block, axes, split_axis=0, concat_axis=0, tiled=True)  27 us
    ppermute x11, starting transfers between devices, along(): return lax.ppermute(block, ('z', 'core'), pairs)  23.2 us
    pallas_call x4, Pallas kernels, select_rows(): call(partial(select_kernel, parts), (jax.ShapeDtypeStruct((rows, width *...  22.3 us
    all_to_all x4, starting transfers between devices, exchange(): lax.all_to_all(block, axes, split_axis=0, concat_axis=0, tiled=True)  18.8 us
    all_to_all x1, blocking collectives, exchange(): lax.all_to_all(block, axes, split_axis=0, concat_axis=0, tiled=True)  16.8 us
    unnamed x24, local copies, waits for them, and re-layouts  5.82 us
  transfers between devices with their start and end apart: 19, of which 9 were waited for; matrix products, arithmetic and copies ran while one was open for 2% of the time, Pallas kernels for 27%

profile of v2, /device:TPU:1, one launch (start us, length us, event | category | flops | bytes accessed | tf_op | source)
XLA Modules:
  0.0 214.4 jit_solution(17346910339753173141)
XLA Ops:
  6.5 3.2 %collective-permute-start = (f32[16,128]{1,0:T(8,128)S(1)}, f32[16,128]{1,0:T(8,128)S(1)}, u32[]{:S(2)}, u32[]{:S(2)}) collective-permute-start(f32[16,128]{1,0:T(8,128)S(1)} %pad_maximum_fusion), channel_id=1, source_target_pairs={{0,1},{1,0},{2,3},{3,2},{4,5},{5,4},{6,7},{7,6},{8,9},{9,8},{10,11... | collective-permute-start | bytes 24584 | tf_op jit(solution)/shard_map/ppermute | solution.py:321
  11.4 3.8 %collective-permute-start.1 = (f32[16,256]{1,0:T(8,128)S(1)}, f32[16,256]{1,0:T(8,128)S(1)}, u32[]{:S(2)}, u32[]{:S(2)}) collective-permute-start(f32[16,256]{1,0:T(8,128)S(1)} %maximum_select_fusion.1.refs_0_), channel_id=1, source_target_pairs={{0,8},{1,57},{8,16},{9,1},{16,24},{17,9},{24,32},{25,17},{32,40},{... | collective-permute-start | bytes 49160 | tf_op jit(solution)/shard_map/ppermute | solution.py:331
  16.4 2.6 %collective-permute-start.3 = (f32[16,256]{1,0:T(8,128)S(1)}, f32[16,256]{1,0:T(8,128)S(1)}, u32[]{:S(2)}, u32[]{:S(2)}) collective-permute-start(f32[16,256]{1,0:T(8,128)S(1)} %maximum_select_fusion.1.refs_0_), channel_id=1, source_target_pairs={{0,24},{1,41},{8,32},{9,49},{16,40},{17,57},{24,48},{25,1},{32,56}... | collective-permute-start | bytes 49160 | tf_op jit(solution)/shard_map/ppermute | solution.py:331
  19.0 2.3 %collective-permute-start.4 = (f32[16,256]{1,0:T(8,128)S(1)}, f32[16,256]{1,0:T(8,128)S(1)}, u32[]{:S(2)}, u32[]{:S(2)}) collective-permute-start(f32[16,256]{1,0:T(8,128)S(1)} %maximum_select_fusion.1.refs_0_), channel_id=1, source_target_pairs={{0,32},{1,33},{8,40},{9,41},{16,48},{17,49},{24,56},{25,57},{32,0}... | collective-permute-start | bytes 49160 | tf_op jit(solution)/shard_map/ppermute | solution.py:331
  22.0 3.7 %collective-permute-done.4.refs_4_ = f32[16,256]{1,0:T(8,128)S(1)} collective-permute-done((f32[16,256]{1,0:T(8,128)S(1)}, f32[16,256]{1,0:T(8,128)S(1)}, u32[]{:S(2)}, u32[]{:S(2)}) %collective-permute-start.4) | collective-permute-done | bytes 16416 | tf_op jit(solution)/shard_map/ppermute | solution.py:331
  26.3 3.3 %shard_map.68 = (f32[5,320,256]{2,1,0:T(8,128)}, f32[4,320,128]{2,1,0:T(8,128)}, f32[8,128]{1,0:T(8,128)}) custom-call(s32[2]{0:T(128)} %pad_add_fusion.1.place_ref, f32[16,256]{1,0:T(8,128)} %copy-done.4, f32[16,256]{1,0:T(8,128)} %copy-done.5, f32[16,256]{1,0:T(8,128)} %copy-done.6, f32[16,256]{1,0:T(8,128)} %copy-done.7, f32[16,256]{1,0:T(8,128)} %copy-done.8), custom_call_target="tpu_custom_call" | custom-call | flops 1000000 | bytes 100000 | tf_op jit(solution)/shard_map/pallas_call | solution.py:339
  29.9 3.4 %collective-permute-start.8 = (bf16[256,1792]{1,0:T(8,128)(2,1)S(1)}, bf16[256,1792]{1,0:T(8,128)(2,1)S(1)}, u32[]{:S(2)}, u32[]{:S(2)}) collective-permute-start(bf16[256,1792]{1,0:T(8,128)(2,1)S(1)} %maximum_select_fusion.refs_0_), channel_id=1, source_target_pairs={{0,8},{1,57},{8,16},{9,1},{16,24},{17,9},{24,32},{25,17},{32,40},{... | collective-permute-start | bytes 2752520 | tf_op jit(solution)/shard_map/ppermute | solution.py:331
  34.4 4.7 %shard_map.69 = (bf16[320,1920]{1,0:T(8,128)(2,1)}, f32[8,128]{1,0:T(8,128)}) custom-call(s32[2]{0:T(128)} %pad_add_fusion.1.place_ref, f32[5,320,256]{2,1,0:T(8,128)} %get-tuple-element.33.onehot_hbm, f32[4,320,128]{2,1,0:T(8,128)} %get-tuple-element.34.gain_hbm, f32[8,128]{1,0:T(8,128)} %get-tuple-element.39.token_ref, bf16[256,1792]{1,0:T(8,128)(2,1)} %copy-done.3), custom_call_target="tpu_custom_call" | custom-call | flops 3300000000 | bytes 2064384 | tf_op jit(solution)/shard_map/pallas_call | solution.py:127
  39.0 4.6 %all-to-all-start.3 = ((bf16[8,40,1920]{2,1,0:T(8,128)(2,1)}), bf16[8,40,1920]{2,1,0:T(8,128)(2,1)S(1)}, u32[]{:S(2)}, u32[]{:S(2)}) async-start(bf16[8,40,1920]{2,1,0:T(8,128)(2,1)} %bitcast.54), calls=%async_computation.3 | async-start | bytes 2457600 | tf_op jit(solution)/shard_map/all_to_all | solution.py:355
  43.6 8.3 %collective-permute-done.8.refs_0_ = bf16[256,1792]{1,0:T(8,128)(2,1)S(1)} collective-permute-done((bf16[256,1792]{1,0:T(8,128)(2,1)S(1)}, bf16[256,1792]{1,0:T(8,128)(2,1)S(1)}, u32[]{:S(2)}, u32[]{:S(2)}) %collective-permute-start.8) | collective-permute-done | bytes 917536 | tf_op jit(solution)/shard_map/ppermute | solution.py:331
  51.9 2.2 %collective-permute-done.9.refs_1_ = bf16[256,1792]{1,0:T(8,128)(2,1)} collective-permute-done((bf16[256,1792]{1,0:T(8,128)(2,1)S(1)}, bf16[256,1792]{1,0:T(8,128)(2,1)}, u32[]{:S(2)}, u32[]{:S(2)}) %collective-permute-start.9) | collective-permute-done | bytes 917536 | tf_op jit(solution)/shard_map/ppermute | solution.py:331
  54.1 2.8 %collective-permute-start.10 = (bf16[256,1792]{1,0:T(8,128)(2,1)}, bf16[256,1792]{1,0:T(8,128)(2,1)S(1)}, u32[]{:S(2)}, u32[]{:S(2)}) collective-permute-start(bf16[256,1792]{1,0:T(8,128)(2,1)} %copy-done.10), channel_id=1, source_target_pairs={{0,8},{1,57},{8,16},{9,1},{16,24},{17,9},{24,32},{25,17},{32,40},{... | collective-permute-start | bytes 2752520 | tf_op jit(solution)/shard_map/ppermute | solution.py:331
  56.9 5.5 %shard_map.70 = (bf16[320,3712]{1,0:T(8,128)(2,1)}, f32[8,128]{1,0:T(8,128)}) custom-call(s32[2]{0:T(128)} %pad_add_fusion.1.place_ref, f32[5,320,256]{2,1,0:T(8,128)} %get-tuple-element.33.onehot_hbm, f32[4,320,128]{2,1,0:T(8,128)} %get-tuple-element.34.gain_hbm, f32[8,128]{1,0:T(8,128)} %get-tuple-element.43.token_ref, bf16[256,1792]{1,0:T(8,128)(2,1)} %copy-done.10, ...), custom_call_target="tpu_custom_call" | custom-call | flops 3300000000 | bytes 4128768 | tf_op jit(solution)/shard_map/pallas_call | solution.py:127
  63.5 5.9 %all-to-all-start.2 = ((bf16[8,40,3712]{2,1,0:T(8,128)(2,1)}), bf16[8,40,3712]{2,1,0:T(8,128)(2,1)S(1)}, u32[]{:S(2)}, u32[]{:S(2)}) async-start(bf16[8,40,3712]{2,1,0:T(8,128)(2,1)} %bitcast.53), calls=%async_computation.2 | async-start | bytes 4751360 | tf_op jit(solution)/shard_map/all_to_all | solution.py:355
  69.4 8.0 %collective-permute-done.11.refs_1_ = bf16[256,1792]{1,0:T(8,128)(2,1)} collective-permute-done((bf16[256,1792]{1,0:T(8,128)(2,1)}, bf16[256,1792]{1,0:T(8,128)(2,1)}, u32[]{:S(2)}, u32[]{:S(2)}) %collective-permute-start.11) | collective-permute-done | bytes 917536 | tf_op jit(solution)/shard_map/ppermute | solution.py:331
  77.4 3.3 %collective-permute-start.12 = (bf16[256,1792]{1,0:T(8,128)(2,1)S(1)}, bf16[256,1792]{1,0:T(8,128)(2,1)}, u32[]{:S(2)}, u32[]{:S(2)}) collective-permute-start(bf16[256,1792]{1,0:T(8,128)(2,1)S(1)} %collective-permute-done.10.refs_0_), channel_id=1, source_target_pairs={{0,8},{1,57},{8,16},{9,1},{16,24},{17,9},{24,32},{25,17},{32,40},{... | collective-permute-start | bytes 2752520 | tf_op jit(solution)/shard_map/ppermute | solution.py:331
  80.7 5.6 %shard_map.71 = (bf16[320,3712]{1,0:T(8,128)(2,1)}, f32[8,128]{1,0:T(8,128)}) custom-call(s32[2]{0:T(128)} %pad_add_fusion.1.place_ref, f32[5,320,256]{2,1,0:T(8,128)} %get-tuple-element.33.onehot_hbm, f32[4,320,128]{2,1,0:T(8,128)} %get-tuple-element.34.gain_hbm, f32[8,128]{1,0:T(8,128)} %get-tuple-element.47.token_ref, bf16[256,1792]{1,0:T(8,128)(2,1)} %copy-done.9, ...), custom_call_target="tpu_custom_call" | custom-call | flops 15399999488 | bytes 4128768 | tf_op jit(solution)/shard_map/pallas_call | solution.py:127
  86.3 12.7 %all-to-all-done.2 = bf16[8,40,3712]{2,1,0:T(8,128)(2,1)S(1)} async-done(((bf16[8,40,3712]{2,1,0:T(8,128)(2,1)}), bf16[8,40,3712]{2,1,0:T(8,128)(2,1)S(1)}, u32[]{:S(2)}, u32[]{:S(2)}) %all-to-all-start.2) | async-done | bytes 2375712 | tf_op jit(solution)/shard_map/all_to_all | solution.py:355
  100.5 4.3 %all-to-all-start.1 = ((bf16[8,40,3712]{2,1,0:T(8,128)(2,1)}), bf16[8,40,3712]{2,1,0:T(8,128)(2,1)}, u32[]{:S(2)}, u32[]{:S(2)}) async-start(bf16[8,40,3712]{2,1,0:T(8,128)(2,1)} %bitcast.52), calls=%async_computation.1 | async-start | bytes 4751360 | tf_op jit(solution)/shard_map/all_to_all | solution.py:355
  104.9 2.7 %collective-permute-start.14 = (bf16[256,1792]{1,0:T(8,128)(2,1)}, bf16[256,1792]{1,0:T(8,128)(2,1)S(1)}, u32[]{:S(2)}, u32[]{:S(2)}) collective-permute-start(bf16[256,1792]{1,0:T(8,128)(2,1)} %collective-permute-done.12.refs_0_), channel_id=1, source_target_pairs={{0,8},{1,57},{8,16},{9,1},{16,24},{17,9},{24,32},{25,17},{32,40},{... | collective-permute-start | bytes 2752520 | tf_op jit(solution)/shard_map/ppermute | solution.py:331
  107.5 10.7 %collective-permute-done.14.refs_2_ = bf16[256,1792]{1,0:T(8,128)(2,1)S(1)} collective-permute-done((bf16[256,1792]{1,0:T(8,128)(2,1)}, bf16[256,1792]{1,0:T(8,128)(2,1)S(1)}, u32[]{:S(2)}, u32[]{:S(2)}) %collective-permute-start.14) | collective-permute-done | bytes 917536 | tf_op jit(solution)/shard_map/ppermute | solution.py:331
  119.1 6.6 %shard_map.72 = (bf16[320,5504]{1,0:T(8,128)(2,1)}, f32[8,128]{1,0:T(8,128)}) custom-call(s32[2]{0:T(128)} %pad_add_fusion.1.place_ref, f32[5,320,256]{2,1,0:T(8,128)} %get-tuple-element.33.onehot_hbm, f32[4,320,128]{2,1,0:T(8,128)} %get-tuple-element.34.gain_hbm, f32[8,128]{1,0:T(8,128)} %get-tuple-element.49.token_ref, ...), custom_call_target="tpu_custom_call" | custom-call | flops 8800000000 | bytes 6193152 | tf_op jit(solution)/shard_map/pallas_call | solution.py:127
  125.8 8.3 %all-to-all-done.1 = bf16[8,40,3712]{2,1,0:T(8,128)(2,1)} async-done(((bf16[8,40,3712]{2,1,0:T(8,128)(2,1)}), bf16[8,40,3712]{2,1,0:T(8,128)(2,1)}, u32[]{:S(2)}, u32[]{:S(2)}) %all-to-all-start.1) | async-done | bytes 2375712 | tf_op jit(solution)/shard_map/all_to_all | solution.py:355
  134.0 4.0 %all-to-all-start = ((bf16[8,40,5504]{2,1,0:T(8,128)(2,1)}), bf16[8,40,5504]{2,1,0:T(8,128)(2,1)S(1)}, u32[]{:S(2)}, u32[]{:S(2)}) async-start(bf16[8,40,5504]{2,1,0:T(8,128)(2,1)} %bitcast.51), calls=%async_computation | async-start | bytes 7045120 | tf_op jit(solution)/shard_map/all_to_all | solution.py:355
  140.4 9.6 %shard_map.73 = (bf16[8,160,1024]{2,1,0:T(8,128)(2,1)}, f32[64,128]{1,0:T(8,128)}) custom-call(s32[1]{0:T(128)} %bitcast.23.zs_ref, bf16[320,1920]{1,0:T(8,128)(2,1)} %bitcast.50, bf16[1024,3584]{1,0:T(8,128)(2,1)} %bitcast.39, bf16[8,160,1024]{2,1,0:T(8,128)(2,1)} %bitcast.43, f32[64,128]{1,0:T(8,128)} %broadcast_in_dim.6.scores_in), custom_call_target="tpu_custom_call" | custom-call | flops 1258291200 | bytes 9224192 | tf_op jit(solution)/shard_map/pallas_call | solution.py:249
  150.1 11.7 %shard_map.74 = (bf16[8,160,1024]{2,1,0:T(8,128)(2,1)}, f32[64,128]{1,0:T(8,128)}) custom-call(s32[2]{0:T(128)} %pad_add_fusion.3.zs_ref, bf16[320,3712]{1,0:T(8,128)(2,1)} %bitcast.49, bf16[1024,3584]{1,0:T(8,128)(2,1)} %bitcast.40, bf16[8,160,1024]{2,1,0:T(8,128)(2,1)} %bitcast.44, ...), custom_call_target="tpu_custom_call", output_to_operand_aliasing={{0}: (5, {})} | custom-call | flops 2432696320 | bytes 11026432 | tf_op jit(solution)/shard_map/pallas_call | solution.py:249
  161.8 11.7 %shard_map.75 = (bf16[8,160,1024]{2,1,0:T(8,128)(2,1)}, f32[64,128]{1,0:T(8,128)}) custom-call(s32[2]{0:T(128)} %pad_add_fusion.2.zs_ref, bf16[320,3712]{1,0:T(8,128)(2,1)} %bitcast.18.x_hbm, bf16[1024,3584]{1,0:T(8,128)(2,1)} %bitcast.41, bf16[8,160,1024]{2,1,0:T(8,128)(2,1)} %bitcast.45, ...), custom_call_target="tpu_custom_call", output_to_operand_aliasing={{0}: (5, {})} | custom-call | flops 2432696320 | bytes 11026432 | tf_op jit(solution)/shard_map/pallas_call | solution.py:249
  173.5 6.0 %all-to-all-done = bf16[8,40,5504]{2,1,0:T(8,128)(2,1)S(1)} async-done(((bf16[8,40,5504]{2,1,0:T(8,128)(2,1)}), bf16[8,40,5504]{2,1,0:T(8,128)(2,1)S(1)}, u32[]{:S(2)}, u32[]{:S(2)}) %all-to-all-start) | async-done | bytes 3522592 | tf_op jit(solution)/shard_map/all_to_all | solution.py:355
  179.5 1.7 copy-done
  181.2 14.7 %shard_map.76 = (bf16[8,160,1024]{2,1,0:T(8,128)(2,1)}, f32[64,128]{1,0:T(8,128)}) custom-call(s32[3]{0:T(128)} %pad_add_fusion.zs_ref, bf16[320,5504]{1,0:T(8,128)(2,1)} %bitcast.48, bf16[1024,3584]{1,0:T(8,128)(2,1)} %bitcast.42, bf16[8,160,1024]{2,1,0:T(8,128)(2,1)} %bitcast.46, ...), custom_call_target="tpu_custom_call", output_to_operand_aliasing={{0}: (5, {})} | custom-call | flops 3607101440 | bytes 12828672 | tf_op jit(solution)/shard_map/pallas_call | solution.py:249
  195.9 16.8 %all_to_all.25 = f32[64,1,128]{2,1,0:T(1,128)} all-to-all(f32[64,1,128]{2,1,0:T(1,128)} %bitcast.59), channel_id=1, replica_groups=mesh['pipe'=4,'z'=8,'x'=4,'core'=2] {'z','x','core'}, dimensions={0} | all-to-all | bytes 65536 | tf_op jit(solution)/shard_map/all_to_all | solution.py:355
  212.7 1.7 shard_map.77
  (52 shorter events, 17.2 us)
Async XLA Ops:
  1.9 27.7 %collective-permute-start.6 = (bf16[128,1792]{1,0:T(8,128)(2,1)S(1)}, bf16[128,1792]{1,0:T(8,128)(2,1)S(1)}, u32[]{:S(2)}, u32[]{:S(2)}) collective-permute-start(bf16[128,1792]{1,0:T(8,128)(2,1)S(1)} %get-tuple-element.64), channel_id=1, source_target_pairs={{64,1},{65,0},{128,65},{129,64},{192,129},{193,128},{66,3},{67,2},... | collective-permute-start | bytes 1376264 | tf_op jit(solution)/shard_map/ppermute | solution.py:315
  3.2 26.4 %collective-permute-start.7 = (bf16[128,1792]{1,0:T(8,128)(2,1)S(1)}, bf16[128,1792]{1,0:T(8,128)(2,1)S(1)}, u32[]{:S(2)}, u32[]{:S(2)}) collective-permute-start(bf16[128,1792]{1,0:T(8,128)(2,1)S(1)} %get-tuple-element.64), channel_id=1, source_target_pairs={{192,193},{193,192},{194,195},{195,194},{196,197},{197,196},{198,1... | collective-permute-start | bytes 1376264 | tf_op jit(solution)/shard_map/ppermute | solution.py:316
  3.9 25.7 %collective-permute-start.5 = (bf16[128,1792]{1,0:T(8,128)(2,1)S(1)}, bf16[128,1792]{1,0:T(8,128)(2,1)S(1)}, u32[]{:S(2)}, u32[]{:S(2)}) collective-permute-start(bf16[128,1792]{1,0:T(8,128)(2,1)S(1)} %get-tuple-element.65), channel_id=1, source_target_pairs={{64,0},{65,1},{128,64},{129,65},{192,128},{193,129},{66,2},{67,3},... | collective-permute-start | bytes 1376264 | tf_op jit(solution)/shard_map/ppermute | solution.py:314
  6.5 4.1 %collective-permute-start = (f32[16,128]{1,0:T(8,128)S(1)}, f32[16,128]{1,0:T(8,128)S(1)}, u32[]{:S(2)}, u32[]{:S(2)}) collective-permute-start(f32[16,128]{1,0:T(8,128)S(1)} %pad_maximum_fusion), channel_id=1, source_target_pairs={{0,1},{1,0},{2,3},{3,2},{4,5},{5,4},{6,7},{7,6},{8,9},{9,8},{10,11... | collective-permute-start | bytes 24584 | tf_op jit(solution)/shard_map/ppermute | solution.py:321
  11.4 14.3 %copy-start.4 = (f32[16,256]{1,0:T(8,128)}, f32[16,256]{1,0:T(8,128)S(1)}, u32[]{:S(2)}) copy-start(f32[16,256]{1,0:T(8,128)S(1)} %maximum_select_fusion.1.refs_0_) | copy-start | bytes 49156
  11.4 5.0 %collective-permute-start.1 = (f32[16,256]{1,0:T(8,128)S(1)}, f32[16,256]{1,0:T(8,128)S(1)}, u32[]{:S(2)}, u32[]{:S(2)}) collective-permute-start(f32[16,256]{1,0:T(8,128)S(1)} %maximum_select_fusion.1.refs_0_), channel_id=1, source_target_pairs={{0,8},{1,57},{8,16},{9,1},{16,24},{17,9},{24,32},{25,17},{32,40},{... | collective-permute-start | bytes 49160 | tf_op jit(solution)/shard_map/ppermute | solution.py:331
  15.2 3.8 %collective-permute-start.2 = (f32[16,256]{1,0:T(8,128)S(1)}, f32[16,256]{1,0:T(8,128)S(1)}, u32[]{:S(2)}, u32[]{:S(2)}) collective-permute-start(f32[16,256]{1,0:T(8,128)S(1)} %maximum_select_fusion.1.refs_0_), channel_id=1, source_target_pairs={{0,16},{1,49},{8,24},{9,57},{16,32},{17,1},{24,40},{25,9},{32,48},... | collective-permute-start | bytes 49160 | tf_op jit(solution)/shard_map/ppermute | solution.py:331
  16.4 9.3 %copy-start.5 = (f32[16,256]{1,0:T(8,128)}, f32[16,256]{1,0:T(8,128)S(1)}, u32[]{:S(2)}) copy-start(f32[16,256]{1,0:T(8,128)S(1)} %collective-permute-done.1.refs_1_) | copy-start | bytes 49156
  16.4 5.6 %collective-permute-start.3 = (f32[16,256]{1,0:T(8,128)S(1)}, f32[16,256]{1,0:T(8,128)S(1)}, u32[]{:S(2)}, u32[]{:S(2)}) collective-permute-start(f32[16,256]{1,0:T(8,128)S(1)} %maximum_select_fusion.1.refs_0_), channel_id=1, source_target_pairs={{0,24},{1,41},{8,32},{9,49},{16,40},{17,57},{24,48},{25,1},{32,56}... | collective-permute-start | bytes 49160 | tf_op jit(solution)/shard_map/ppermute | solution.py:331
  19.0 6.7 %copy-start.6 = (f32[16,256]{1,0:T(8,128)}, f32[16,256]{1,0:T(8,128)S(1)}, u32[]{:S(2)}) copy-start(f32[16,256]{1,0:T(8,128)S(1)} %collective-permute-done.2.refs_2_) | copy-start | bytes 49156
  19.0 6.7 %collective-permute-start.4 = (f32[16,256]{1,0:T(8,128)S(1)}, f32[16,256]{1,0:T(8,128)S(1)}, u32[]{:S(2)}, u32[]{:S(2)}) collective-permute-start(f32[16,256]{1,0:T(8,128)S(1)} %maximum_select_fusion.1.refs_0_), channel_id=1, source_target_pairs={{0,32},{1,33},{8,40},{9,41},{16,48},{17,49},{24,56},{25,57},{32,0}... | collective-permute-start | bytes 49160 | tf_op jit(solution)/shard_map/ppermute | solution.py:331
  22.0 3.7 %copy-start.7 = (f32[16,256]{1,0:T(8,128)}, f32[16,256]{1,0:T(8,128)S(1)}, u32[]{:S(2)}) copy-start(f32[16,256]{1,0:T(8,128)S(1)} %collective-permute-done.3.refs_3_) | copy-start | bytes 49156
  25.7 0.6 copy-start.8
  29.9 4.5 %copy-start.3 = (bf16[256,1792]{1,0:T(8,128)(2,1)}, bf16[256,1792]{1,0:T(8,128)(2,1)S(1)}, u32[]{:S(2)}) copy-start(bf16[256,1792]{1,0:T(8,128)(2,1)S(1)} %maximum_select_fusion.refs_0_) | copy-start | bytes 2752516
  29.9 22.0 %collective-permute-start.8 = (bf16[256,1792]{1,0:T(8,128)(2,1)S(1)}, bf16[256,1792]{1,0:T(8,128)(2,1)S(1)}, u32[]{:S(2)}, u32[]{:S(2)}) collective-permute-start(bf16[256,1792]{1,0:T(8,128)(2,1)S(1)} %maximum_select_fusion.refs_0_), channel_id=1, source_target_pairs={{0,8},{1,57},{8,16},{9,1},{16,24},{17,9},{24,32},{25,17},{32,40},{... | collective-permute-start | bytes 2752520 | tf_op jit(solution)/shard_map/ppermute | solution.py:331
  33.3 20.8 %collective-permute-start.9 = (bf16[256,1792]{1,0:T(8,128)(2,1)S(1)}, bf16[256,1792]{1,0:T(8,128)(2,1)}, u32[]{:S(2)}, u32[]{:S(2)}) collective-permute-start(bf16[256,1792]{1,0:T(8,128)(2,1)S(1)} %maximum_select_fusion.refs_0_), channel_id=1, source_target_pairs={{1,8},{0,57},{9,16},{8,1},{17,24},{16,9},{25,32},{24,17},{33,40},{... | collective-permute-start | bytes 2752520 | tf_op jit(solution)/shard_map/ppermute | solution.py:331
  39.0 23.4 %all-to-all-start.3 = ((bf16[8,40,1920]{2,1,0:T(8,128)(2,1)}), bf16[8,40,1920]{2,1,0:T(8,128)(2,1)S(1)}, u32[]{:S(2)}, u32[]{:S(2)}) async-start(bf16[8,40,1920]{2,1,0:T(8,128)(2,1)} %bitcast.54), calls=%async_computation.3 | async-start | bytes 2457600 | tf_op jit(solution)/shard_map/all_to_all | solution.py:355
  51.9 2.2 %copy-start.10 = (bf16[256,1792]{1,0:T(8,128)(2,1)}, bf16[256,1792]{1,0:T(8,128)(2,1)S(1)}, u32[]{:S(2)}) copy-start(bf16[256,1792]{1,0:T(8,128)(2,1)S(1)} %collective-permute-done.8.refs_0_) | copy-start | bytes 2752516
  54.1 15.3 %collective-permute-start.10 = (bf16[256,1792]{1,0:T(8,128)(2,1)}, bf16[256,1792]{1,0:T(8,128)(2,1)S(1)}, u32[]{:S(2)}, u32[]{:S(2)}) collective-permute-start(bf16[256,1792]{1,0:T(8,128)(2,1)} %copy-done.10), channel_id=1, source_target_pairs={{0,8},{1,57},{8,16},{9,1},{16,24},{17,9},{24,32},{25,17},{32,40},{... | collective-permute-start | bytes 2752520 | tf_op jit(solution)/shard_map/ppermute | solution.py:331
  56.9 20.5 %collective-permute-start.11 = (bf16[256,1792]{1,0:T(8,128)(2,1)}, bf16[256,1792]{1,0:T(8,128)(2,1)}, u32[]{:S(2)}, u32[]{:S(2)}) collective-permute-start(bf16[256,1792]{1,0:T(8,128)(2,1)} %collective-permute-done.9.refs_1_), channel_id=1, source_target_pairs={{0,8},{1,57},{8,16},{9,1},{16,24},{17,9},{24,32},{25,17},{32,40},{... | collective-permute-start | bytes 2752520 | tf_op jit(solution)/shard_map/ppermute | solution.py:331
  62.4 1.1 copy-start.2
  63.5 35.5 %all-to-all-start.2 = ((bf16[8,40,3712]{2,1,0:T(8,128)(2,1)}), bf16[8,40,3712]{2,1,0:T(8,128)(2,1)S(1)}, u32[]{:S(2)}, u32[]{:S(2)}) async-start(bf16[8,40,3712]{2,1,0:T(8,128)(2,1)} %bitcast.53), calls=%async_computation.2 | async-start | bytes 4751360 | tf_op jit(solution)/shard_map/all_to_all | solution.py:355
  69.4 11.3 %copy-start.9 = (bf16[256,1792]{1,0:T(8,128)(2,1)}, bf16[256,1792]{1,0:T(8,128)(2,1)S(1)}, u32[]{:S(2)}) copy-start(bf16[256,1792]{1,0:T(8,128)(2,1)S(1)} %collective-permute-done.10.refs_0_) | copy-start | bytes 2752516
  77.4 27.5 %collective-permute-start.12 = (bf16[256,1792]{1,0:T(8,128)(2,1)S(1)}, bf16[256,1792]{1,0:T(8,128)(2,1)}, u32[]{:S(2)}, u32[]{:S(2)}) collective-permute-start(bf16[256,1792]{1,0:T(8,128)(2,1)S(1)} %collective-permute-done.10.refs_0_), channel_id=1, source_target_pairs={{0,8},{1,57},{8,16},{9,1},{16,24},{17,9},{24,32},{25,17},{32,40},{... | collective-permute-start | bytes 2752520 | tf_op jit(solution)/shard_map/ppermute | solution.py:331
  80.7 24.2 %collective-permute-start.13 = (bf16[256,1792]{1,0:T(8,128)(2,1)}, bf16[256,1792]{1,0:T(8,128)(2,1)}, u32[]{:S(2)}, u32[]{:S(2)}) collective-permute-start(bf16[256,1792]{1,0:T(8,128)(2,1)} %collective-permute-done.11.refs_1_), channel_id=1, source_target_pairs={{0,8},{1,57},{8,16},{9,1},{16,24},{17,9},{24,32},{25,17},{32,40},{... | collective-permute-start | bytes 2752520 | tf_op jit(solution)/shard_map/ppermute | solution.py:331
  99.0 1.5 copy-start.1
  100.5 33.5 %all-to-all-start.1 = ((bf16[8,40,3712]{2,1,0:T(8,128)(2,1)}), bf16[8,40,3712]{2,1,0:T(8,128)(2,1)}, u32[]{:S(2)}, u32[]{:S(2)}) async-start(bf16[8,40,3712]{2,1,0:T(8,128)(2,1)} %bitcast.52), calls=%async_computation.1 | async-start | bytes 4751360 | tf_op jit(solution)/shard_map/all_to_all | solution.py:355
  104.9 13.3 %collective-permute-start.14 = (bf16[256,1792]{1,0:T(8,128)(2,1)}, bf16[256,1792]{1,0:T(8,128)(2,1)S(1)}, u32[]{:S(2)}, u32[]{:S(2)}) collective-permute-start(bf16[256,1792]{1,0:T(8,128)(2,1)} %collective-permute-done.12.refs_0_), channel_id=1, source_target_pairs={{0,8},{1,57},{8,16},{9,1},{16,24},{17,9},{24,32},{25,17},{32,40},{... | collective-permute-start | bytes 2752520 | tf_op jit(solution)/shard_map/ppermute | solution.py:331
  118.2 0.9 copy-start.11
  134.0 45.5 %all-to-all-start = ((bf16[8,40,5504]{2,1,0:T(8,128)(2,1)}), bf16[8,40,5504]{2,1,0:T(8,128)(2,1)S(1)}, u32[]{:S(2)}, u32[]{:S(2)}) async-start(bf16[8,40,5504]{2,1,0:T(8,128)(2,1)} %bitcast.51), calls=%async_computation | async-start | bytes 7045120 | tf_op jit(solution)/shard_map/all_to_all | solution.py:355
  179.5 1.7 copy-start

commit v3 on v2

--- a/solution.py
+++ b/solution.py
@@ -12,8 +12,8 @@
 COSTS = 3.0, 3.0, 14.0, 8.0
 COLUMNS = 4
 LANES = 128
-SMALL_VMEM = 60 * 2**20
-PROJECT_VMEM = 57 * 2**20
+SMALL_VMEM = 12 * 2**20
+PROJECT_VMEM = 16 * 2**20
 
 
 def iota(shape, dim):
@@ -78,41 +78,29 @@
                 gain_ref[last, here] += jnp.where(lane == 1, column, 0.0)
 
 
-def select_kernel(parts, place_ref, onehot_hbm, gain_hbm, token_ref, *refs):
+def select_kernel(parts, place_ref, onehot_ref, gain_in, token_ref, *refs):
     blocks = refs[: len(parts)]
-    out_hbm, token_out, onehot_ref, gain_in, gain_ref, in_ref, out_ref, sems, in_sems, out_sems = refs[len(parts) :]
-    count, tokens, width = in_ref.shape
+    out_hbm, token_out, gain_ref, out_ref, out_sems = refs[len(parts) :]
+    count, _, width = out_ref.shape
     tile = width // 2
+    first = parts[0]
     token_out[...] = token_ref[...]
-    first = parts[0]
-    tables = [
-        pltpu.make_async_copy(onehot_hbm.at[pl.ds(first, onehot_ref.shape[0])], onehot_ref, sems.at[0]),
-        pltpu.make_async_copy(gain_hbm.at[first], gain_in, sems.at[1]),
-    ]
-    loads, targets = [], []
+    gain_ref[...] = gain_in[first].astype(jnp.bfloat16)
+    stores = [pltpu.make_async_copy(gain_ref, out_hbm.at[:, count * width :], out_sems.at[2 * count])]
+    stores[0].start()
     for j in range(count):
+        onehot = onehot_ref[parts[j]].astype(jnp.bfloat16)
         half = j if count == 1 or j == 2 else jnp.bitwise_xor(j, place_ref[1])
         for h in range(2):
             lanes = slice(h * tile, (h + 1) * tile)
-            loads.append(pltpu.make_async_copy(blocks[j].at[:, lanes], in_ref.at[j, :, lanes], in_sems.at[len(loads)]))
+            rows = jnp.dot(onehot, blocks[j][:, lanes], preferred_element_type=jnp.float32)
+            out_ref[j, :, lanes] = rows.astype(jnp.bfloat16)
             at = pl.multiple_of(half * width + h * tile, LANES)
-            targets.append(out_hbm.at[:, pl.ds(at, tile)])
-    for load in tables[:1] + loads + tables[1:]:
-        load.start()
-    tables[0].wait()
-    onehots = [onehot_ref[i].astype(jnp.bfloat16) for i in range(onehot_ref.shape[0])]
-    stores = []
-    for i, load in enumerate(loads):
-        j, lanes = i // 2, slice(i % 2 * tile, (i % 2 + 1) * tile)
-        load.wait()
-        rows = jnp.dot(onehots[parts[j] - first], in_ref[j, :, lanes], preferred_element_type=jnp.float32)
-        out_ref[j, :, lanes] = rows.astype(jnp.bfloat16)
-        stores.append(pltpu.make_async_copy(out_ref.at[j, :, lanes], targets[i], out_sems.at[i]))
-        stores[-1].start()
-    tables[1].wait()
-    gain_ref[...] = gain_in[...].astype(jnp.bfloat16)
-    stores.append(pltpu.make_async_copy(gain_ref, out_hbm.at[:, count * width :], out_sems.at[len(loads)]))
-    stores[-1].start()
+            store = pltpu.make_async_copy(
+                out_ref.at[j, :, lanes], out_hbm.at[:, pl.ds(at, tile)], out_sems.at[2 * j + h]
+            )
+            store.start()
+            stores.append(store)
     for store in stores:
         store.wait()
 
@@ -121,7 +109,6 @@
     tokens, width = blocks[0].shape
     rows = onehots.shape[1]
     count = len(blocks)
-    groups = max(parts) - parts[0] + 1
     outside = pl.BlockSpec(memory_space=pltpu.HBM)
     inside = pl.BlockSpec(memory_space=pltpu.VMEM)
     return call(
@@ -133,55 +120,27 @@
         (int(micros * 1.1e9), 2 * (rows + tokens) * width * count),
         grid_spec=pltpu.PrefetchScalarGridSpec(
             num_scalar_prefetch=1,
-            in_specs=[outside, outside, inside] + [outside] * count,
+            in_specs=[inside] * (3 + count),
             out_specs=(outside, inside),
             scratch_shapes=[
-                pltpu.VMEM((groups, rows, tokens), jnp.float32),
-                pltpu.VMEM((rows, LANES), jnp.float32),
                 pltpu.VMEM((rows, LANES), jnp.bfloat16),
-                pltpu.VMEM((count, tokens, width), jnp.bfloat16),
                 pltpu.VMEM((count, rows, width), jnp.bfloat16),
-                pltpu.SemaphoreType.DMA((2,)),
-                pltpu.SemaphoreType.DMA((2 * count,)),
                 pltpu.SemaphoreType.DMA((2 * count + 1,)),
             ],
         ),
     )(place, onehots, gains, token, *blocks)
 
 
-def project_kernel(full, half, capacity, zs_ref, x_hbm, w_hbm, saved_hbm, scores_in, *refs):
-    hidden_hbm, scores_ref = refs[-12:-10]
-    x_ref, gain_ref, w_ref, saved_ref, y_ref, out_ref, x_sems, w_sems, saved_sems, out_sems = refs[-10:]
+def project_kernel(full, half, capacity, zs_ref, x_ref, w_ref, saved_ref, scores_in, *refs):
+    hidden_hbm, scores_ref, y_ref, out_ref, out_sems = refs[-5:]
     blocks, slots, units = out_ref.shape
-    middle = x_ref.shape[2]
+    features = w_ref.shape[1]
+    middle = features // 2
     width = y_ref.shape[1]
     chunks = units // width
     dims = (((1,), (1,)), ((), ()))
-    pieces = []
-    if full:
-        for c in range(2):
-            pieces.append((x_hbm.at[:, c * middle : (c + 1) * middle], x_ref.at[c, : 2 * slots]))
-    if half:
-        at = 2 * middle * full
-        for c in range(2):
-            pieces.append(
-                (x_hbm.at[c * slots : (c + 1) * slots, at : at + middle], x_ref.at[c, 2 * slots * full :])
-            )
-    at = middle * (2 * full + half)
-    pieces.append((x_hbm.at[:, at : at + LANES], gain_ref))
-    loads = [pltpu.make_async_copy(a, b, x_sems.at[i]) for i, (a, b) in enumerate(pieces)]
-    w_loads = [
-        pltpu.make_async_copy(
-            w_hbm.at[n * width : (n + 1) * width], w_ref.at[n * width : (n + 1) * width], w_sems.at[n]
-        )
-        for n in range(chunks)
-    ]
-    saved_loads = [
-        pltpu.make_async_copy(saved_hbm.at[zs_ref[j]], saved_ref.at[j], saved_sems.at[j]) for j in range(blocks)
-    ]
-    for load in loads + w_loads[:1] + saved_loads + w_loads[1:]:
-        load.start()
-
+    at = features * full
+    gain_at = at + middle * half
     def times(x, w):
         return lax.dot_general(x, w, dims, preferred_element_type=jnp.float32)
 
@@ -189,30 +148,31 @@
     own_lane = iota((slots, LANES), 1) == row % capacity
     sources = slots // capacity
     scores_ref[...] = scores_in[...]
-    for load in loads:
-        load.wait()
     gains, totals = [], []
     for j in range(blocks):
         whole = full and j < CORES
         top = j * slots if whole else 0
         lane = 0 if whole or not full else 1
-        column = gain_ref[top : top + slots, lane : lane + 1].astype(jnp.float32)
+        tile = x_ref[top : top + slots, gain_at : gain_at + LANES].astype(jnp.float32)
+        column = tile[:, lane : lane + 1]
         gains.append(jnp.broadcast_to(column, (slots, LANES)))
         totals.append(jnp.zeros((slots, LANES), jnp.float32))
 
     stores = []
     for n in range(chunks):
         here = slice(n * width, (n + 1) * width)
-        w_loads[n].wait()
-        y_ref[...] = times(x_ref[0], w_ref[here, :middle]) + times(x_ref[1], w_ref[here, middle:])
+        if full:
+            y_ref[: 2 * slots] = times(x_ref[:, :features], w_ref[here])
+        if half:
+            y_ref[2 * slots * full :] = times(x_ref[:slots, at : at + middle], w_ref[here, :middle]) + times(
+                x_ref[slots:, at : at + middle], w_ref[here, middle:]
+            )
         for j in range(blocks):
-            if n == 0:
-                saved_loads[j].wait()
             for i in range(0, width, LANES):
                 lanes = slice(n * width + i, n * width + i + LANES)
                 projected = y_ref[j * slots : (j + 1) * slots, i : i + LANES]
                 out_ref[j, :, lanes] = (gains[j] * projected).astype(jnp.bfloat16)
-                totals[j] += projected * saved_ref[j, :, lanes].astype(jnp.float32)
+                totals[j] += projected * saved_ref[zs_ref[j], :, lanes].astype(jnp.float32)
             store = pltpu.make_async_copy(
                 out_ref.at[j, :, here], hidden_hbm.at[zs_ref[j], :, here], out_sems.at[n * blocks + j]
             )
@@ -239,7 +199,7 @@
     width = 256
     inside = pl.BlockSpec(memory_space=pltpu.VMEM)
     outside = pl.BlockSpec(memory_space=pltpu.HBM)
-    in_specs = [outside] * 3 + [inside]
+    in_specs = [inside] * 4
     operands = [zs, rows, weight, saved, scores]
     aliases = {}
     if hidden is not None:
@@ -259,15 +219,8 @@
             in_specs=in_specs,
             out_specs=(outside, inside),
             scratch_shapes=[
-                pltpu.VMEM((2, count * slots, features // 2), jnp.bfloat16),
-                pltpu.VMEM((2 * slots, LANES), jnp.bfloat16),
-                pltpu.VMEM(weight.shape, weight.dtype),
-                pltpu.VMEM((count, slots, units), saved.dtype),
                 pltpu.VMEM((count * slots, width), jnp.float32),
                 pltpu.VMEM((count, slots, units), jnp.bfloat16),
-                pltpu.SemaphoreType.DMA((2 * full + 2 * half + 1,)),
-                pltpu.SemaphoreType.DMA((units // width,)),
-                pltpu.SemaphoreType.DMA((count,)),
                 pltpu.SemaphoreType.DMA((units // width * count,)),
             ],
         ),
@@ -331,23 +284,27 @@
         return lax.ppermute(block, ("z", "core"), pairs)
 
     reach = depth // 2
-    choices_at = [in_order(choices, choices_mate, 1)]
-    choices_at += [along(choices_at[0], k) for k in range(1, reach + 1)]
     place = jnp.stack([z, core])
     rows = local * CORES * capacity
     inside = pl.BlockSpec(memory_space=pltpu.VMEM)
-    onehots, gains, token = call(
-        partial(match_kernel, capacity),
-        (
-            jax.ShapeDtypeStruct((reach + 1, rows, CORES * tokens), jnp.float32),
-            jax.ShapeDtypeStruct((reach, rows, LANES), jnp.float32),
-            jax.ShapeDtypeStruct((8, LANES), jnp.float32),
-        ),
-        (10**6, 10**5),
-        grid_spec=pltpu.PrefetchScalarGridSpec(
-            num_scalar_prefetch=1, in_specs=[inside] * (reach + 1), out_specs=(inside,) * 3
-        ),
-    )(place, *choices_at)
+
+    def match(choices_at):
+        count = len(choices_at)
+        return call(
+            partial(match_kernel, capacity),
+            (
+                jax.ShapeDtypeStruct((count, rows, CORES * tokens), jnp.float32),
+                jax.ShapeDtypeStruct((max(1, count - 1), rows, LANES), jnp.float32),
+                jax.ShapeDtypeStruct((8, LANES), jnp.float32),
+            ),
+            (10**6, 10**5),
+            grid_spec=pltpu.PrefetchScalarGridSpec(
+                num_scalar_prefetch=1, in_specs=[inside] * count, out_specs=(inside,) * 3
+            ),
+        )(place, *choices_at)
+
+    choices = in_order(choices, choices_mate, 1)
+    onehots, gains, token = match([choices])
 
     def exchange(block, axes, parts):
         shape = block.shape
@@ -364,23 +321,26 @@
     def at(*distances):
         return jnp.stack([(z + d) % depth for d in distances])
 
-    def columns(blocks, parts, micros):
+    def columns(onehots, gains, token, blocks, parts, micros):
         rows, after = select_rows(place, onehots, gains, token, blocks, parts, micros)
         return exchange(rows, ("core", "x"), local), after
 
     groups = []
     same, cross = along(held, 1), along(held, 1, cross=True)
-    got, token = columns([held], (0,), COSTS[0])
+    got, token = columns(onehots, gains, token, [held], (0,), COSTS[0])
+    choices, token = lax.optimization_barrier((choices, token))
+    onehots, gains, matched = match([along(choices, k) for k in range(1, reach + 1)])
+    token += matched
     groups.append((got, at(0), 0, 1))
     for k in range(1, reach - 1):
         same, cross, token = lax.optimization_barrier((same, cross, token))
         ahead = along(same, 1), along(cross, 1)
-        got, token = columns([same, cross], (k, k), COSTS[k])
+        got, token = columns(onehots, gains, token, [same, cross], (k - 1, k - 1), COSTS[k])
         groups.append((got, at(-k, k), 1, 0))
         same, cross = ahead
     k = reach - 1
     same, cross, token = lax.optimization_barrier((same, cross, token))
-    got, token = columns([same, cross, along(same, 1)], (k, k, k + 1), COSTS[k])
+    got, token = columns(onehots, gains, token, [same, cross, along(same, 1)], (k - 1, k - 1, k), COSTS[k])
     groups.append((got, at(-k, k, reach), 1, 1))
 
     hidden = None

time: 218 us -> 221 us (1.014); the launches traced: 214 us -> 220 us
  Pallas kernels: 75 us -> 37.6 us
  waiting for transfers between devices: 60.6 us -> 84.2 us
  local copies, waits for them, and re-layouts: 7.65 us -> 26 us
    pallas_call x4, Pallas kernels: 47.7 us -> 21.4 us  [project(): call(partial(project_kernel, full, half, capacity), (jax.ShapeDtypeStruct...]
    unnamed x24 -> x44, local copies, waits for them, and re-layouts: 5.82 us -> 24.8 us
    ppermute x1, waiting for transfers between devices: 0.01 us -> 15.2 us  [on_device(): lax.ppermute(mine, ('pipe', 'core'), [(i * CORES + c, (i - 1) * CORES + c...]
    all_to_all x4, waiting for transfers between devices: 27 us -> 39.1 us  [exchange(): lax.all_to_all(block, axes, split_axis=0, concat_axis=0, tiled=True)]
    pallas_call x4, Pallas kernels: 22.3 us -> 13.6 us  [select_rows(): call(partial(select_kernel, parts), (jax.ShapeDtypeStruct((rows, width *...]
    ppermute x11, waiting for transfers between devices: 32.8 us -> 29.1 us  [along(): return lax.ppermute(block, ('z', 'core'), pairs)]
  transfers between devices with their start and end apart: 19 -> 19, of which waited for: 9 -> 9; matrix products, arithmetic and copies ran while one was open for 2% -> 1% of each run, Pallas kernels for 27% -> 13%
where the time goes in v3:
time: 221 us; the launch traced here: 220 us
  waiting for transfers between devices  84.2 us (38%)
  starting transfers between devices  49.8 us (23%)
  Pallas kernels  37.6 us (17%)
  local copies, waits for them, and re-layouts  26 us (12%)
  blocking collectives  18.5 us (8%)
  other arithmetic  2.78 us (1%)
    all_to_all x4, waiting for transfers between devices, exchange(): lax.all_to_all(block, axes, split_axis=0, concat_axis=0, tiled=True)  39.1 us
    ppermute x11, waiting for transfers between devices, along(): return lax.ppermute(block, ('z', 'core'), pairs)  29.1 us
    unnamed x44, local copies, waits for them, and re-layouts  24.8 us
    ppermute x11, starting transfers between devices, along(): return lax.ppermute(block, ('z', 'core'), pairs)  24 us
    pallas_call x4, Pallas kernels, project(): call(partial(project_kernel, full, half, capacity), (jax.ShapeDtypeStruct...  21.4 us
    all_to_all x4, starting transfers between devices, exchange(): lax.all_to_all(block, axes, split_axis=0, concat_axis=0, tiled=True)  19.3 us
    all_to_all x1, blocking collectives, exchange(): lax.all_to_all(block, axes, split_axis=0, concat_axis=0, tiled=True)  18.5 us
    ppermute x1, waiting for transfers between devices, on_device(): lax.ppermute(mine, ('pipe', 'core'), [(i * CORES + c, (i - 1) * CORES + c...  15.2 us
  transfers between devices with their start and end apart: 19, of which 9 were waited for; matrix products, arithmetic and copies ran while one was open for 1% of the time, Pallas kernels for 13%

profile of v3, /device:TPU:1, one launch (start us, length us, event | category | flops | bytes accessed | tf_op | source)
XLA Modules:
  0.0 219.8 jit_solution(16407272752390222715)
XLA Ops:
  6.5 3.2 %collective-permute-start = (f32[16,128]{1,0:T(8,128)S(1)}, f32[16,128]{1,0:T(8,128)S(1)}, u32[]{:S(2)}, u32[]{:S(2)}) collective-permute-start(f32[16,128]{1,0:T(8,128)S(1)} %pad_maximum_fusion), channel_id=1, source_target_pairs={{0,1},{1,0},{2,3},{3,2},{4,5},{5,4},{6,7},{7,6},{8,9},{9,8},{10,11... | collective-permute-start | bytes 24584 | tf_op jit(solution)/shard_map/ppermute | solution.py:274
  12.2 15.2 %collective-permute-done.1 = bf16[128,1792]{1,0:T(8,128)(2,1)S(1)} collective-permute-done((bf16[128,1792]{1,0:T(8,128)(2,1)S(1)}, bf16[128,1792]{1,0:T(8,128)(2,1)S(1)}, u32[]{:S(2)}, u32[]{:S(2)}) %collective-permute-start.1) | collective-permute-done | bytes 458784 | tf_op jit(solution)/shard_map/ppermute | solution.py:267
  27.7 5.7 %collective-permute-start.8 = (bf16[256,1792]{1,0:T(8,128)(2,1)S(1)}, bf16[256,1792]{1,0:T(8,128)(2,1)S(1)}, u32[]{:S(2)}, u32[]{:S(2)}) collective-permute-start(bf16[256,1792]{1,0:T(8,128)(2,1)S(1)} %maximum_select_fusion.refs_0_), channel_id=1, source_target_pairs={{0,8},{1,57},{8,16},{9,1},{16,24},{17,9},{24,32},{25,17},{32,40},{... | collective-permute-start | bytes 2752520 | tf_op jit(solution)/shard_map/ppermute | solution.py:284
  33.4 1.9 shard_map.69
  35.3 5.4 %all-to-all-start.3 = ((bf16[8,40,1920]{2,1,0:T(8,128)(2,1)}), bf16[8,40,1920]{2,1,0:T(8,128)(2,1)S(1)}, u32[]{:S(2)}, u32[]{:S(2)}) async-start(bf16[8,40,1920]{2,1,0:T(8,128)(2,1)} %bitcast.24), calls=%async_computation.3 | async-start | bytes 2457600 | tf_op jit(solution)/shard_map/all_to_all | solution.py:312
  43.1 2.8 %collective-permute-start.6 = (f32[16,256]{1,0:T(8,128)S(1)}, f32[16,256]{1,0:T(8,128)S(1)}, u32[]{:S(2)}, u32[]{:S(2)}) collective-permute-start(f32[16,256]{1,0:T(8,128)S(1)} %maximum_select_fusion.1.refs_0_), channel_id=1, source_target_pairs={{0,24},{1,41},{8,32},{9,49},{16,40},{17,57},{24,48},{25,1},{32,56}... | collective-permute-start | bytes 49160 | tf_op jit(solution)/shard_map/ppermute | solution.py:284
  45.9 7.2 %collective-permute-done.4.refs_0_ = f32[16,256]{1,0:T(8,128)S(1)} collective-permute-done((f32[16,256]{1,0:T(8,128)S(1)}, f32[16,256]{1,0:T(8,128)S(1)}, u32[]{:S(2)}, u32[]{:S(2)}) %collective-permute-start.4) | collective-permute-done | bytes 16416 | tf_op jit(solution)/shard_map/ppermute | solution.py:284
  53.1 3.4 %collective-permute-start.7 = (f32[16,256]{1,0:T(8,128)S(1)}, f32[16,256]{1,0:T(8,128)S(1)}, u32[]{:S(2)}, u32[]{:S(2)}) collective-permute-start(f32[16,256]{1,0:T(8,128)S(1)} %maximum_select_fusion.1.refs_0_), channel_id=1, source_target_pairs={{0,32},{1,33},{8,40},{9,41},{16,48},{17,49},{24,56},{25,57},{32,0}... | collective-permute-start | bytes 49160 | tf_op jit(solution)/shard_map/ppermute | solution.py:284
  56.5 3.2 %collective-permute-done.7.refs_3_ = f32[16,256]{1,0:T(8,128)S(1)} collective-permute-done((f32[16,256]{1,0:T(8,128)S(1)}, f32[16,256]{1,0:T(8,128)S(1)}, u32[]{:S(2)}, u32[]{:S(2)}) %collective-permute-start.7) | collective-permute-done | bytes 16416 | tf_op jit(solution)/shard_map/ppermute | solution.py:284
  60.7 3.4 %collective-permute-start.10 = (bf16[256,1792]{1,0:T(8,128)(2,1)S(1)}, bf16[256,1792]{1,0:T(8,128)(2,1)}, u32[]{:S(2)}, u32[]{:S(2)}) collective-permute-start(bf16[256,1792]{1,0:T(8,128)(2,1)S(1)} %collective-permute-done.8.refs_0_), channel_id=1, source_target_pairs={{0,8},{1,57},{8,16},{9,1},{16,24},{17,9},{24,32},{25,17},{32,40},{... | collective-permute-start | bytes 2752520 | tf_op jit(solution)/shard_map/ppermute | solution.py:284
  64.2 3.3 %shard_map.71 = (bf16[320,3712]{1,0:T(8,128)(2,1)S(1)}, f32[8,128]{1,0:T(8,128)S(1)}) custom-call(s32[2]{0:T(128)S(1)} %pad_add_fusion.1.place_ref, f32[4,320,256]{2,1,0:T(8,128)S(1)} %get-tuple-element.47.onehot_ref, f32[3,320,128]{2,1,0:T(8,128)S(1)} %get-tuple-element.48.gain_in, f32[8,128]{1,0:T(8,128)S(1)} %add.63.token_ref, ...), custom_call_target="tpu_custom_call" | custom-call | flops 3300000000 | bytes 4128768 | tf_op jit(solution)/shard_map/pallas_call | solution.py:114
  71.8 4.6 %all-to-all-start.2 = ((bf16[8,40,3712]{2,1,0:T(8,128)(2,1)}), bf16[8,40,3712]{2,1,0:T(8,128)(2,1)S(1)}, u32[]{:S(2)}, u32[]{:S(2)}) async-start(bf16[8,40,3712]{2,1,0:T(8,128)(2,1)} %bitcast.53), calls=%async_computation.2 | async-start | bytes 4751360 | tf_op jit(solution)/shard_map/all_to_all | solution.py:312
  76.4 8.0 %collective-permute-done.11.refs_1_ = bf16[256,1792]{1,0:T(8,128)(2,1)} collective-permute-done((bf16[256,1792]{1,0:T(8,128)(2,1)}, bf16[256,1792]{1,0:T(8,128)(2,1)}, u32[]{:S(2)}, u32[]{:S(2)}) %collective-permute-start.11) | collective-permute-done | bytes 917536 | tf_op jit(solution)/shard_map/ppermute | solution.py:284
  84.4 3.3 %collective-permute-start.12 = (bf16[256,1792]{1,0:T(8,128)(2,1)}, bf16[256,1792]{1,0:T(8,128)(2,1)S(1)}, u32[]{:S(2)}, u32[]{:S(2)}) collective-permute-start(bf16[256,1792]{1,0:T(8,128)(2,1)} %collective-permute-done.10.refs_0_), channel_id=1, source_target_pairs={{0,8},{1,57},{8,16},{9,1},{16,24},{17,9},{24,32},{25,17},{32,40},{... | collective-permute-start | bytes 2752520 | tf_op jit(solution)/shard_map/ppermute | solution.py:284
  90.0 3.6 %shard_map.72 = (bf16[320,3712]{1,0:T(8,128)(2,1)S(1)}, f32[8,128]{1,0:T(8,128)S(1)}) custom-call(s32[2]{0:T(128)S(1)} %pad_add_fusion.1.place_ref, f32[4,320,256]{2,1,0:T(8,128)S(1)} %copy-done.15, f32[3,320,128]{2,1,0:T(8,128)S(1)} %copy-done.18, f32[8,128]{1,0:T(8,128)S(1)} %get-tuple-element.57.token_ref, ...), custom_call_target="tpu_custom_call" | custom-call | flops 15399999488 | bytes 4128768 | tf_op jit(solution)/shard_map/pallas_call | solution.py:114
  95.1 10.9 %all-to-all-done.2 = bf16[8,40,3712]{2,1,0:T(8,128)(2,1)S(1)} async-done(((bf16[8,40,3712]{2,1,0:T(8,128)(2,1)}), bf16[8,40,3712]{2,1,0:T(8,128)(2,1)S(1)}, u32[]{:S(2)}, u32[]{:S(2)}) %all-to-all-start.2) | async-done | bytes 2375712 | tf_op jit(solution)/shard_map/all_to_all | solution.py:312
  107.4 4.3 %all-to-all-start.1 = ((bf16[8,40,3712]{2,1,0:T(8,128)(2,1)}), bf16[8,40,3712]{2,1,0:T(8,128)(2,1)}, u32[]{:S(2)}, u32[]{:S(2)}) async-start(bf16[8,40,3712]{2,1,0:T(8,128)(2,1)} %bitcast.52), calls=%async_computation.1 | async-start | bytes 4751360 | tf_op jit(solution)/shard_map/all_to_all | solution.py:312
  111.8 2.9 %collective-permute-start.14 = (bf16[256,1792]{1,0:T(8,128)(2,1)S(1)}, bf16[256,1792]{1,0:T(8,128)(2,1)S(1)}, u32[]{:S(2)}, u32[]{:S(2)}) collective-permute-start(bf16[256,1792]{1,0:T(8,128)(2,1)S(1)} %collective-permute-done.12.refs_0_), channel_id=1, source_target_pairs={{0,8},{1,57},{8,16},{9,1},{16,24},{17,9},{24,32},{25,17},{32,40},{... | collective-permute-start | bytes 2752520 | tf_op jit(solution)/shard_map/ppermute | solution.py:284
  114.7 10.8 %collective-permute-done.14.refs_2_ = bf16[256,1792]{1,0:T(8,128)(2,1)S(1)} collective-permute-done((bf16[256,1792]{1,0:T(8,128)(2,1)S(1)}, bf16[256,1792]{1,0:T(8,128)(2,1)S(1)}, u32[]{:S(2)}, u32[]{:S(2)}) %collective-permute-start.14) | collective-permute-done | bytes 917536 | tf_op jit(solution)/shard_map/ppermute | solution.py:284
  127.8 4.7 %shard_map.73 = (bf16[320,5504]{1,0:T(8,128)(2,1)S(1)}, f32[8,128]{1,0:T(8,128)}) custom-call(s32[2]{0:T(128)S(1)} %pad_add_fusion.1.place_ref, f32[4,320,256]{2,1,0:T(8,128)S(1)} %copy-done.16, f32[3,320,128]{2,1,0:T(8,128)S(1)} %copy-done.19, f32[8,128]{1,0:T(8,128)S(1)} %get-tuple-element.59.token_ref, ...), custom_call_target="tpu_custom_call" | custom-call | flops 8800000000 | bytes 6193152 | tf_op jit(solution)/shard_map/pallas_call | solution.py:114
  132.5 1.7 copy-done.9
  134.2 6.7 %all-to-all-done.1 = bf16[8,40,3712]{2,1,0:T(8,128)(2,1)} async-done(((bf16[8,40,3712]{2,1,0:T(8,128)(2,1)}), bf16[8,40,3712]{2,1,0:T(8,128)(2,1)}, u32[]{:S(2)}, u32[]{:S(2)}) %all-to-all-start.1) | async-done | bytes 2375712 | tf_op jit(solution)/shard_map/all_to_all | solution.py:312
  141.0 5.0 %all-to-all-start = ((bf16[8,40,5504]{2,1,0:T(8,128)(2,1)}), bf16[8,40,5504]{2,1,0:T(8,128)(2,1)}, u32[]{:S(2)}, u32[]{:S(2)}) async-start(bf16[8,40,5504]{2,1,0:T(8,128)(2,1)} %bitcast.51), calls=%async_computation | async-start | bytes 7045120 | tf_op jit(solution)/shard_map/all_to_all | solution.py:312
  146.2 3.1 %copy-done = bf16[1,1,1024,3584]{3,2,1,0:T(8,128)(2,1)S(1)} copy-done((bf16[1,1,1024,3584]{3,2,1,0:T(8,128)(2,1)S(1)}, bf16[1,1,1024,3584]{3,2,1,0:T(8,128)(2,1)}, u32[]{:S(2)}) %copy-start) | copy-done | bytes 7340056
  149.3 1.7 copy-done.2
  152.3 3.4 %shard_map.74 = (bf16[8,160,1024]{2,1,0:T(8,128)(2,1)}, f32[64,128]{1,0:T(8,128)S(1)}) custom-call(s32[1]{0:T(128)} %bitcast.23.zs_ref, bf16[320,1920]{1,0:T(8,128)(2,1)S(1)} %bitcast.50, bf16[1024,3584]{1,0:T(8,128)(2,1)S(1)} %bitcast.39, bf16[8,160,1024]{2,1,0:T(8,128)(2,1)S(1)} %bitcast.45, f32[64,128]{1,0:T(8,128)S(1)} %broadcast_in_dim.6.scores_in), custom_call_target="tpu_custom_call" | custom-call | flops 1258291200 | bytes 9224192 | tf_op jit(solution)/shard_map/pallas_call | solution.py:209
  156.0 4.2 %shard_map.75 = (bf16[8,160,1024]{2,1,0:T(8,128)(2,1)}, f32[64,128]{1,0:T(8,128)S(1)}) custom-call(s32[2]{0:T(128)S(1)} %pad_add_fusion.3.zs_ref, bf16[320,3712]{1,0:T(8,128)(2,1)S(1)} %bitcast.49, bf16[1024,3584]{1,0:T(8,128)(2,1)S(1)} %bitcast.42, bf16[8,160,1024]{2,1,0:T(8,128)(2,1)S(1)} %bitcast.46, ...), custom_call_target="tpu_custom_call", output_to_operand_aliasing={{0}: (5, {})} | custom-call | flops 2432696320 | bytes 11026432 | tf_op jit(solution)/shard_map/pallas_call | solution.py:209
  160.2 5.8 %shard_map.76 = (bf16[8,160,1024]{2,1,0:T(8,128)(2,1)}, f32[64,128]{1,0:T(8,128)S(1)}) custom-call(s32[2]{0:T(128)S(1)} %pad_add_fusion.2.zs_ref, bf16[320,3712]{1,0:T(8,128)(2,1)} %bitcast.18.x_ref, bf16[1024,3584]{1,0:T(8,128)(2,1)S(1)} %bitcast.43, bf16[8,160,1024]{2,1,0:T(8,128)(2,1)S(1)} %bitcast.47, ...), custom_call_target="tpu_custom_call", output_to_operand_aliasing={{0}: (5, {})} | custom-call | flops 2432696320 | bytes 11026432 | tf_op jit(solution)/shard_map/pallas_call | solution.py:209
  166.0 21.5 %all-to-all-done = bf16[8,40,5504]{2,1,0:T(8,128)(2,1)} async-done(((bf16[8,40,5504]{2,1,0:T(8,128)(2,1)}), bf16[8,40,5504]{2,1,0:T(8,128)(2,1)}, u32[]{:S(2)}, u32[]{:S(2)}) %all-to-all-start) | async-done | bytes 3522592 | tf_op jit(solution)/shard_map/all_to_all | solution.py:312
  187.6 3.1 %copy-done.1 = bf16[1,1,1024,3584]{3,2,1,0:T(8,128)(2,1)S(1)} copy-done((bf16[1,1,1024,3584]{3,2,1,0:T(8,128)(2,1)S(1)}, bf16[1,1,1024,3584]{3,2,1,0:T(8,128)(2,1)}, u32[]{:S(2)}) %copy-start.1) | copy-done | bytes 7340056
  192.4 8.0 %shard_map.77 = (bf16[8,160,1024]{2,1,0:T(8,128)(2,1)}, f32[64,128]{1,0:T(8,128)S(1)}) custom-call(s32[3]{0:T(128)S(1)} %pad_add_fusion.zs_ref, bf16[320,5504]{1,0:T(8,128)(2,1)} %bitcast.12.x_ref, bf16[1024,3584]{1,0:T(8,128)(2,1)S(1)} %bitcast.44, bf16[8,160,1024]{2,1,0:T(8,128)(2,1)S(1)} %bitcast.48, ...), custom_call_target="tpu_custom_call", output_to_operand_aliasing={{0}: (5, {})} | custom-call | flops 3607101440 | bytes 12828672 | tf_op jit(solution)/shard_map/pallas_call | solution.py:209
  200.4 18.5 %all_to_all.25 = f32[64,1,128]{2,1,0:T(1,128)S(1)} all-to-all(f32[64,1,128]{2,1,0:T(1,128)S(1)} %bitcast.58), channel_id=1, replica_groups=mesh['pipe'=4,'z'=8,'x'=4,'core'=2] {'z','x','core'}, dimensions={0} | all-to-all | bytes 65536 | tf_op jit(solution)/shard_map/all_to_all | solution.py:312
  (75 shorter events, 28.4 us)
Async XLA Ops:
  1.9 25.5 %collective-permute-start.2 = (bf16[128,1792]{1,0:T(8,128)(2,1)S(1)}, bf16[128,1792]{1,0:T(8,128)(2,1)S(1)}, u32[]{:S(2)}, u32[]{:S(2)}) collective-permute-start(bf16[128,1792]{1,0:T(8,128)(2,1)S(1)} %get-tuple-element.74), channel_id=1, source_target_pairs={{64,1},{65,0},{128,65},{129,64},{192,129},{193,128},{66,3},{67,2},... | collective-permute-start | bytes 1376264 | tf_op jit(solution)/shard_map/ppermute | solution.py:268
  3.2 24.2 %collective-permute-start.3 = (bf16[128,1792]{1,0:T(8,128)(2,1)S(1)}, bf16[128,1792]{1,0:T(8,128)(2,1)S(1)}, u32[]{:S(2)}, u32[]{:S(2)}) collective-permute-start(bf16[128,1792]{1,0:T(8,128)(2,1)S(1)} %get-tuple-element.74), channel_id=1, source_target_pairs={{192,193},{193,192},{194,195},{195,194},{196,197},{197,196},{198,1... | collective-permute-start | bytes 1376264 | tf_op jit(solution)/shard_map/ppermute | solution.py:269
  3.9 23.5 %collective-permute-start.1 = (bf16[128,1792]{1,0:T(8,128)(2,1)S(1)}, bf16[128,1792]{1,0:T(8,128)(2,1)S(1)}, u32[]{:S(2)}, u32[]{:S(2)}) collective-permute-start(bf16[128,1792]{1,0:T(8,128)(2,1)S(1)} %get-tuple-element.75), channel_id=1, source_target_pairs={{64,0},{65,1},{128,64},{129,65},{192,128},{193,129},{66,2},{67,3},... | collective-permute-start | bytes 1376264 | tf_op jit(solution)/shard_map/ppermute | solution.py:267
  6.5 4.1 %collective-permute-start = (f32[16,128]{1,0:T(8,128)S(1)}, f32[16,128]{1,0:T(8,128)S(1)}, u32[]{:S(2)}, u32[]{:S(2)}) collective-permute-start(f32[16,128]{1,0:T(8,128)S(1)} %pad_maximum_fusion), channel_id=1, source_target_pairs={{0,1},{1,0},{2,3},{3,2},{4,5},{5,4},{6,7},{7,6},{8,9},{9,8},{10,11... | collective-permute-start | bytes 24584 | tf_op jit(solution)/shard_map/ppermute | solution.py:274
  27.7 33.0 %collective-permute-start.8 = (bf16[256,1792]{1,0:T(8,128)(2,1)S(1)}, bf16[256,1792]{1,0:T(8,128)(2,1)S(1)}, u32[]{:S(2)}, u32[]{:S(2)}) collective-permute-start(bf16[256,1792]{1,0:T(8,128)(2,1)S(1)} %maximum_select_fusion.refs_0_), channel_id=1, source_target_pairs={{0,8},{1,57},{8,16},{9,1},{16,24},{17,9},{24,32},{25,17},{32,40},{... | collective-permute-start | bytes 2752520 | tf_op jit(solution)/shard_map/ppermute | solution.py:284
  33.4 27.3 %collective-permute-start.9 = (bf16[256,1792]{1,0:T(8,128)(2,1)S(1)}, bf16[256,1792]{1,0:T(8,128)(2,1)}, u32[]{:S(2)}, u32[]{:S(2)}) collective-permute-start(bf16[256,1792]{1,0:T(8,128)(2,1)S(1)} %maximum_select_fusion.refs_0_), channel_id=1, source_target_pairs={{1,8},{0,57},{9,16},{8,1},{17,24},{16,9},{25,32},{24,17},{33,40},{... | collective-permute-start | bytes 2752520 | tf_op jit(solution)/shard_map/ppermute | solution.py:284
  35.3 35.4 %all-to-all-start.3 = ((bf16[8,40,1920]{2,1,0:T(8,128)(2,1)}), bf16[8,40,1920]{2,1,0:T(8,128)(2,1)S(1)}, u32[]{:S(2)}, u32[]{:S(2)}) async-start(bf16[8,40,1920]{2,1,0:T(8,128)(2,1)} %bitcast.24), calls=%async_computation.3 | async-start | bytes 2457600 | tf_op jit(solution)/shard_map/all_to_all | solution.py:312
  40.7 12.4 %collective-permute-start.4 = (f32[16,256]{1,0:T(8,128)S(1)}, f32[16,256]{1,0:T(8,128)S(1)}, u32[]{:S(2)}, u32[]{:S(2)}) collective-permute-start(f32[16,256]{1,0:T(8,128)S(1)} %maximum_select_fusion.1.refs_0_), channel_id=1, source_target_pairs={{0,8},{1,57},{8,16},{9,1},{16,24},{17,9},{24,32},{25,17},{32,40},{... | collective-permute-start | bytes 49160 | tf_op jit(solution)/shard_map/ppermute | solution.py:284
  41.4 15.1 %collective-permute-start.5 = (f32[16,256]{1,0:T(8,128)S(1)}, f32[16,256]{1,0:T(8,128)S(1)}, u32[]{:S(2)}, u32[]{:S(2)}) collective-permute-start(f32[16,256]{1,0:T(8,128)S(1)} %maximum_select_fusion.1.refs_0_), channel_id=1, source_target_pairs={{0,16},{1,49},{8,24},{9,57},{16,32},{17,1},{24,40},{25,9},{32,48},... | collective-permute-start | bytes 49160 | tf_op jit(solution)/shard_map/ppermute | solution.py:284
  43.1 13.5 %collective-permute-start.6 = (f32[16,256]{1,0:T(8,128)S(1)}, f32[16,256]{1,0:T(8,128)S(1)}, u32[]{:S(2)}, u32[]{:S(2)}) collective-permute-start(f32[16,256]{1,0:T(8,128)S(1)} %maximum_select_fusion.1.refs_0_), channel_id=1, source_target_pairs={{0,24},{1,41},{8,32},{9,49},{16,40},{17,57},{24,48},{25,1},{32,56}... | collective-permute-start | bytes 49160 | tf_op jit(solution)/shard_map/ppermute | solution.py:284
  53.1 6.6 %collective-permute-start.7 = (f32[16,256]{1,0:T(8,128)S(1)}, f32[16,256]{1,0:T(8,128)S(1)}, u32[]{:S(2)}, u32[]{:S(2)}) collective-permute-start(f32[16,256]{1,0:T(8,128)S(1)} %maximum_select_fusion.1.refs_0_), channel_id=1, source_target_pairs={{0,32},{1,33},{8,40},{9,41},{16,48},{17,49},{24,56},{25,57},{32,0}... | collective-permute-start | bytes 49160 | tf_op jit(solution)/shard_map/ppermute | solution.py:284
  60.7 15.7 %collective-permute-start.10 = (bf16[256,1792]{1,0:T(8,128)(2,1)S(1)}, bf16[256,1792]{1,0:T(8,128)(2,1)}, u32[]{:S(2)}, u32[]{:S(2)}) collective-permute-start(bf16[256,1792]{1,0:T(8,128)(2,1)S(1)} %collective-permute-done.8.refs_0_), channel_id=1, source_target_pairs={{0,8},{1,57},{8,16},{9,1},{16,24},{17,9},{24,32},{25,17},{32,40},{... | collective-permute-start | bytes 2752520 | tf_op jit(solution)/shard_map/ppermute | solution.py:284
  64.1 20.3 %collective-permute-start.11 = (bf16[256,1792]{1,0:T(8,128)(2,1)}, bf16[256,1792]{1,0:T(8,128)(2,1)}, u32[]{:S(2)}, u32[]{:S(2)}) collective-permute-start(bf16[256,1792]{1,0:T(8,128)(2,1)} %collective-permute-done.9.refs_1_), channel_id=1, source_target_pairs={{0,8},{1,57},{8,16},{9,1},{16,24},{17,9},{24,32},{25,17},{32,40},{... | collective-permute-start | bytes 2752520 | tf_op jit(solution)/shard_map/ppermute | solution.py:284
  71.8 34.2 %all-to-all-start.2 = ((bf16[8,40,3712]{2,1,0:T(8,128)(2,1)}), bf16[8,40,3712]{2,1,0:T(8,128)(2,1)S(1)}, u32[]{:S(2)}, u32[]{:S(2)}) async-start(bf16[8,40,3712]{2,1,0:T(8,128)(2,1)} %bitcast.53), calls=%async_computation.2 | async-start | bytes 4751360 | tf_op jit(solution)/shard_map/all_to_all | solution.py:312
  84.4 27.4 %collective-permute-start.12 = (bf16[256,1792]{1,0:T(8,128)(2,1)}, bf16[256,1792]{1,0:T(8,128)(2,1)S(1)}, u32[]{:S(2)}, u32[]{:S(2)}) collective-permute-start(bf16[256,1792]{1,0:T(8,128)(2,1)} %collective-permute-done.10.refs_0_), channel_id=1, source_target_pairs={{0,8},{1,57},{8,16},{9,1},{16,24},{17,9},{24,32},{25,17},{32,40},{... | collective-permute-start | bytes 2752520 | tf_op jit(solution)/shard_map/ppermute | solution.py:284
  87.7 24.1 %collective-permute-start.13 = (bf16[256,1792]{1,0:T(8,128)(2,1)}, bf16[256,1792]{1,0:T(8,128)(2,1)}, u32[]{:S(2)}, u32[]{:S(2)}) collective-permute-start(bf16[256,1792]{1,0:T(8,128)(2,1)} %collective-permute-done.11.refs_1_), channel_id=1, source_target_pairs={{0,8},{1,57},{8,16},{9,1},{16,24},{17,9},{24,32},{25,17},{32,40},{... | collective-permute-start | bytes 2752520 | tf_op jit(solution)/shard_map/ppermute | solution.py:284
  93.7 1.4 copy-start.10
  106.0 1.4 copy-start.5
  107.4 33.5 %all-to-all-start.1 = ((bf16[8,40,3712]{2,1,0:T(8,128)(2,1)}), bf16[8,40,3712]{2,1,0:T(8,128)(2,1)}, u32[]{:S(2)}, u32[]{:S(2)}) async-start(bf16[8,40,3712]{2,1,0:T(8,128)(2,1)} %bitcast.52), calls=%async_computation.1 | async-start | bytes 4751360 | tf_op jit(solution)/shard_map/all_to_all | solution.py:312
  111.8 13.6 %collective-permute-start.14 = (bf16[256,1792]{1,0:T(8,128)(2,1)S(1)}, bf16[256,1792]{1,0:T(8,128)(2,1)S(1)}, u32[]{:S(2)}, u32[]{:S(2)}) collective-permute-start(bf16[256,1792]{1,0:T(8,128)(2,1)S(1)} %collective-permute-done.12.refs_0_), channel_id=1, source_target_pairs={{0,8},{1,57},{8,16},{9,1},{16,24},{17,9},{24,32},{25,17},{32,40},{... | collective-permute-start | bytes 2752520 | tf_op jit(solution)/shard_map/ppermute | solution.py:284
  132.5 1.8 copy-start.9
  140.9 14.8 %slice-start = ((s8[7340032]{0:T(1024)(128)(4,1)}), s8[3145728]{0:T(1024)(128)(4,1)S(1)}, s32[]{:S(2)}) async-start(s8[7340032]{0:T(1024)(128)(4,1)} %bitcast.40), calls=%async_computation.5 | async-start | bytes 6291456
  141.0 46.6 %all-to-all-start = ((bf16[8,40,5504]{2,1,0:T(8,128)(2,1)}), bf16[8,40,5504]{2,1,0:T(8,128)(2,1)}, u32[]{:S(2)}, u32[]{:S(2)}) async-start(bf16[8,40,5504]{2,1,0:T(8,128)(2,1)} %bitcast.51), calls=%async_computation | async-start | bytes 7045120 | tf_op jit(solution)/shard_map/all_to_all | solution.py:312
  146.2 3.1 %copy-start = (bf16[1,1,1024,3584]{3,2,1,0:T(8,128)(2,1)S(1)}, bf16[1,1,1024,3584]{3,2,1,0:T(8,128)(2,1)}, u32[]{:S(2)}) copy-start(bf16[1,1,1024,3584]{3,2,1,0:T(8,128)(2,1)} %param.8) | copy-start | bytes 22020100
  149.3 1.7 copy-start.2
  152.3 3.4 %slice-start.1 = ((s8[7340032]{0:T(1024)(128)(4,1)}), s8[4194304]{0:T(1024)(128)(4,1)S(1)}, s32[]{:S(2)}) async-start(s8[7340032]{0:T(1024)(128)(4,1)} %bitcast.40), calls=%async_computation.6 | async-start | bytes 8388608
  152.3 3.4 %copy-start.3 = (bf16[1,1,1280,1024]{3,2,1,0:T(8,128)(2,1)S(1)}, bf16[1,1,1280,1024]{3,2,1,0:T(8,128)(2,1)}, u32[]{:S(2)}) copy-start(bf16[1,1,1280,1024]{3,2,1,0:T(8,128)(2,1)} %param.9) | copy-start | bytes 7864324
  152.3 3.7 %copy-start.6 = (bf16[8,40,3712]{2,1,0:T(8,128)(2,1)S(1)}, bf16[8,40,3712]{2,1,0:T(8,128)(2,1)}, u32[]{:S(2)}) copy-start(bf16[8,40,3712]{2,1,0:T(8,128)(2,1)} %copy-done.5) | copy-start | bytes 7127044
  187.6 3.1 %copy-start.1 = (bf16[1,1,1024,3584]{3,2,1,0:T(8,128)(2,1)S(1)}, bf16[1,1,1024,3584]{3,2,1,0:T(8,128)(2,1)}, u32[]{:S(2)}) copy-start(bf16[1,1,1024,3584]{3,2,1,0:T(8,128)(2,1)} %param.8) | copy-start | bytes 22020100
  190.6 1.7 copy-start.4
  192.4 26.5 %copy-start.12 = (f32[1,128,8]{1,2,0:T(8,128)S(1)}, f32[1,128,8]{1,2,0:T(8,128)}, u32[]{:S(2)}) copy-start(f32[1,128,8]{1,2,0:T(8,128)} %param.7) | copy-start | bytes 12292
  192.4 26.5 %copy-start.13 = (s32[1,128,8]{1,2,0:T(8,128)S(1)}, s32[1,128,8]{1,2,0:T(8,128)}, u32[]{:S(2)}) copy-start(s32[1,128,8]{1,2,0:T(8,128)} %param.6) | copy-start | bytes 12292
  (9 other events, 10.3 us)

commit v4 on v3

v4 whole, which is shorter than its diff:
```python
from functools import partial

import jax
import jax.numpy as jnp
from jax import lax
from jax.experimental import pallas as pl
from jax.experimental.pallas import tpu as pltpu
from jax.sharding import Mesh, PartitionSpec as P

SCALE_ROUTED = 2.5
CORES = 2
WIDTH = 512
COSTS = 3.0, 3.0, 14.0, 8.0
COLUMNS = 4
LANES = 128
SMALL_VMEM = 12 * 2**20
PROJECT_VMEM = 57 * 2**20


def iota(shape, dim):
    return lax.broadcasted_iota(jnp.int32, shape, dim)


def call(body, out_shape, cost, vmem=SMALL_VMEM, **kwargs):
    return pl.pallas_call(
        body,
        out_shape=out_shape,
        cost_estimate=pl.CostEstimate(flops=cost[0], bytes_accessed=cost[1], transcendentals=0),
        compiler_params=pltpu.CompilerParams(vmem_limit_bytes=vmem),
        **kwargs,
    )


def ranks_before(hits):
    tokens = hits.shape[1]
    first, second = iota((tokens, tokens), 0), iota((tokens, tokens), 1)
    ahead = (first < second) & (first // LANES == second // LANES)
    ahead = jnp.where(ahead, 1.0, 0.0).astype(jnp.bfloat16)
    return jnp.dot(hits.astype(jnp.bfloat16), ahead, preferred_element_type=jnp.float32)


def gate_rows(affinity):
    total = jnp.sum(affinity, axis=0, keepdims=True)
    weights = (SCALE_ROUTED * affinity / total).astype(jnp.bfloat16).astype(jnp.float32)
    return total, weights


def matches(group_ref, z, experts, each):
    top, tokens = group_ref.shape[0] // 2, group_ref.shape[1]
    _, weights = gate_rows(group_ref[top:])
    labels = (z * experts + iota((16, tokens), 0)).astype(jnp.float32)
    hits = jnp.zeros((16, tokens), jnp.float32)
    gains = jnp.zeros((16, tokens), jnp.float32)
    for k in range(top):
        named = group_ref[k : k + 1, :] == labels
        hits += jnp.where(named, 1.0, 0.0)
        gains += jnp.where(named, weights[k : k + 1, :], 0.0)
    slot = ranks_before(hits).astype(jnp.int32) + (iota((16, tokens), 1) // LANES) * (each // CORES)
    slot = jnp.where(hits > 0, slot, -1)
    order = iota((each, tokens), 0)
    lines, columns = [], []
    for at in range(experts):
        s = (at % COLUMNS) * CORES + at // COLUMNS
        found = order == slot[s : s + 1, :]
        lines.append(jnp.where(found, 1.0, 0.0))
        columns.append(jnp.sum(jnp.where(found, gains[s : s + 1, :], 0.0), axis=1, keepdims=True))
    return jnp.concatenate(lines, axis=0).astype(jnp.bfloat16), jnp.concatenate(columns, axis=0)


def select_kernel(parts, capacity, place_ref, token_ref, *refs):
    groups = refs[: max(parts) + 1]
    blocks = refs[len(groups) : len(groups) + len(parts)]
    out_hbm, token_out, gain_ref, out_ref, out_sems = refs[-5:]
    count, rows, width = out_ref.shape
    tile = width // 2
    each = CORES * capacity
    token_out[...] = token_ref[...]
    found = [matches(group_ref, place_ref[0], rows // each, each) for group_ref in groups]
    stores = []
    for j in range(count):
        half = j if count == 1 or j == 2 else jnp.bitwise_xor(j, place_ref[1])
        for h in range(2):
            lanes = slice(h * tile, (h + 1) * tile)
            picked = jnp.dot(found[parts[j]][0], blocks[j][:, lanes], preferred_element_type=jnp.float32)
            out_ref[j, :, lanes] = picked.astype(jnp.bfloat16)
            at = pl.multiple_of(half * width + h * tile, LANES)
            store = pltpu.make_async_copy(
                out_ref.at[j, :, lanes], out_hbm.at[:, pl.ds(at, tile)], out_sems.at[2 * j + h]
            )
            store.start()
            stores.append(store)
    lane = iota((rows, LANES), 1)
    table = jnp.zeros((rows, LANES), jnp.float32)
    for i, (_, column) in enumerate(found):
        table = jnp.where(lane == i, column, table)
    gain_ref[...] = table.astype(jnp.bfloat16)
    store = pltpu.make_async_copy(gain_ref, out_hbm.at[:, count * width :], out_sems.at[2 * count])
    store.start()
    for store in stores + [store]:
        store.wait()


def select_rows(place, token, groups, blocks, parts, rows, capacity, micros):
    tokens, width = blocks[0].shape
    count = len(blocks)
    outside = pl.BlockSpec(memory_space=pltpu.HBM)
    inside = pl.BlockSpec(memory_space=pltpu.VMEM)
    return call(
        partial(select_kernel, parts, capacity),
        (
            jax.ShapeDtypeStruct((rows, width * count + LANES), jnp.bfloat16),
            jax.ShapeDtypeStruct(token.shape, token.dtype),
        ),
        (int(micros * 1.1e9), 2 * (rows + tokens) * width * count),
        grid_spec=pltpu.PrefetchScalarGridSpec(
            num_scalar_prefetch=1,
            in_specs=[inside] * (1 + len(groups) + count),
            out_specs=(outside, inside),
            scratch_shapes=[
                pltpu.VMEM((rows, LANES), jnp.bfloat16),
                pltpu.VMEM((count, rows, width), jnp.bfloat16),
                pltpu.SemaphoreType.DMA((2 * count + 1,)),
            ],
        ),
    )(place, token, *groups, *blocks)


def project_kernel(full, half, capacity, zs_ref, x_ref, w_ref, *refs):
    count = CORES * full + half
    saved, scores_in = refs[:count], refs[count]
    hidden_hbm, scores_ref, y_ref, out_ref, total_ref, out_sems = refs[-6:]
    n, chunks = pl.program_id(0), out_ref.shape[0]
    slots, width = out_ref.shape[2:]
    features = w_ref.shape[1]
    middle = features // 2
    at = features * full
    gain_at = at + middle * half
    dims = (((1,), (1,)), ((), ()))

    def times(x, w):
        return lax.dot_general(x, w, dims, preferred_element_type=jnp.float32)

    def store(step, j):
        lanes = pl.ds(pl.multiple_of(step * width, LANES), width)
        return pltpu.make_async_copy(
            out_ref.at[step, j], hidden_hbm.at[zs_ref[j], :, lanes], out_sems.at[step, j]
        )

    @pl.when(n == 0)
    def _():
        total_ref[...] = jnp.zeros(total_ref.shape, jnp.float32)
        scores_ref[...] = scores_in[...]

    if full:
        y_ref[: 2 * slots] = times(x_ref[:, :features], w_ref[...])
    if half:
        y_ref[2 * slots * full :] = times(x_ref[:slots, at : at + middle], w_ref[:, :middle]) + times(
            x_ref[slots:, at : at + middle], w_ref[:, middle:]
        )
    for j in range(count):
        whole = full and j < CORES
        top = j * slots if whole else 0
        lane = 0 if whole or not full else 1
        tile = x_ref[top : top + slots, gain_at : gain_at + LANES].astype(jnp.float32)
        gain = jnp.broadcast_to(tile[:, lane : lane + 1], (slots, LANES))
        total = total_ref[j]
        for i in range(0, width, LANES):
            lanes = slice(i, i + LANES)
            projected = y_ref[j * slots : (j + 1) * slots, lanes]
            out_ref[n, j, :, lanes] = (gain * projected).astype(jnp.bfloat16)
            total += projected * saved[j][0, :, lanes].astype(jnp.float32)
        total_ref[j] = total
        store(n, j).start()

    @pl.when(n == chunks - 1)
    def _():
        row = iota((slots, LANES), 0)
        own_lane = iota((slots, LANES), 1) == row % capacity
        sources = slots // capacity
        place = iota((sources, LANES), 0)
        for j in range(count):
            column = jnp.sum(total_ref[j], axis=1, keepdims=True)
            spread = jnp.where(own_lane, column, 0.0)
            table = jnp.zeros((sources, LANES), jnp.float32)
            for s in range(sources):
                line = jnp.sum(jnp.where(row // capacity == s, spread, 0.0), axis=0, keepdims=True)
                table = jnp.where(place == s, line, table)
            scores_ref[pl.ds(pl.multiple_of(zs_ref[j] * sources, sources), sources), :] = table
        for step in range(chunks):
            for j in range(count):
                store(step, j).wait()


def project(zs, rows, weight, saved, scores, hidden, full, half, capacity):
    count = CORES * full + half
    blocks, slots, units = saved.shape
    width = WIDTH
    chunks = units // width
    whole = lambda n, zs: (0, 0)
    inside = pl.BlockSpec(memory_space=pltpu.VMEM)
    outside = pl.BlockSpec(memory_space=pltpu.HBM)
    in_specs = [inside, pl.BlockSpec((width, weight.shape[1]), lambda n, zs: (n, 0))]
    in_specs += [pl.BlockSpec((1, slots, width), lambda n, zs, j=j: (zs[j], 0, n)) for j in range(count)]
    in_specs += [pl.BlockSpec(scores.shape, whole)]
    operands = [zs, rows, weight] + [saved] * count + [scores]
    aliases = {}
    if hidden is not None:
        in_specs.append(outside)
        aliases = {len(operands): 0}
        operands.append(hidden)
    return call(
        partial(project_kernel, full, half, capacity),
        (
            jax.ShapeDtypeStruct(saved.shape, jnp.bfloat16),
            jax.ShapeDtypeStruct(scores.shape, jnp.float32),
        ),
        (2 * rows.size * units, 2 * (rows.size + weight.size + 2 * count * slots * units)),
        vmem=PROJECT_VMEM,
        grid_spec=pltpu.PrefetchScalarGridSpec(
            num_scalar_prefetch=1,
            grid=(chunks,),
            in_specs=in_specs,
            out_specs=(outside, pl.BlockSpec(scores.shape, whole)),
            scratch_shapes=[
                pltpu.VMEM((count * slots, width), jnp.float32),
                pltpu.VMEM((chunks, count, slots, width), jnp.bfloat16),
                pltpu.VMEM((count, slots, LANES), jnp.float32),
                pltpu.SemaphoreType.DMA((chunks, count)),
            ],
        ),
        input_output_aliases=aliases,
    )(*operands)


def gate_kernel(capacity, scores_ref, routes_ref, affinity_ref, out_ref):
    top = routes_ref.shape[0]
    total, weights = gate_rows(affinity_ref[...])
    labels = iota(scores_ref.shape, 0)
    hits = jnp.zeros(labels.shape, jnp.float32)
    for k in range(top):
        hits += jnp.where(routes_ref[k : k + 1, :] == labels, 1.0, 0.0)
    slot = jnp.where(hits > 0, ranks_before(hits), -1.0).astype(jnp.int32)
    found = jnp.zeros(labels.shape, jnp.float32)
    for r in range(capacity):
        found = jnp.where(slot == r, scores_ref[:, r : r + 1], found)
    place = iota((top, LANES), 0)
    grad = jnp.zeros((top, LANES), jnp.float32)
    for k in range(top):
        line = jnp.sum(jnp.where(routes_ref[k : k + 1, :] == labels, found, 0.0), axis=0, keepdims=True)
        grad = jnp.where(place == k, line, grad)
    weighted = jnp.sum(weights * grad, axis=0, keepdims=True)
    out_ref[...] = (SCALE_ROUTED / total) * grad - weighted / total


def on_device(upstream, routes, affinity, w_down, saved_hidden):
    sections, depth = lax.axis_size("pipe"), lax.axis_size("z")
    section, z, core = lax.axis_index("pipe"), lax.axis_index("z"), lax.axis_index("core")
    everyone = ("z", "x", "core")
    expert_count = depth * COLUMNS * CORES
    local = COLUMNS * CORES
    slot_total, units = saved_hidden.shape[2:]
    capacity = slot_total // expert_count
    tokens, features = upstream.shape[1:]
    half = features // 2
    cores = range(CORES)

    mine = lax.dynamic_slice(upstream[0], (0, core * half), (tokens, half))
    other = lax.dynamic_slice(upstream[0], (0, (1 - core) * half), (tokens, half))
    hop = range(1, sections)
    last = sections - 1
    near = lax.ppermute(mine, ("pipe", "core"), [(i * CORES + c, (i - 1) * CORES + c) for i in hop for c in cores])
    far = lax.ppermute(other, ("pipe", "core"), [(i * CORES + c, (i - 1) * CORES + 1 - c) for i in hop for c in cores])
    stay = lax.ppermute(other, ("pipe", "core"), [(last * CORES + c, last * CORES + 1 - c) for c in cores])

    routes_own = routes[0].T
    affinity_own = affinity[0].T
    choices = jnp.concatenate([routes_own.astype(jnp.float32), affinity_own], 0)
    choices_mate = lax.ppermute(choices, "core", [(c, 1 - c) for c in cores])

    def in_order(a, b, axis):
        return jnp.where(core == 0, jnp.concatenate([a, b], axis), jnp.concatenate([b, a], axis))

    def along(block, distance, cross=False):
        pairs = []
        for i in range(depth):
            pairs.append((i * CORES + (1 if cross else 0), (i + distance) % depth * CORES))
            pairs.append((i * CORES + (0 if cross else 1), (i - distance) % depth * CORES + 1))
        return lax.ppermute(block, ("z", "core"), pairs)

    reach = depth // 2
    place = jnp.stack([z, core])
    rows = local * CORES * capacity
    choices = [in_order(choices, choices_mate, 1)]
    choices += [along(choices[0], k) for k in range(1, reach + 1)]
    token = jnp.zeros((8, LANES), jnp.float32)

    def exchange(block, axes, parts):
        shape = block.shape
        block = block.reshape(parts, shape[0] // parts, shape[1])
        return lax.all_to_all(block, axes, split_axis=0, concat_axis=0, tiled=True).reshape(shape)

    near, far, stay, choices = lax.optimization_barrier((near, far, stay, choices))
    is_last = section == last
    held = in_order(jnp.where(is_last, mine, near), jnp.where(is_last, stay, far), 0)
    weight = w_down[0, 0]
    saved = saved_hidden[0, 0].reshape(depth, slot_total // depth, units)
    scores = jnp.zeros((expert_count, LANES), jnp.float32)

    def at(*distances):
        return jnp.stack([(z + d) % depth for d in distances])

    def columns(groups, blocks, parts, micros):
        picked, after = select_rows(place, token, groups, blocks, parts, rows, capacity, micros)
        return exchange(picked, ("core", "x"), local), after

    groups = []
    same, cross = along(held, 1), along(held, 1, cross=True)
    got, token = columns(choices[:1], [held], (0,), COSTS[0])
    groups.append((got, at(0), 0, 1))
    for k in range(1, reach - 1):
        same, cross, token = lax.optimization_barrier((same, cross, token))
        ahead = along(same, 1), along(cross, 1)
        got, token = columns([choices[k]], [same, cross], (0, 0), COSTS[k])
        groups.append((got, at(-k, k), 1, 0))
        same, cross = ahead
    k = reach - 1
    same, cross, token = lax.optimization_barrier((same, cross, token))
    got, token = columns(choices[k:], [same, cross, along(same, 1)], (0, 0, 1), COSTS[k])
    groups.append((got, at(-k, k, reach), 1, 1))

    hidden = None
    for got, zs, full, part in groups:
        hidden, scores = project(zs, got, weight, saved, scores, hidden, full, part, capacity)

    returned = exchange(scores, everyone, expert_count)
    affinity_grad = call(
        partial(gate_kernel, capacity),
        jax.ShapeDtypeStruct(affinity_own.shape, jnp.float32),
        (10**6, 10**5),
    )(returned, routes_own, affinity_own)
    return hidden.reshape(1, 1, slot_total, units), affinity_grad.T[None]


def solution(mesh):
    sections, experts = mesh.devices.shape
    grid = mesh.devices.reshape(sections, experts // (COLUMNS * CORES), COLUMNS, CORES)
    rows = ("z", "x", "core")
    return jax.shard_map(
        on_device,
        mesh=Mesh(grid, ("pipe",) + rows),
        in_specs=(
            P("pipe", rows, None),
            P("pipe", rows, None),
            P("pipe", rows, None),
            P("pipe", rows, None, None),
            P("pipe", rows, None, None),
        ),
        out_specs=(P("pipe", rows, None, None), P("pipe", rows, None)),
        check_vma=False,
    )
```

time: 221 us -> 206 us (0.932)
  local copies, waits for them, and re-layouts: 26 us -> 3.6 us
  Pallas kernels: 37.6 us -> 46.7 us
  other arithmetic: 2.78 us -> 5.39 us
  blocking collectives: 18.5 us -> 16.1 us
    unnamed x44 -> x6, local copies, waits for them, and re-layouts: 24.8 us -> 1.76 us
    ppermute x11, waiting for transfers between devices: 29.1 us -> 41.3 us  [along(): return lax.ppermute(block, ('z', 'core'), pairs)]
    ppermute x1, waiting for transfers between devices: 15.2 us -> 3.19 us  [on_device(): lax.ppermute(mine, ('pipe', 'core'), [(i * CORES + c, (i - 1) * CORES + c...]
    pallas_call x4, Pallas kernels: 21.4 us -> 32.8 us  [project(): call(partial(project_kernel, full, half, capacity), (jax.ShapeDtypeStruct...]
    ppermute x11, starting transfers between devices: 24 us -> 26.4 us  [along(): return lax.ppermute(block, ('z', 'core'), pairs)]
    pallas_call x6 -> x4, Pallas kernels: 15.4 us -> 12.9 us  [select_rows(): call(partial(select_kernel, parts, capacity), (jax.ShapeDtypeStruct((rows...]
    all_to_all x1, blocking collectives: 18.5 us -> 16.1 us  [exchange(): lax.all_to_all(block, axes, split_axis=0, concat_axis=0, tiled=True)]
  transfers between devices with their start and end apart: 19 -> 19, of which waited for: 9 -> 14; matrix products, arithmetic and copies ran while one was open for 1% -> 2% of each run, Pallas kernels for 13% -> 17%
where the time goes in v4:
time: 206 us; the launch traced here: 205 us
  waiting for transfers between devices  82.4 us (40%)
  starting transfers between devices  50.2 us (24%)
  Pallas kernels  46.7 us (23%)
  blocking collectives  16.1 us (8%)
  other arithmetic  5.39 us (3%)
  local copies, waits for them, and re-layouts  3.6 us (2%)
    ppermute x11, waiting for transfers between devices, along(): return lax.ppermute(block, ('z', 'core'), pairs)  41.3 us
    all_to_all x4, waiting for transfers between devices, exchange(): lax.all_to_all(block, axes, split_axis=0, concat_axis=0, tiled=True)  37.1 us
    pallas_call x4, Pallas kernels, project(): call(partial(project_kernel, full, half, capacity), (jax.ShapeDtypeStruct...  32.8 us
    ppermute x11, starting transfers between devices, along(): return lax.ppermute(block, ('z', 'core'), pairs)  26.4 us
    all_to_all x4, starting transfers between devices, exchange(): lax.all_to_all(block, axes, split_axis=0, concat_axis=0, tiled=True)  17.3 us
    all_to_all x1, blocking collectives, exchange(): lax.all_to_all(block, axes, split_axis=0, concat_axis=0, tiled=True)  16.1 us
    pallas_call x4, Pallas kernels, select_rows(): call(partial(select_kernel, parts, capacity), (jax.ShapeDtypeStruct((rows...  12.9 us
  transfers between devices with their start and end apart: 19, of which 14 were waited for; matrix products, arithmetic and copies ran while one was open for 2% of the time, Pallas kernels for 17%

profile of v4, /device:TPU:1, one launch (start us, length us, event | category | flops | bytes accessed | tf_op | source)
XLA Modules:
  0.0 205.2 jit_solution(2780231697465157261)
XLA Ops:
  6.5 3.2 %collective-permute-start.3 = (f32[16,128]{1,0:T(8,128)S(1)}, f32[16,128]{1,0:T(8,128)S(1)}, u32[]{:S(2)}, u32[]{:S(2)}) collective-permute-start(f32[16,128]{1,0:T(8,128)S(1)} %pad_maximum_fusion), channel_id=1, source_target_pairs={{0,1},{1,0},{2,3},{3,2},{4,5},{5,4},{6,7},{7,6},{8,9},{9,8},{10,11... | collective-permute-start | bytes 24584 | tf_op jit(solution)/shard_map/ppermute | solution.py:278
  11.4 5.2 %collective-permute-start.7 = (f32[16,256]{1,0:T(8,128)S(1)}, f32[16,256]{1,0:T(8,128)S(1)}, u32[]{:S(2)}, u32[]{:S(2)}) collective-permute-start(f32[16,256]{1,0:T(8,128)S(1)} %maximum_select_fusion.1.refs_0_), channel_id=1, source_target_pairs={{0,32},{1,33},{8,40},{9,41},{16,48},{17,49},{24,56},{25,57},{32,0}... | collective-permute-start | bytes 49160 | tf_op jit(solution)/shard_map/ppermute | solution.py:288
  18.0 4.2 %collective-permute-start.5 = (f32[16,256]{1,0:T(8,128)S(1)}, f32[16,256]{1,0:T(8,128)S(1)}, u32[]{:S(2)}, u32[]{:S(2)}) collective-permute-start(f32[16,256]{1,0:T(8,128)S(1)} %maximum_select_fusion.1.refs_0_), channel_id=1, source_target_pairs={{0,16},{1,49},{8,24},{9,57},{16,32},{17,1},{24,40},{25,9},{32,48},... | collective-permute-start | bytes 49160 | tf_op jit(solution)/shard_map/ppermute | solution.py:288
  23.0 2.1 %collective-permute-done.4.refs_0_ = f32[16,256]{1,0:T(8,128)S(1)} collective-permute-done((f32[16,256]{1,0:T(8,128)S(1)}, f32[16,256]{1,0:T(8,128)S(1)}, u32[]{:S(2)}, u32[]{:S(2)}) %collective-permute-start.4) | collective-permute-done | bytes 16416 | tf_op jit(solution)/shard_map/ppermute | solution.py:288
  25.2 3.2 %collective-permute-done = bf16[128,1792]{1,0:T(8,128)(2,1)} collective-permute-done((bf16[128,1792]{1,0:T(8,128)(2,1)S(1)}, bf16[128,1792]{1,0:T(8,128)(2,1)}, u32[]{:S(2)}, u32[]{:S(2)}) %collective-permute-start) | collective-permute-done | bytes 458784 | tf_op jit(solution)/shard_map/ppermute | solution.py:271
  29.7 2.0 collective-permute-start.9
  31.7 3.6 %collective-permute-start.8 = (bf16[256,1792]{1,0:T(8,128)(2,1)S(1)}, bf16[256,1792]{1,0:T(8,128)(2,1)}, u32[]{:S(2)}, u32[]{:S(2)}) collective-permute-start(bf16[256,1792]{1,0:T(8,128)(2,1)S(1)} %maximum_select_fusion.refs_1_), channel_id=1, source_target_pairs={{0,8},{1,57},{8,16},{9,1},{16,24},{17,9},{24,32},{25,17},{32,40},{... | collective-permute-start | bytes 2752520 | tf_op jit(solution)/shard_map/ppermute | solution.py:288
  35.3 2.1 %shard_map.68 = (bf16[320,1920]{1,0:T(8,128)(2,1)}, f32[8,128]{1,0:T(8,128)S(1)}) custom-call(s32[2]{0:T(128)S(1)} %pad_add_fusion.1.place_ref, f32[8,128]{1,0:T(8,128)S(1)} %broadcast_in_dim.9.token_ref, f32[16,256]{1,0:T(8,128)S(1)} %maximum_select_fusion.1.refs_0_, bf16[256,1792]{1,0:T(8,128)(2,1)S(1)} %maximum_select_fusion.refs_1_), custom_call_target="tpu_custom_call" | custom-call | flops 3300000000 | bytes 2064384 | tf_op jit(solution)/shard_map/pallas_call | solution.py:108
  37.4 4.6 %all-to-all-start.3 = ((bf16[8,40,1920]{2,1,0:T(8,128)(2,1)}), bf16[8,40,1920]{2,1,0:T(8,128)(2,1)}, u32[]{:S(2)}, u32[]{:S(2)}) async-start(bf16[8,40,1920]{2,1,0:T(8,128)(2,1)} %bitcast.24), calls=%async_computation.3 | async-start | bytes 2457600 | tf_op jit(solution)/shard_map/all_to_all | solution.py:300
  42.0 9.6 %collective-permute-done.9.refs_2_ = bf16[256,1792]{1,0:T(8,128)(2,1)S(1)} collective-permute-done((bf16[256,1792]{1,0:T(8,128)(2,1)S(1)}, bf16[256,1792]{1,0:T(8,128)(2,1)S(1)}, u32[]{:S(2)}, u32[]{:S(2)}) %collective-permute-start.9) | collective-permute-done | bytes 917536 | tf_op jit(solution)/shard_map/ppermute | solution.py:288
  51.6 3.4 %collective-permute-done.8.refs_1_ = bf16[256,1792]{1,0:T(8,128)(2,1)} collective-permute-done((bf16[256,1792]{1,0:T(8,128)(2,1)S(1)}, bf16[256,1792]{1,0:T(8,128)(2,1)}, u32[]{:S(2)}, u32[]{:S(2)}) %collective-permute-start.8) | collective-permute-done | bytes 917536 | tf_op jit(solution)/shard_map/ppermute | solution.py:288
  55.0 3.9 %collective-permute-start.10 = (bf16[256,1792]{1,0:T(8,128)(2,1)}, bf16[256,1792]{1,0:T(8,128)(2,1)S(1)}, u32[]{:S(2)}, u32[]{:S(2)}) collective-permute-start(bf16[256,1792]{1,0:T(8,128)(2,1)} %collective-permute-done.8.refs_1_), channel_id=1, source_target_pairs={{0,8},{1,57},{8,16},{9,1},{16,24},{17,9},{24,32},{25,17},{32,40},{... | collective-permute-start | bytes 2752520 | tf_op jit(solution)/shard_map/ppermute | solution.py:288
  59.0 3.6 %shard_map.69 = (bf16[320,3712]{1,0:T(8,128)(2,1)}, f32[8,128]{1,0:T(8,128)S(1)}) custom-call(s32[2]{0:T(128)S(1)} %pad_add_fusion.1.place_ref, f32[8,128]{1,0:T(8,128)S(1)} %get-tuple-element.41.token_ref, f32[16,256]{1,0:T(8,128)S(1)} %collective-permute-done.4.refs_0_, bf16[256,1792]{1,0:T(8,128)(2,1)} %collective-permute-done.8.refs_1_, ...), custom_call_target="tpu_custom_call" | custom-call | flops 3300000000 | bytes 4128768 | tf_op jit(solution)/shard_map/pallas_call | solution.py:108
  62.6 4.4 %all-to-all-start.2 = ((bf16[8,40,3712]{2,1,0:T(8,128)(2,1)}), bf16[8,40,3712]{2,1,0:T(8,128)(2,1)}, u32[]{:S(2)}, u32[]{:S(2)}) async-start(bf16[8,40,3712]{2,1,0:T(8,128)(2,1)} %bitcast.21), calls=%async_computation.2 | async-start | bytes 4751360 | tf_op jit(solution)/shard_map/all_to_all | solution.py:300
  67.0 2.6 %collective-permute-done.10.refs_1_ = bf16[256,1792]{1,0:T(8,128)(2,1)S(1)} collective-permute-done((bf16[256,1792]{1,0:T(8,128)(2,1)}, bf16[256,1792]{1,0:T(8,128)(2,1)S(1)}, u32[]{:S(2)}, u32[]{:S(2)}) %collective-permute-start.10) | collective-permute-done | bytes 917536 | tf_op jit(solution)/shard_map/ppermute | solution.py:288
  69.6 9.7 %collective-permute-done.11.refs_2_ = bf16[256,1792]{1,0:T(8,128)(2,1)S(1)} collective-permute-done((bf16[256,1792]{1,0:T(8,128)(2,1)S(1)}, bf16[256,1792]{1,0:T(8,128)(2,1)S(1)}, u32[]{:S(2)}, u32[]{:S(2)}) %collective-permute-start.11) | collective-permute-done | bytes 917536 | tf_op jit(solution)/shard_map/ppermute | solution.py:288
  79.3 3.5 %collective-permute-start.12 = (bf16[256,1792]{1,0:T(8,128)(2,1)S(1)}, bf16[256,1792]{1,0:T(8,128)(2,1)S(1)}, u32[]{:S(2)}, u32[]{:S(2)}) collective-permute-start(bf16[256,1792]{1,0:T(8,128)(2,1)S(1)} %collective-permute-done.10.refs_1_), channel_id=1, source_target_pairs={{0,8},{1,57},{8,16},{9,1},{16,24},{17,9},{24,32},{25,17},{32,40},{... | collective-permute-start | bytes 2752520 | tf_op jit(solution)/shard_map/ppermute | solution.py:288
  82.9 2.5 %shard_map.70 = (bf16[320,3712]{1,0:T(8,128)(2,1)}, f32[8,128]{1,0:T(8,128)S(1)}) custom-call(s32[2]{0:T(128)S(1)} %pad_add_fusion.1.place_ref, f32[8,128]{1,0:T(8,128)S(1)} %get-tuple-element.46.token_ref, f32[16,256]{1,0:T(8,128)S(1)} %collective-permute-done.5.refs_0_, bf16[256,1792]{1,0:T(8,128)(2,1)S(1)} %collective-permute-done.10.refs_1_, ...), custom_call_target="tpu_custom_call" | custom-call | flops 15399999488 | bytes 4128768 | tf_op jit(solution)/shard_map/pallas_call | solution.py:108
  85.5 11.2 %all-to-all-done.2 = bf16[8,40,3712]{2,1,0:T(8,128)(2,1)} async-done(((bf16[8,40,3712]{2,1,0:T(8,128)(2,1)}), bf16[8,40,3712]{2,1,0:T(8,128)(2,1)}, u32[]{:S(2)}, u32[]{:S(2)}) %all-to-all-start.2) | async-done | bytes 2375712 | tf_op jit(solution)/shard_map/all_to_all | solution.py:300
  96.6 4.3 %all-to-all-start.1 = ((bf16[8,40,3712]{2,1,0:T(8,128)(2,1)}), bf16[8,40,3712]{2,1,0:T(8,128)(2,1)}, u32[]{:S(2)}, u32[]{:S(2)}) async-start(bf16[8,40,3712]{2,1,0:T(8,128)(2,1)} %bitcast.17), calls=%async_computation.1 | async-start | bytes 4751360 | tf_op jit(solution)/shard_map/all_to_all | solution.py:300
  101.0 2.1 %collective-permute-done.13.refs_3_ = bf16[256,1792]{1,0:T(8,128)(2,1)} collective-permute-done((bf16[256,1792]{1,0:T(8,128)(2,1)S(1)}, bf16[256,1792]{1,0:T(8,128)(2,1)}, u32[]{:S(2)}, u32[]{:S(2)}) %collective-permute-start.13) | collective-permute-done | bytes 917536 | tf_op jit(solution)/shard_map/ppermute | solution.py:288
  103.0 3.2 %collective-permute-start.14 = (bf16[256,1792]{1,0:T(8,128)(2,1)S(1)}, bf16[256,1792]{1,0:T(8,128)(2,1)S(1)}, u32[]{:S(2)}, u32[]{:S(2)}) collective-permute-start(bf16[256,1792]{1,0:T(8,128)(2,1)S(1)} %collective-permute-done.12.refs_2_), channel_id=1, source_target_pairs={{0,8},{1,57},{8,16},{9,1},{16,24},{17,9},{24,32},{25,17},{32,40},{... | collective-permute-start | bytes 2752520 | tf_op jit(solution)/shard_map/ppermute | solution.py:288
  106.3 10.3 %collective-permute-done.14.refs_4_ = bf16[256,1792]{1,0:T(8,128)(2,1)S(1)} collective-permute-done((bf16[256,1792]{1,0:T(8,128)(2,1)S(1)}, bf16[256,1792]{1,0:T(8,128)(2,1)S(1)}, u32[]{:S(2)}, u32[]{:S(2)}) %collective-permute-start.14) | collective-permute-done | bytes 917536 | tf_op jit(solution)/shard_map/ppermute | solution.py:288
  116.6 4.7 %shard_map.71 = (bf16[320,5504]{1,0:T(8,128)(2,1)}, f32[8,128]{1,0:T(8,128)}) custom-call(s32[2]{0:T(128)S(1)} %pad_add_fusion.1.place_ref, f32[8,128]{1,0:T(8,128)S(1)} %get-tuple-element.49.token_ref, f32[16,256]{1,0:T(8,128)S(1)} %collective-permute-done.6.refs_0_, f32[16,256]{1,0:T(8,128)S(1)} %collective-permute-done.7.refs_1_, ...), custom_call_target="tpu_custom_call" | custom-call | flops 8800000000 | bytes 6193152 | tf_op jit(solution)/shard_map/pallas_call | solution.py:108
  121.3 9.0 %all-to-all-done.1 = bf16[8,40,3712]{2,1,0:T(8,128)(2,1)} async-done(((bf16[8,40,3712]{2,1,0:T(8,128)(2,1)}), bf16[8,40,3712]{2,1,0:T(8,128)(2,1)}, u32[]{:S(2)}, u32[]{:S(2)}) %all-to-all-start.1) | async-done | bytes 2375712 | tf_op jit(solution)/shard_map/all_to_all | solution.py:300
  130.3 4.0 %all-to-all-start = ((bf16[8,40,5504]{2,1,0:T(8,128)(2,1)}), bf16[8,40,5504]{2,1,0:T(8,128)(2,1)S(1)}, u32[]{:S(2)}, u32[]{:S(2)}) async-start(bf16[8,40,5504]{2,1,0:T(8,128)(2,1)} %bitcast.11), calls=%async_computation | async-start | bytes 7045120 | tf_op jit(solution)/shard_map/all_to_all | solution.py:300
  136.7 6.5 %shard_map.72 = (bf16[8,160,1024]{2,1,0:T(8,128)(2,1)}, f32[64,128]{1,0:T(8,128)}) custom-call(s32[1]{0:T(128)} %bitcast.23.zs_ref, bf16[320,1920]{1,0:T(8,128)(2,1)} %bitcast.25.x_ref, bf16[1024,3584]{1,0:T(8,128)(2,1)} %bitcast.52, bf16[8,160,1024]{2,1,0:T(8,128)(2,1)} %bitcast.44, f32[64,128]{1,0:T(8,128)} %broadcast_in_dim.10.refs_1_), custom_call_target="tpu_custom_call" | custom-call | flops 1258291200 | bytes 9224192 | tf_op jit(solution)/shard_map/pallas_call | solution.py:211
  143.2 7.8 %shard_map.73 = (bf16[8,160,1024]{2,1,0:T(8,128)(2,1)}, f32[64,128]{1,0:T(8,128)}) custom-call(s32[2]{0:T(128)} %pad_add_fusion.3.zs_ref, bf16[320,3712]{1,0:T(8,128)(2,1)} %bitcast.22.x_ref, bf16[1024,3584]{1,0:T(8,128)(2,1)} %bitcast.53, bf16[8,160,1024]{2,1,0:T(8,128)(2,1)} %bitcast.45, ...), custom_call_target="tpu_custom_call", output_to_operand_aliasing={{0}: (6, {})} | custom-call | flops 2432696320 | bytes 11026432 | tf_op jit(solution)/shard_map/pallas_call | solution.py:211
  151.0 7.8 %shard_map.74 = (bf16[8,160,1024]{2,1,0:T(8,128)(2,1)}, f32[64,128]{1,0:T(8,128)}) custom-call(s32[2]{0:T(128)} %pad_add_fusion.2.zs_ref, bf16[320,3712]{1,0:T(8,128)(2,1)} %bitcast.18.x_ref, bf16[1024,3584]{1,0:T(8,128)(2,1)} %bitcast.54, bf16[8,160,1024]{2,1,0:T(8,128)(2,1)} %bitcast.47, ...), custom_call_target="tpu_custom_call", output_to_operand_aliasing={{0}: (6, {})} | custom-call | flops 2432696320 | bytes 11026432 | tf_op jit(solution)/shard_map/pallas_call | solution.py:211
  158.8 16.9 %all-to-all-done = bf16[8,40,5504]{2,1,0:T(8,128)(2,1)S(1)} async-done(((bf16[8,40,5504]{2,1,0:T(8,128)(2,1)}), bf16[8,40,5504]{2,1,0:T(8,128)(2,1)S(1)}, u32[]{:S(2)}, u32[]{:S(2)}) %all-to-all-start) | async-done | bytes 3522592 | tf_op jit(solution)/shard_map/all_to_all | solution.py:300
  177.5 10.7 %shard_map.75 = (bf16[8,160,1024]{2,1,0:T(8,128)(2,1)}, f32[64,128]{1,0:T(8,128)}) custom-call(s32[3]{0:T(128)} %pad_add_fusion.zs_ref, bf16[320,5504]{1,0:T(8,128)(2,1)} %bitcast.57, bf16[1024,3584]{1,0:T(8,128)(2,1)} %bitcast.55, bf16[8,160,1024]{2,1,0:T(8,128)(2,1)} %bitcast.49, bf16[8,160,1024]{2,1,0:T(8,128)(2,1)} %bitcast.50, ...), custom_call_target="tpu_custom_call", output_to_operand_aliasing={{0}: (7, {})} | custom-call | flops 3607101440 | bytes 12828672 | tf_op jit(solution)/shard_map/pallas_call | solution.py:211
  188.2 16.1 %all_to_all.25 = f32[64,1,128]{2,1,0:T(1,128)S(1)} all-to-all(f32[64,1,128]{2,1,0:T(1,128)} %bitcast.58), channel_id=1, replica_groups=mesh['pipe'=4,'z'=8,'x'=4,'core'=2] {'z','x','core'}, dimensions={0} | all-to-all | bytes 65536 | tf_op jit(solution)/shard_map/all_to_all | solution.py:300
  (34 shorter events, 16.3 us)
Async XLA Ops:
  1.9 23.3 %collective-permute-start.2 = (bf16[128,1792]{1,0:T(8,128)(2,1)S(1)}, bf16[128,1792]{1,0:T(8,128)(2,1)S(1)}, u32[]{:S(2)}, u32[]{:S(2)}) collective-permute-start(bf16[128,1792]{1,0:T(8,128)(2,1)S(1)} %get-tuple-element.66), channel_id=1, source_target_pairs={{192,193},{193,192},{194,195},{195,194},{196,197},{197,196},{198,1... | collective-permute-start | bytes 1376264 | tf_op jit(solution)/shard_map/ppermute | solution.py:273
  2.6 22.6 %collective-permute-start.1 = (bf16[128,1792]{1,0:T(8,128)(2,1)S(1)}, bf16[128,1792]{1,0:T(8,128)(2,1)S(1)}, u32[]{:S(2)}, u32[]{:S(2)}) collective-permute-start(bf16[128,1792]{1,0:T(8,128)(2,1)S(1)} %get-tuple-element.66), channel_id=1, source_target_pairs={{64,1},{65,0},{128,65},{129,64},{192,129},{193,128},{66,3},{67,2},... | collective-permute-start | bytes 1376264 | tf_op jit(solution)/shard_map/ppermute | solution.py:272
  3.9 24.5 %collective-permute-start = (bf16[128,1792]{1,0:T(8,128)(2,1)S(1)}, bf16[128,1792]{1,0:T(8,128)(2,1)}, u32[]{:S(2)}, u32[]{:S(2)}) collective-permute-start(bf16[128,1792]{1,0:T(8,128)(2,1)S(1)} %get-tuple-element.67), channel_id=1, source_target_pairs={{64,0},{65,1},{128,64},{129,65},{192,128},{193,129},{66,2},{67,3},... | collective-permute-start | bytes 1376264 | tf_op jit(solution)/shard_map/ppermute | solution.py:271
  6.5 4.1 %collective-permute-start.3 = (f32[16,128]{1,0:T(8,128)S(1)}, f32[16,128]{1,0:T(8,128)S(1)}, u32[]{:S(2)}, u32[]{:S(2)}) collective-permute-start(f32[16,128]{1,0:T(8,128)S(1)} %pad_maximum_fusion), channel_id=1, source_target_pairs={{0,1},{1,0},{2,3},{3,2},{4,5},{5,4},{6,7},{7,6},{8,9},{9,8},{10,11... | collective-permute-start | bytes 24584 | tf_op jit(solution)/shard_map/ppermute | solution.py:278
  11.4 6.6 %collective-permute-start.7 = (f32[16,256]{1,0:T(8,128)S(1)}, f32[16,256]{1,0:T(8,128)S(1)}, u32[]{:S(2)}, u32[]{:S(2)}) collective-permute-start(f32[16,256]{1,0:T(8,128)S(1)} %maximum_select_fusion.1.refs_0_), channel_id=1, source_target_pairs={{0,32},{1,33},{8,40},{9,41},{16,48},{17,49},{24,56},{25,57},{32,0}... | collective-permute-start | bytes 49160 | tf_op jit(solution)/shard_map/ppermute | solution.py:288
  16.5 5.6 %collective-permute-start.6 = (f32[16,256]{1,0:T(8,128)S(1)}, f32[16,256]{1,0:T(8,128)S(1)}, u32[]{:S(2)}, u32[]{:S(2)}) collective-permute-start(f32[16,256]{1,0:T(8,128)S(1)} %maximum_select_fusion.1.refs_0_), channel_id=1, source_target_pairs={{0,24},{1,41},{8,32},{9,49},{16,40},{17,57},{24,48},{25,1},{32,56}... | collective-permute-start | bytes 49160 | tf_op jit(solution)/shard_map/ppermute | solution.py:288
  18.0 5.1 %collective-permute-start.5 = (f32[16,256]{1,0:T(8,128)S(1)}, f32[16,256]{1,0:T(8,128)S(1)}, u32[]{:S(2)}, u32[]{:S(2)}) collective-permute-start(f32[16,256]{1,0:T(8,128)S(1)} %maximum_select_fusion.1.refs_0_), channel_id=1, source_target_pairs={{0,16},{1,49},{8,24},{9,57},{16,32},{17,1},{24,40},{25,9},{32,48},... | collective-permute-start | bytes 49160 | tf_op jit(solution)/shard_map/ppermute | solution.py:288
  22.2 3.0 %collective-permute-start.4 = (f32[16,256]{1,0:T(8,128)S(1)}, f32[16,256]{1,0:T(8,128)S(1)}, u32[]{:S(2)}, u32[]{:S(2)}) collective-permute-start(f32[16,256]{1,0:T(8,128)S(1)} %maximum_select_fusion.1.refs_0_), channel_id=1, source_target_pairs={{0,8},{1,57},{8,16},{9,1},{16,24},{17,9},{24,32},{25,17},{32,40},{... | collective-permute-start | bytes 49160 | tf_op jit(solution)/shard_map/ppermute | solution.py:288
  29.7 21.9 %collective-permute-start.9 = (bf16[256,1792]{1,0:T(8,128)(2,1)S(1)}, bf16[256,1792]{1,0:T(8,128)(2,1)S(1)}, u32[]{:S(2)}, u32[]{:S(2)}) collective-permute-start(bf16[256,1792]{1,0:T(8,128)(2,1)S(1)} %maximum_select_fusion.refs_1_), channel_id=1, source_target_pairs={{1,8},{0,57},{9,16},{8,1},{17,24},{16,9},{25,32},{24,17},{33,40},{... | collective-permute-start | bytes 2752520 | tf_op jit(solution)/shard_map/ppermute | solution.py:288
  31.7 23.4 %collective-permute-start.8 = (bf16[256,1792]{1,0:T(8,128)(2,1)S(1)}, bf16[256,1792]{1,0:T(8,128)(2,1)}, u32[]{:S(2)}, u32[]{:S(2)}) collective-permute-start(bf16[256,1792]{1,0:T(8,128)(2,1)S(1)} %maximum_select_fusion.refs_1_), channel_id=1, source_target_pairs={{0,8},{1,57},{8,16},{9,1},{16,24},{17,9},{24,32},{25,17},{32,40},{... | collective-permute-start | bytes 2752520 | tf_op jit(solution)/shard_map/ppermute | solution.py:288
  37.4 25.2 %all-to-all-start.3 = ((bf16[8,40,1920]{2,1,0:T(8,128)(2,1)}), bf16[8,40,1920]{2,1,0:T(8,128)(2,1)}, u32[]{:S(2)}, u32[]{:S(2)}) async-start(bf16[8,40,1920]{2,1,0:T(8,128)(2,1)} %bitcast.24), calls=%async_computation.3 | async-start | bytes 2457600 | tf_op jit(solution)/shard_map/all_to_all | solution.py:300
  55.0 14.6 %collective-permute-start.10 = (bf16[256,1792]{1,0:T(8,128)(2,1)}, bf16[256,1792]{1,0:T(8,128)(2,1)S(1)}, u32[]{:S(2)}, u32[]{:S(2)}) collective-permute-start(bf16[256,1792]{1,0:T(8,128)(2,1)} %collective-permute-done.8.refs_1_), channel_id=1, source_target_pairs={{0,8},{1,57},{8,16},{9,1},{16,24},{17,9},{24,32},{25,17},{32,40},{... | collective-permute-start | bytes 2752520 | tf_op jit(solution)/shard_map/ppermute | solution.py:288
  59.0 20.4 %collective-permute-start.11 = (bf16[256,1792]{1,0:T(8,128)(2,1)S(1)}, bf16[256,1792]{1,0:T(8,128)(2,1)S(1)}, u32[]{:S(2)}, u32[]{:S(2)}) collective-permute-start(bf16[256,1792]{1,0:T(8,128)(2,1)S(1)} %collective-permute-done.9.refs_2_), channel_id=1, source_target_pairs={{0,8},{1,57},{8,16},{9,1},{16,24},{17,9},{24,32},{25,17},{32,40},{... | collective-permute-start | bytes 2752520 | tf_op jit(solution)/shard_map/ppermute | solution.py:288
  62.6 34.0 %all-to-all-start.2 = ((bf16[8,40,3712]{2,1,0:T(8,128)(2,1)}), bf16[8,40,3712]{2,1,0:T(8,128)(2,1)}, u32[]{:S(2)}, u32[]{:S(2)}) async-start(bf16[8,40,3712]{2,1,0:T(8,128)(2,1)} %bitcast.21), calls=%async_computation.2 | async-start | bytes 4751360 | tf_op jit(solution)/shard_map/all_to_all | solution.py:300
  79.3 21.6 %collective-permute-start.12 = (bf16[256,1792]{1,0:T(8,128)(2,1)S(1)}, bf16[256,1792]{1,0:T(8,128)(2,1)S(1)}, u32[]{:S(2)}, u32[]{:S(2)}) collective-permute-start(bf16[256,1792]{1,0:T(8,128)(2,1)S(1)} %collective-permute-done.10.refs_1_), channel_id=1, source_target_pairs={{0,8},{1,57},{8,16},{9,1},{16,24},{17,9},{24,32},{25,17},{32,40},{... | collective-permute-start | bytes 2752520 | tf_op jit(solution)/shard_map/ppermute | solution.py:288
  82.9 20.2 %collective-permute-start.13 = (bf16[256,1792]{1,0:T(8,128)(2,1)S(1)}, bf16[256,1792]{1,0:T(8,128)(2,1)}, u32[]{:S(2)}, u32[]{:S(2)}) collective-permute-start(bf16[256,1792]{1,0:T(8,128)(2,1)S(1)} %collective-permute-done.11.refs_2_), channel_id=1, source_target_pairs={{0,8},{1,57},{8,16},{9,1},{16,24},{17,9},{24,32},{25,17},{32,40},{... | collective-permute-start | bytes 2752520 | tf_op jit(solution)/shard_map/ppermute | solution.py:288
  96.6 33.6 %all-to-all-start.1 = ((bf16[8,40,3712]{2,1,0:T(8,128)(2,1)}), bf16[8,40,3712]{2,1,0:T(8,128)(2,1)}, u32[]{:S(2)}, u32[]{:S(2)}) async-start(bf16[8,40,3712]{2,1,0:T(8,128)(2,1)} %bitcast.17), calls=%async_computation.1 | async-start | bytes 4751360 | tf_op jit(solution)/shard_map/all_to_all | solution.py:300
  103.0 13.6 %collective-permute-start.14 = (bf16[256,1792]{1,0:T(8,128)(2,1)S(1)}, bf16[256,1792]{1,0:T(8,128)(2,1)S(1)}, u32[]{:S(2)}, u32[]{:S(2)}) collective-permute-start(bf16[256,1792]{1,0:T(8,128)(2,1)S(1)} %collective-permute-done.12.refs_2_), channel_id=1, source_target_pairs={{0,8},{1,57},{8,16},{9,1},{16,24},{17,9},{24,32},{25,17},{32,40},{... | collective-permute-start | bytes 2752520 | tf_op jit(solution)/shard_map/ppermute | solution.py:288
  130.3 45.5 %all-to-all-start = ((bf16[8,40,5504]{2,1,0:T(8,128)(2,1)}), bf16[8,40,5504]{2,1,0:T(8,128)(2,1)S(1)}, u32[]{:S(2)}, u32[]{:S(2)}) async-start(bf16[8,40,5504]{2,1,0:T(8,128)(2,1)} %bitcast.11), calls=%async_computation | async-start | bytes 7045120 | tf_op jit(solution)/shard_map/all_to_all | solution.py:300
  175.7 1.7 copy-start.2
  177.5 26.8 %copy-start = (f32[1,128,8]{1,2,0:T(8,128)S(1)}, f32[1,128,8]{1,2,0:T(8,128)}, u32[]{:S(2)}) copy-start(f32[1,128,8]{1,2,0:T(8,128)} %param.7) | copy-start | bytes 12292
  177.5 26.8 %copy-start.1 = (s32[1,128,8]{1,2,0:T(8,128)S(1)}, s32[1,128,8]{1,2,0:T(8,128)}, u32[]{:S(2)}) copy-start(s32[1,128,8]{1,2,0:T(8,128)} %param.6) | copy-start | bytes 12292

commit v5 on v4

--- a/solution.py
+++ b/solution.py
@@ -15,6 +15,7 @@
 LANES = 128
 SMALL_VMEM = 12 * 2**20
 PROJECT_VMEM = 57 * 2**20
+LAST_VMEM = 48 * 2**20
 
 
 def iota(shape, dim):
@@ -215,7 +216,7 @@
             jax.ShapeDtypeStruct(scores.shape, jnp.float32),
         ),
         (2 * rows.size * units, 2 * (rows.size + weight.size + 2 * count * slots * units)),
-        vmem=PROJECT_VMEM,
+        vmem=LAST_VMEM if full and half else PROJECT_VMEM,
         grid_spec=pltpu.PrefetchScalarGridSpec(
             num_scalar_prefetch=1,
             grid=(chunks,),

time: 206 us -> 205 us (level)
  no operation moved by 1% of the time
where the time goes in v5:
time: 205 us; the launch traced here: 204 us
  waiting for transfers between devices  83 us (40%)
  starting transfers between devices  51 us (25%)
  Pallas kernels  45.7 us (22%)
  blocking collectives  15.9 us (8%)
  other arithmetic  4.84 us (2%)
  local copies, waits for them, and re-layouts  2.61 us (1%)
    ppermute x11, waiting for transfers between devices, along(): return lax.ppermute(block, ('z', 'core'), pairs)  41.3 us
    all_to_all x4, waiting for transfers between devices, exchange(): lax.all_to_all(block, axes, split_axis=0, concat_axis=0, tiled=True)  37.7 us
    pallas_call x4, Pallas kernels, project(): call(partial(project_kernel, full, half, capacity), (jax.ShapeDtypeStruct...  31.8 us
    ppermute x11, starting transfers between devices, along(): return lax.ppermute(block, ('z', 'core'), pairs)  26.4 us
    all_to_all x4, starting transfers between devices, exchange(): lax.all_to_all(block, axes, split_axis=0, concat_axis=0, tiled=True)  18.1 us
    all_to_all x1, blocking collectives, exchange(): lax.all_to_all(block, axes, split_axis=0, concat_axis=0, tiled=True)  15.9 us
    pallas_call x4, Pallas kernels, select_rows(): call(partial(select_kernel, parts, capacity), (jax.ShapeDtypeStruct((rows...  12.9 us
  transfers between devices with their start and end apart: 19, of which 14 were waited for; matrix products, arithmetic and copies ran while one was open for 2% of the time, Pallas kernels for 17%

profile of v5, /device:TPU:1, one launch (start us, length us, event | category | flops | bytes accessed | tf_op | source)
XLA Modules:
  0.0 203.8 jit_solution(7270384672050662454)
XLA Ops:
  6.5 3.2 %collective-permute-start.3 = (f32[16,128]{1,0:T(8,128)S(1)}, f32[16,128]{1,0:T(8,128)S(1)}, u32[]{:S(2)}, u32[]{:S(2)}) collective-permute-start(f32[16,128]{1,0:T(8,128)S(1)} %pad_maximum_fusion), channel_id=1, source_target_pairs={{0,1},{1,0},{2,3},{3,2},{4,5},{5,4},{6,7},{7,6},{8,9},{9,8},{10,11... | collective-permute-start | bytes 24584 | tf_op jit(solution)/shard_map/ppermute | solution.py:279
  11.4 5.2 %collective-permute-start.7 = (f32[16,256]{1,0:T(8,128)S(1)}, f32[16,256]{1,0:T(8,128)S(1)}, u32[]{:S(2)}, u32[]{:S(2)}) collective-permute-start(f32[16,256]{1,0:T(8,128)S(1)} %maximum_select_fusion.1.refs_0_), channel_id=1, source_target_pairs={{0,32},{1,33},{8,40},{9,41},{16,48},{17,49},{24,56},{25,57},{32,0}... | collective-permute-start | bytes 49160 | tf_op jit(solution)/shard_map/ppermute | solution.py:289
  18.0 4.2 %collective-permute-start.5 = (f32[16,256]{1,0:T(8,128)S(1)}, f32[16,256]{1,0:T(8,128)S(1)}, u32[]{:S(2)}, u32[]{:S(2)}) collective-permute-start(f32[16,256]{1,0:T(8,128)S(1)} %maximum_select_fusion.1.refs_0_), channel_id=1, source_target_pairs={{0,16},{1,49},{8,24},{9,57},{16,32},{17,1},{24,40},{25,9},{32,48},... | collective-permute-start | bytes 49160 | tf_op jit(solution)/shard_map/ppermute | solution.py:289
  23.0 2.1 %collective-permute-done.4.refs_0_ = f32[16,256]{1,0:T(8,128)S(1)} collective-permute-done((f32[16,256]{1,0:T(8,128)S(1)}, f32[16,256]{1,0:T(8,128)S(1)}, u32[]{:S(2)}, u32[]{:S(2)}) %collective-permute-start.4) | collective-permute-done | bytes 16416 | tf_op jit(solution)/shard_map/ppermute | solution.py:289
  25.2 3.2 %collective-permute-done = bf16[128,1792]{1,0:T(8,128)(2,1)} collective-permute-done((bf16[128,1792]{1,0:T(8,128)(2,1)S(1)}, bf16[128,1792]{1,0:T(8,128)(2,1)}, u32[]{:S(2)}, u32[]{:S(2)}) %collective-permute-start) | collective-permute-done | bytes 458784 | tf_op jit(solution)/shard_map/ppermute | solution.py:272
  29.7 2.0 collective-permute-start.9
  31.7 3.6 %collective-permute-start.8 = (bf16[256,1792]{1,0:T(8,128)(2,1)S(1)}, bf16[256,1792]{1,0:T(8,128)(2,1)}, u32[]{:S(2)}, u32[]{:S(2)}) collective-permute-start(bf16[256,1792]{1,0:T(8,128)(2,1)S(1)} %maximum_select_fusion.refs_1_), channel_id=1, source_target_pairs={{0,8},{1,57},{8,16},{9,1},{16,24},{17,9},{24,32},{25,17},{32,40},{... | collective-permute-start | bytes 2752520 | tf_op jit(solution)/shard_map/ppermute | solution.py:289
  35.3 2.1 %shard_map.68 = (bf16[320,1920]{1,0:T(8,128)(2,1)}, f32[8,128]{1,0:T(8,128)S(1)}) custom-call(s32[2]{0:T(128)S(1)} %pad_add_fusion.1.place_ref, f32[8,128]{1,0:T(8,128)S(1)} %broadcast_in_dim.9.token_ref, f32[16,256]{1,0:T(8,128)S(1)} %maximum_select_fusion.1.refs_0_, bf16[256,1792]{1,0:T(8,128)(2,1)S(1)} %maximum_select_fusion.refs_1_), custom_call_target="tpu_custom_call" | custom-call | flops 3300000000 | bytes 2064384 | tf_op jit(solution)/shard_map/pallas_call | solution.py:109
  37.4 4.6 %all-to-all-start.3 = ((bf16[8,40,1920]{2,1,0:T(8,128)(2,1)}), bf16[8,40,1920]{2,1,0:T(8,128)(2,1)}, u32[]{:S(2)}, u32[]{:S(2)}) async-start(bf16[8,40,1920]{2,1,0:T(8,128)(2,1)} %bitcast.24), calls=%async_computation.3 | async-start | bytes 2457600 | tf_op jit(solution)/shard_map/all_to_all | solution.py:301
  42.0 9.6 %collective-permute-done.9.refs_2_ = bf16[256,1792]{1,0:T(8,128)(2,1)S(1)} collective-permute-done((bf16[256,1792]{1,0:T(8,128)(2,1)S(1)}, bf16[256,1792]{1,0:T(8,128)(2,1)S(1)}, u32[]{:S(2)}, u32[]{:S(2)}) %collective-permute-start.9) | collective-permute-done | bytes 917536 | tf_op jit(solution)/shard_map/ppermute | solution.py:289
  51.6 3.4 %collective-permute-done.8.refs_1_ = bf16[256,1792]{1,0:T(8,128)(2,1)} collective-permute-done((bf16[256,1792]{1,0:T(8,128)(2,1)S(1)}, bf16[256,1792]{1,0:T(8,128)(2,1)}, u32[]{:S(2)}, u32[]{:S(2)}) %collective-permute-start.8) | collective-permute-done | bytes 917536 | tf_op jit(solution)/shard_map/ppermute | solution.py:289
  55.0 3.9 %collective-permute-start.10 = (bf16[256,1792]{1,0:T(8,128)(2,1)}, bf16[256,1792]{1,0:T(8,128)(2,1)S(1)}, u32[]{:S(2)}, u32[]{:S(2)}) collective-permute-start(bf16[256,1792]{1,0:T(8,128)(2,1)} %collective-permute-done.8.refs_1_), channel_id=1, source_target_pairs={{0,8},{1,57},{8,16},{9,1},{16,24},{17,9},{24,32},{25,17},{32,40},{... | collective-permute-start | bytes 2752520 | tf_op jit(solution)/shard_map/ppermute | solution.py:289
  59.0 3.6 %shard_map.69 = (bf16[320,3712]{1,0:T(8,128)(2,1)}, f32[8,128]{1,0:T(8,128)S(1)}) custom-call(s32[2]{0:T(128)S(1)} %pad_add_fusion.1.place_ref, f32[8,128]{1,0:T(8,128)S(1)} %get-tuple-element.41.token_ref, f32[16,256]{1,0:T(8,128)S(1)} %collective-permute-done.4.refs_0_, bf16[256,1792]{1,0:T(8,128)(2,1)} %collective-permute-done.8.refs_1_, ...), custom_call_target="tpu_custom_call" | custom-call | flops 3300000000 | bytes 4128768 | tf_op jit(solution)/shard_map/pallas_call | solution.py:109
  62.6 4.4 %all-to-all-start.2 = ((bf16[8,40,3712]{2,1,0:T(8,128)(2,1)}), bf16[8,40,3712]{2,1,0:T(8,128)(2,1)}, u32[]{:S(2)}, u32[]{:S(2)}) async-start(bf16[8,40,3712]{2,1,0:T(8,128)(2,1)} %bitcast.21), calls=%async_computation.2 | async-start | bytes 4751360 | tf_op jit(solution)/shard_map/all_to_all | solution.py:301
  67.0 2.6 %collective-permute-done.10.refs_1_ = bf16[256,1792]{1,0:T(8,128)(2,1)S(1)} collective-permute-done((bf16[256,1792]{1,0:T(8,128)(2,1)}, bf16[256,1792]{1,0:T(8,128)(2,1)S(1)}, u32[]{:S(2)}, u32[]{:S(2)}) %collective-permute-start.10) | collective-permute-done | bytes 917536 | tf_op jit(solution)/shard_map/ppermute | solution.py:289
  69.6 9.7 %collective-permute-done.11.refs_2_ = bf16[256,1792]{1,0:T(8,128)(2,1)S(1)} collective-permute-done((bf16[256,1792]{1,0:T(8,128)(2,1)S(1)}, bf16[256,1792]{1,0:T(8,128)(2,1)S(1)}, u32[]{:S(2)}, u32[]{:S(2)}) %collective-permute-start.11) | collective-permute-done | bytes 917536 | tf_op jit(solution)/shard_map/ppermute | solution.py:289
  79.3 3.5 %collective-permute-start.12 = (bf16[256,1792]{1,0:T(8,128)(2,1)S(1)}, bf16[256,1792]{1,0:T(8,128)(2,1)S(1)}, u32[]{:S(2)}, u32[]{:S(2)}) collective-permute-start(bf16[256,1792]{1,0:T(8,128)(2,1)S(1)} %collective-permute-done.10.refs_1_), channel_id=1, source_target_pairs={{0,8},{1,57},{8,16},{9,1},{16,24},{17,9},{24,32},{25,17},{32,40},{... | collective-permute-start | bytes 2752520 | tf_op jit(solution)/shard_map/ppermute | solution.py:289
  82.9 2.5 %shard_map.70 = (bf16[320,3712]{1,0:T(8,128)(2,1)}, f32[8,128]{1,0:T(8,128)S(1)}) custom-call(s32[2]{0:T(128)S(1)} %pad_add_fusion.1.place_ref, f32[8,128]{1,0:T(8,128)S(1)} %get-tuple-element.46.token_ref, f32[16,256]{1,0:T(8,128)S(1)} %collective-permute-done.5.refs_0_, bf16[256,1792]{1,0:T(8,128)(2,1)S(1)} %collective-permute-done.10.refs_1_, ...), custom_call_target="tpu_custom_call" | custom-call | flops 15399999488 | bytes 4128768 | tf_op jit(solution)/shard_map/pallas_call | solution.py:109
  85.4 11.2 %all-to-all-done.2 = bf16[8,40,3712]{2,1,0:T(8,128)(2,1)} async-done(((bf16[8,40,3712]{2,1,0:T(8,128)(2,1)}), bf16[8,40,3712]{2,1,0:T(8,128)(2,1)}, u32[]{:S(2)}, u32[]{:S(2)}) %all-to-all-start.2) | async-done | bytes 2375712 | tf_op jit(solution)/shard_map/all_to_all | solution.py:301
  96.6 4.4 %all-to-all-start.1 = ((bf16[8,40,3712]{2,1,0:T(8,128)(2,1)}), bf16[8,40,3712]{2,1,0:T(8,128)(2,1)}, u32[]{:S(2)}, u32[]{:S(2)}) async-start(bf16[8,40,3712]{2,1,0:T(8,128)(2,1)} %bitcast.17), calls=%async_computation.1 | async-start | bytes 4751360 | tf_op jit(solution)/shard_map/all_to_all | solution.py:301
  101.0 2.0 collective-permute-done.13.refs_3_
  103.0 3.2 %collective-permute-start.14 = (bf16[256,1792]{1,0:T(8,128)(2,1)S(1)}, bf16[256,1792]{1,0:T(8,128)(2,1)S(1)}, u32[]{:S(2)}, u32[]{:S(2)}) collective-permute-start(bf16[256,1792]{1,0:T(8,128)(2,1)S(1)} %collective-permute-done.12.refs_2_), channel_id=1, source_target_pairs={{0,8},{1,57},{8,16},{9,1},{16,24},{17,9},{24,32},{25,17},{32,40},{... | collective-permute-start | bytes 2752520 | tf_op jit(solution)/shard_map/ppermute | solution.py:289
  106.3 10.3 %collective-permute-done.14.refs_4_ = bf16[256,1792]{1,0:T(8,128)(2,1)S(1)} collective-permute-done((bf16[256,1792]{1,0:T(8,128)(2,1)S(1)}, bf16[256,1792]{1,0:T(8,128)(2,1)S(1)}, u32[]{:S(2)}, u32[]{:S(2)}) %collective-permute-start.14) | collective-permute-done | bytes 917536 | tf_op jit(solution)/shard_map/ppermute | solution.py:289
  116.6 4.7 %shard_map.71 = (bf16[320,5504]{1,0:T(8,128)(2,1)}, f32[8,128]{1,0:T(8,128)}) custom-call(s32[2]{0:T(128)S(1)} %pad_add_fusion.1.place_ref, f32[8,128]{1,0:T(8,128)S(1)} %get-tuple-element.49.token_ref, f32[16,256]{1,0:T(8,128)S(1)} %collective-permute-done.6.refs_0_, f32[16,256]{1,0:T(8,128)S(1)} %collective-permute-done.7.refs_1_, ...), custom_call_target="tpu_custom_call" | custom-call | flops 8800000000 | bytes 6193152 | tf_op jit(solution)/shard_map/pallas_call | solution.py:109
  121.3 9.0 %all-to-all-done.1 = bf16[8,40,3712]{2,1,0:T(8,128)(2,1)} async-done(((bf16[8,40,3712]{2,1,0:T(8,128)(2,1)}), bf16[8,40,3712]{2,1,0:T(8,128)(2,1)}, u32[]{:S(2)}, u32[]{:S(2)}) %all-to-all-start.1) | async-done | bytes 2375712 | tf_op jit(solution)/shard_map/all_to_all | solution.py:301
  130.3 4.8 %all-to-all-start = ((bf16[8,40,5504]{2,1,0:T(8,128)(2,1)}), bf16[8,40,5504]{2,1,0:T(8,128)(2,1)}, u32[]{:S(2)}, u32[]{:S(2)}) async-start(bf16[8,40,5504]{2,1,0:T(8,128)(2,1)} %bitcast.11), calls=%async_computation | async-start | bytes 7045120 | tf_op jit(solution)/shard_map/all_to_all | solution.py:301
  136.9 6.5 %shard_map.72 = (bf16[8,160,1024]{2,1,0:T(8,128)(2,1)}, f32[64,128]{1,0:T(8,128)}) custom-call(s32[1]{0:T(128)} %bitcast.23.zs_ref, bf16[320,1920]{1,0:T(8,128)(2,1)} %bitcast.25.x_ref, bf16[1024,3584]{1,0:T(8,128)(2,1)} %bitcast.53, bf16[8,160,1024]{2,1,0:T(8,128)(2,1)} %bitcast.39, f32[64,128]{1,0:T(8,128)} %broadcast_in_dim.10.refs_1_), custom_call_target="tpu_custom_call" | custom-call | flops 1258291200 | bytes 9224192 | tf_op jit(solution)/shard_map/pallas_call | solution.py:212
  143.4 7.8 %shard_map.73 = (bf16[8,160,1024]{2,1,0:T(8,128)(2,1)}, f32[64,128]{1,0:T(8,128)}) custom-call(s32[2]{0:T(128)} %pad_add_fusion.3.zs_ref, bf16[320,3712]{1,0:T(8,128)(2,1)} %bitcast.22.x_ref, bf16[1024,3584]{1,0:T(8,128)(2,1)} %bitcast.54, bf16[8,160,1024]{2,1,0:T(8,128)(2,1)} %bitcast.40, ...), custom_call_target="tpu_custom_call", output_to_operand_aliasing={{0}: (6, {})} | custom-call | flops 2432696320 | bytes 11026432 | tf_op jit(solution)/shard_map/pallas_call | solution.py:212
  151.2 8.0 %shard_map.74 = (bf16[8,160,1024]{2,1,0:T(8,128)(2,1)}, f32[64,128]{1,0:T(8,128)}) custom-call(s32[2]{0:T(128)} %pad_add_fusion.2.zs_ref, bf16[320,3712]{1,0:T(8,128)(2,1)} %bitcast.18.x_ref, bf16[1024,3584]{1,0:T(8,128)(2,1)} %bitcast.55, bf16[8,160,1024]{2,1,0:T(8,128)(2,1)} %bitcast.42, ...), custom_call_target="tpu_custom_call", output_to_operand_aliasing={{0}: (6, {})} | custom-call | flops 2432696320 | bytes 11026432 | tf_op jit(solution)/shard_map/pallas_call | solution.py:212
  159.2 17.4 %all-to-all-done = bf16[8,40,5504]{2,1,0:T(8,128)(2,1)} async-done(((bf16[8,40,5504]{2,1,0:T(8,128)(2,1)}), bf16[8,40,5504]{2,1,0:T(8,128)(2,1)}, u32[]{:S(2)}, u32[]{:S(2)}) %all-to-all-start) | async-done | bytes 3522592 | tf_op jit(solution)/shard_map/all_to_all | solution.py:301
  177.4 9.6 %shard_map.75 = (bf16[8,160,1024]{2,1,0:T(8,128)(2,1)}, f32[64,128]{1,0:T(8,128)S(1)}) custom-call(s32[3]{0:T(128)S(1)} %pad_add_fusion.zs_ref, bf16[320,5504]{1,0:T(8,128)(2,1)} %bitcast.12.x_ref, bf16[1024,3584]{1,0:T(8,128)(2,1)} %bitcast.56, bf16[8,160,1024]{2,1,0:T(8,128)(2,1)S(1)} %bitcast.44, ...), custom_call_target="tpu_custom_call", output_to_operand_aliasing={{0}: (7, {})} | custom-call | flops 3607101440 | bytes 12828672 | tf_op jit(solution)/shard_map/pallas_call | solution.py:212
  187.0 15.9 %all_to_all.25 = f32[64,1,128]{2,1,0:T(1,128)S(1)} all-to-all(f32[64,1,128]{2,1,0:T(1,128)S(1)} %bitcast.51), channel_id=1, replica_groups=mesh['pipe'=4,'z'=8,'x'=4,'core'=2] {'z','x','core'}, dimensions={0} | all-to-all | bytes 65536 | tf_op jit(solution)/shard_map/all_to_all | solution.py:301
  (36 shorter events, 14.8 us)
Async XLA Ops:
  1.9 23.3 %collective-permute-start.2 = (bf16[128,1792]{1,0:T(8,128)(2,1)S(1)}, bf16[128,1792]{1,0:T(8,128)(2,1)S(1)}, u32[]{:S(2)}, u32[]{:S(2)}) collective-permute-start(bf16[128,1792]{1,0:T(8,128)(2,1)S(1)} %get-tuple-element.66), channel_id=1, source_target_pairs={{192,193},{193,192},{194,195},{195,194},{196,197},{197,196},{198,1... | collective-permute-start | bytes 1376264 | tf_op jit(solution)/shard_map/ppermute | solution.py:274
  2.6 22.6 %collective-permute-start.1 = (bf16[128,1792]{1,0:T(8,128)(2,1)S(1)}, bf16[128,1792]{1,0:T(8,128)(2,1)S(1)}, u32[]{:S(2)}, u32[]{:S(2)}) collective-permute-start(bf16[128,1792]{1,0:T(8,128)(2,1)S(1)} %get-tuple-element.66), channel_id=1, source_target_pairs={{64,1},{65,0},{128,65},{129,64},{192,129},{193,128},{66,3},{67,2},... | collective-permute-start | bytes 1376264 | tf_op jit(solution)/shard_map/ppermute | solution.py:273
  3.9 24.5 %collective-permute-start = (bf16[128,1792]{1,0:T(8,128)(2,1)S(1)}, bf16[128,1792]{1,0:T(8,128)(2,1)}, u32[]{:S(2)}, u32[]{:S(2)}) collective-permute-start(bf16[128,1792]{1,0:T(8,128)(2,1)S(1)} %get-tuple-element.67), channel_id=1, source_target_pairs={{64,0},{65,1},{128,64},{129,65},{192,128},{193,129},{66,2},{67,3},... | collective-permute-start | bytes 1376264 | tf_op jit(solution)/shard_map/ppermute | solution.py:272
  6.5 4.1 %collective-permute-start.3 = (f32[16,128]{1,0:T(8,128)S(1)}, f32[16,128]{1,0:T(8,128)S(1)}, u32[]{:S(2)}, u32[]{:S(2)}) collective-permute-start(f32[16,128]{1,0:T(8,128)S(1)} %pad_maximum_fusion), channel_id=1, source_target_pairs={{0,1},{1,0},{2,3},{3,2},{4,5},{5,4},{6,7},{7,6},{8,9},{9,8},{10,11... | collective-permute-start | bytes 24584 | tf_op jit(solution)/shard_map/ppermute | solution.py:279
  11.4 6.6 %collective-permute-start.7 = (f32[16,256]{1,0:T(8,128)S(1)}, f32[16,256]{1,0:T(8,128)S(1)}, u32[]{:S(2)}, u32[]{:S(2)}) collective-permute-start(f32[16,256]{1,0:T(8,128)S(1)} %maximum_select_fusion.1.refs_0_), channel_id=1, source_target_pairs={{0,32},{1,33},{8,40},{9,41},{16,48},{17,49},{24,56},{25,57},{32,0}... | collective-permute-start | bytes 49160 | tf_op jit(solution)/shard_map/ppermute | solution.py:289
  16.5 5.6 %collective-permute-start.6 = (f32[16,256]{1,0:T(8,128)S(1)}, f32[16,256]{1,0:T(8,128)S(1)}, u32[]{:S(2)}, u32[]{:S(2)}) collective-permute-start(f32[16,256]{1,0:T(8,128)S(1)} %maximum_select_fusion.1.refs_0_), channel_id=1, source_target_pairs={{0,24},{1,41},{8,32},{9,49},{16,40},{17,57},{24,48},{25,1},{32,56}... | collective-permute-start | bytes 49160 | tf_op jit(solution)/shard_map/ppermute | solution.py:289
  18.0 5.1 %collective-permute-start.5 = (f32[16,256]{1,0:T(8,128)S(1)}, f32[16,256]{1,0:T(8,128)S(1)}, u32[]{:S(2)}, u32[]{:S(2)}) collective-permute-start(f32[16,256]{1,0:T(8,128)S(1)} %maximum_select_fusion.1.refs_0_), channel_id=1, source_target_pairs={{0,16},{1,49},{8,24},{9,57},{16,32},{17,1},{24,40},{25,9},{32,48},... | collective-permute-start | bytes 49160 | tf_op jit(solution)/shard_map/ppermute | solution.py:289
  22.2 3.0 %collective-permute-start.4 = (f32[16,256]{1,0:T(8,128)S(1)}, f32[16,256]{1,0:T(8,128)S(1)}, u32[]{:S(2)}, u32[]{:S(2)}) collective-permute-start(f32[16,256]{1,0:T(8,128)S(1)} %maximum_select_fusion.1.refs_0_), channel_id=1, source_target_pairs={{0,8},{1,57},{8,16},{9,1},{16,24},{17,9},{24,32},{25,17},{32,40},{... | collective-permute-start | bytes 49160 | tf_op jit(solution)/shard_map/ppermute | solution.py:289
  29.7 21.9 %collective-permute-start.9 = (bf16[256,1792]{1,0:T(8,128)(2,1)S(1)}, bf16[256,1792]{1,0:T(8,128)(2,1)S(1)}, u32[]{:S(2)}, u32[]{:S(2)}) collective-permute-start(bf16[256,1792]{1,0:T(8,128)(2,1)S(1)} %maximum_select_fusion.refs_1_), channel_id=1, source_target_pairs={{1,8},{0,57},{9,16},{8,1},{17,24},{16,9},{25,32},{24,17},{33,40},{... | collective-permute-start | bytes 2752520 | tf_op jit(solution)/shard_map/ppermute | solution.py:289
  31.7 23.4 %collective-permute-start.8 = (bf16[256,1792]{1,0:T(8,128)(2,1)S(1)}, bf16[256,1792]{1,0:T(8,128)(2,1)}, u32[]{:S(2)}, u32[]{:S(2)}) collective-permute-start(bf16[256,1792]{1,0:T(8,128)(2,1)S(1)} %maximum_select_fusion.refs_1_), channel_id=1, source_target_pairs={{0,8},{1,57},{8,16},{9,1},{16,24},{17,9},{24,32},{25,17},{32,40},{... | collective-permute-start | bytes 2752520 | tf_op jit(solution)/shard_map/ppermute | solution.py:289
  37.4 25.2 %all-to-all-start.3 = ((bf16[8,40,1920]{2,1,0:T(8,128)(2,1)}), bf16[8,40,1920]{2,1,0:T(8,128)(2,1)}, u32[]{:S(2)}, u32[]{:S(2)}) async-start(bf16[8,40,1920]{2,1,0:T(8,128)(2,1)} %bitcast.24), calls=%async_computation.3 | async-start | bytes 2457600 | tf_op jit(solution)/shard_map/all_to_all | solution.py:301
  55.0 14.6 %collective-permute-start.10 = (bf16[256,1792]{1,0:T(8,128)(2,1)}, bf16[256,1792]{1,0:T(8,128)(2,1)S(1)}, u32[]{:S(2)}, u32[]{:S(2)}) collective-permute-start(bf16[256,1792]{1,0:T(8,128)(2,1)} %collective-permute-done.8.refs_1_), channel_id=1, source_target_pairs={{0,8},{1,57},{8,16},{9,1},{16,24},{17,9},{24,32},{25,17},{32,40},{... | collective-permute-start | bytes 2752520 | tf_op jit(solution)/shard_map/ppermute | solution.py:289
  59.0 20.4 %collective-permute-start.11 = (bf16[256,1792]{1,0:T(8,128)(2,1)S(1)}, bf16[256,1792]{1,0:T(8,128)(2,1)S(1)}, u32[]{:S(2)}, u32[]{:S(2)}) collective-permute-start(bf16[256,1792]{1,0:T(8,128)(2,1)S(1)} %collective-permute-done.9.refs_2_), channel_id=1, source_target_pairs={{0,8},{1,57},{8,16},{9,1},{16,24},{17,9},{24,32},{25,17},{32,40},{... | collective-permute-start | bytes 2752520 | tf_op jit(solution)/shard_map/ppermute | solution.py:289
  62.6 34.0 %all-to-all-start.2 = ((bf16[8,40,3712]{2,1,0:T(8,128)(2,1)}), bf16[8,40,3712]{2,1,0:T(8,128)(2,1)}, u32[]{:S(2)}, u32[]{:S(2)}) async-start(bf16[8,40,3712]{2,1,0:T(8,128)(2,1)} %bitcast.21), calls=%async_computation.2 | async-start | bytes 4751360 | tf_op jit(solution)/shard_map/all_to_all | solution.py:301
  79.3 21.7 %collective-permute-start.12 = (bf16[256,1792]{1,0:T(8,128)(2,1)S(1)}, bf16[256,1792]{1,0:T(8,128)(2,1)S(1)}, u32[]{:S(2)}, u32[]{:S(2)}) collective-permute-start(bf16[256,1792]{1,0:T(8,128)(2,1)S(1)} %collective-permute-done.10.refs_1_), channel_id=1, source_target_pairs={{0,8},{1,57},{8,16},{9,1},{16,24},{17,9},{24,32},{25,17},{32,40},{... | collective-permute-start | bytes 2752520 | tf_op jit(solution)/shard_map/ppermute | solution.py:289
  82.9 20.2 %collective-permute-start.13 = (bf16[256,1792]{1,0:T(8,128)(2,1)S(1)}, bf16[256,1792]{1,0:T(8,128)(2,1)}, u32[]{:S(2)}, u32[]{:S(2)}) collective-permute-start(bf16[256,1792]{1,0:T(8,128)(2,1)S(1)} %collective-permute-done.11.refs_2_), channel_id=1, source_target_pairs={{0,8},{1,57},{8,16},{9,1},{16,24},{17,9},{24,32},{25,17},{32,40},{... | collective-permute-start | bytes 2752520 | tf_op jit(solution)/shard_map/ppermute | solution.py:289
  96.6 33.6 %all-to-all-start.1 = ((bf16[8,40,3712]{2,1,0:T(8,128)(2,1)}), bf16[8,40,3712]{2,1,0:T(8,128)(2,1)}, u32[]{:S(2)}, u32[]{:S(2)}) async-start(bf16[8,40,3712]{2,1,0:T(8,128)(2,1)} %bitcast.17), calls=%async_computation.1 | async-start | bytes 4751360 | tf_op jit(solution)/shard_map/all_to_all | solution.py:301
  103.0 13.6 %collective-permute-start.14 = (bf16[256,1792]{1,0:T(8,128)(2,1)S(1)}, bf16[256,1792]{1,0:T(8,128)(2,1)S(1)}, u32[]{:S(2)}, u32[]{:S(2)}) collective-permute-start(bf16[256,1792]{1,0:T(8,128)(2,1)S(1)} %collective-permute-done.12.refs_2_), channel_id=1, source_target_pairs={{0,8},{1,57},{8,16},{9,1},{16,24},{17,9},{24,32},{25,17},{32,40},{... | collective-permute-start | bytes 2752520 | tf_op jit(solution)/shard_map/ppermute | solution.py:289
  130.3 46.4 %all-to-all-start = ((bf16[8,40,5504]{2,1,0:T(8,128)(2,1)}), bf16[8,40,5504]{2,1,0:T(8,128)(2,1)}, u32[]{:S(2)}, u32[]{:S(2)}) async-start(bf16[8,40,5504]{2,1,0:T(8,128)(2,1)} %bitcast.11), calls=%async_computation | async-start | bytes 7045120 | tf_op jit(solution)/shard_map/all_to_all | solution.py:301
  151.2 25.4 %copy-start = (bf16[1,1,1280,1024]{3,2,1,0:T(8,128)(2,1)S(1)}, bf16[1,1,1280,1024]{3,2,1,0:T(8,128)(2,1)}, u32[]{:S(2)}) copy-start(bf16[1,1,1280,1024]{3,2,1,0:T(8,128)(2,1)} %param.9) | copy-start | bytes 7864324
  176.6 0.8 copy-start.2
  177.4 25.5 %copy-start.1 = (f32[1,128,8]{1,2,0:T(8,128)S(1)}, f32[1,128,8]{1,2,0:T(8,128)}, u32[]{:S(2)}) copy-start(f32[1,128,8]{1,2,0:T(8,128)} %param.7) | copy-start | bytes 12292
  177.4 25.5 %copy-start.3 = (s32[1,128,8]{1,2,0:T(8,128)S(1)}, s32[1,128,8]{1,2,0:T(8,128)}, u32[]{:S(2)}) copy-start(s32[1,128,8]{1,2,0:T(8,128)} %param.6) | copy-start | bytes 12292

commit v6 on v5

--- a/solution.py
+++ b/solution.py
@@ -265,13 +265,8 @@
     half = features // 2
     cores = range(CORES)
 
-    mine = lax.dynamic_slice(upstream[0], (0, core * half), (tokens, half))
-    other = lax.dynamic_slice(upstream[0], (0, (1 - core) * half), (tokens, half))
-    hop = range(1, sections)
     last = sections - 1
-    near = lax.ppermute(mine, ("pipe", "core"), [(i * CORES + c, (i - 1) * CORES + c) for i in hop for c in cores])
-    far = lax.ppermute(other, ("pipe", "core"), [(i * CORES + c, (i - 1) * CORES + 1 - c) for i in hop for c in cores])
-    stay = lax.ppermute(other, ("pipe", "core"), [(last * CORES + c, last * CORES + 1 - c) for c in cores])
+    near = lax.ppermute(upstream[0], "pipe", [(i, i - 1) for i in range(1, sections)])
 
     routes_own = routes[0].T
     affinity_own = affinity[0].T
@@ -300,9 +295,12 @@
         block = block.reshape(parts, shape[0] // parts, shape[1])
         return lax.all_to_all(block, axes, split_axis=0, concat_axis=0, tiled=True).reshape(shape)
 
-    near, far, stay, choices = lax.optimization_barrier((near, far, stay, choices))
-    is_last = section == last
-    held = in_order(jnp.where(is_last, mine, near), jnp.where(is_last, stay, far), 0)
+    near, choices = lax.optimization_barrier((near, choices))
+    incoming = jnp.where(section == last, upstream[0], near)
+    mine = lax.dynamic_slice(incoming, (0, core * half), (tokens, half))
+    other = lax.dynamic_slice(incoming, (0, (1 - core) * half), (tokens, half))
+    mate = lax.ppermute(other, "core", [(c, 1 - c) for c in cores])
+    held = in_order(mine, mate, 0)
     weight = w_down[0, 0]
     saved = saved_hidden[0, 0].reshape(depth, slot_total // depth, units)
     scores = jnp.zeros((expert_count, LANES), jnp.float32)

time: 205 us -> 204 us (level)
    ppermute x3 -> x2, starting transfers between devices: 3.27 us -> 4.87 us  [the longest x1 3.58 us: on_device(): mate = lax.ppermute(other, 'core', [(c, 1 - c) for c in cores])]
  transfers between devices with their start and end apart: 19 -> 18, of which waited for: 14 -> 14; matrix products, arithmetic and copies ran while one was open for 2% -> 2% of each run, Pallas kernels for 17% -> 17%
where the time goes in v6:
time: 204 us
  waiting for transfers between devices  82.3 us (40%)
  starting transfers between devices  52.8 us (26%)
  Pallas kernels  45.6 us (22%)
  blocking collectives  15.8 us (8%)
  other arithmetic  4.89 us (2%)
    ppermute x11, waiting for transfers between devices, along(): return lax.ppermute(block, ('z', 'core'), pairs)  39.9 us
    all_to_all x4, waiting for transfers between devices, exchange(): lax.all_to_all(block, axes, split_axis=0, concat_axis=0, tiled=True)  37.8 us
    pallas_call x4, Pallas kernels, project(): call(partial(project_kernel, full, half, capacity), (jax.ShapeDtypeStruct...  31.9 us
    ppermute x11, starting transfers between devices, along(): return lax.ppermute(block, ('z', 'core'), pairs)  26.6 us
    all_to_all x4, starting transfers between devices, exchange(): lax.all_to_all(block, axes, split_axis=0, concat_axis=0, tiled=True)  18.1 us
    all_to_all x1, blocking collectives, exchange(): lax.all_to_all(block, axes, split_axis=0, concat_axis=0, tiled=True)  15.8 us
    pallas_call x4, Pallas kernels, select_rows(): call(partial(select_kernel, parts, capacity), (jax.ShapeDtypeStruct((rows...  12.9 us
  transfers between devices with their start and end apart: 18, of which 14 were waited for; matrix products, arithmetic and copies ran while one was open for 2% of the time, Pallas kernels for 17%

profile of v6, /device:TPU:1, one launch (start us, length us, event | category | flops | bytes accessed | tf_op | source)
XLA Modules:
  0.0 203.6 jit_solution(16115958419012621877)
XLA Ops:
  3.3 3.2 %collective-permute-start.1 = (f32[16,128]{1,0:T(8,128)S(1)}, f32[16,128]{1,0:T(8,128)S(1)}, u32[]{:S(2)}, u32[]{:S(2)}) collective-permute-start(f32[16,128]{1,0:T(8,128)S(1)} %pad_maximum_fusion), channel_id=1, source_target_pairs={{0,1},{1,0},{2,3},{3,2},{4,5},{5,4},{6,7},{7,6},{8,9},{9,8},{10,11... | collective-permute-start | bytes 24584 | tf_op jit(solution)/shard_map/ppermute | solution.py:274
  8.1 5.2 %collective-permute-start.5 = (f32[16,256]{1,0:T(8,128)S(1)}, f32[16,256]{1,0:T(8,128)S(1)}, u32[]{:S(2)}, u32[]{:S(2)}) collective-permute-start(f32[16,256]{1,0:T(8,128)S(1)} %maximum_select_fusion.1.refs_0_), channel_id=1, source_target_pairs={{0,32},{1,33},{8,40},{9,41},{16,48},{17,49},{24,56},{25,57},{32,0}... | collective-permute-start | bytes 49160 | tf_op jit(solution)/shard_map/ppermute | solution.py:284
  13.3 4.0 %collective-permute-start.3 = (f32[16,256]{1,0:T(8,128)S(1)}, f32[16,256]{1,0:T(8,128)S(1)}, u32[]{:S(2)}, u32[]{:S(2)}) collective-permute-start(f32[16,256]{1,0:T(8,128)S(1)} %maximum_select_fusion.1.refs_0_), channel_id=1, source_target_pairs={{0,16},{1,49},{8,24},{9,57},{16,32},{17,1},{24,40},{25,9},{32,48},... | collective-permute-start | bytes 49160 | tf_op jit(solution)/shard_map/ppermute | solution.py:284
  20.2 2.4 %collective-permute-done = bf16[128,3584]{1,0:T(8,128)(2,1)S(1)} collective-permute-done((bf16[128,3584]{1,0:T(8,128)(2,1)}, bf16[128,3584]{1,0:T(8,128)(2,1)S(1)}, u32[]{:S(2)}, u32[]{:S(2)}) %collective-permute-start) | collective-permute-done | bytes 917536 | tf_op jit(solution)/shard_map/ppermute | solution.py:269
  24.0 3.6 %collective-permute-start.6 = (bf16[128,1792]{1,0:T(8,128)(2,1)S(1)}, bf16[128,1792]{1,0:T(8,128)(2,1)S(1)}, u32[]{:S(2)}, u32[]{:S(2)}) collective-permute-start(bf16[128,1792]{1,0:T(8,128)(2,1)S(1)} %get-tuple-element.63), channel_id=1, source_target_pairs={{0,1},{1,0},{2,3},{3,2},{4,5},{5,4},{6,7},{7,6},{8,9},{9,8},{10,11... | collective-permute-start | bytes 1376264 | tf_op jit(solution)/shard_map/ppermute | solution.py:302
  29.2 2.1 %collective-permute-start.8 = (bf16[256,1792]{1,0:T(8,128)(2,1)S(1)}, bf16[256,1792]{1,0:T(8,128)(2,1)S(1)}, u32[]{:S(2)}, u32[]{:S(2)}) collective-permute-start(bf16[256,1792]{1,0:T(8,128)(2,1)S(1)} %maximum_select_fusion.refs_1_), channel_id=1, source_target_pairs={{1,8},{0,57},{9,16},{8,1},{17,24},{16,9},{25,32},{24,17},{33,40},{... | collective-permute-start | bytes 2752520 | tf_op jit(solution)/shard_map/ppermute | solution.py:284
  31.4 3.8 %collective-permute-start.7 = (bf16[256,1792]{1,0:T(8,128)(2,1)S(1)}, bf16[256,1792]{1,0:T(8,128)(2,1)}, u32[]{:S(2)}, u32[]{:S(2)}) collective-permute-start(bf16[256,1792]{1,0:T(8,128)(2,1)S(1)} %maximum_select_fusion.refs_1_), channel_id=1, source_target_pairs={{0,8},{1,57},{8,16},{9,1},{16,24},{17,9},{24,32},{25,17},{32,40},{... | collective-permute-start | bytes 2752520 | tf_op jit(solution)/shard_map/ppermute | solution.py:284
  35.2 2.1 %shard_map.68 = (bf16[320,1920]{1,0:T(8,128)(2,1)}, f32[8,128]{1,0:T(8,128)S(1)}) custom-call(s32[2]{0:T(128)S(1)} %pad_add_fusion.1.place_ref, f32[8,128]{1,0:T(8,128)S(1)} %broadcast_in_dim.9.token_ref, f32[16,256]{1,0:T(8,128)S(1)} %maximum_select_fusion.1.refs_0_, bf16[256,1792]{1,0:T(8,128)(2,1)S(1)} %maximum_select_fusion.refs_1_), custom_call_target="tpu_custom_call" | custom-call | flops 3300000000 | bytes 2064384 | tf_op jit(solution)/shard_map/pallas_call | solution.py:109
  37.3 4.6 %all-to-all-start.3 = ((bf16[8,40,1920]{2,1,0:T(8,128)(2,1)}), bf16[8,40,1920]{2,1,0:T(8,128)(2,1)}, u32[]{:S(2)}, u32[]{:S(2)}) async-start(bf16[8,40,1920]{2,1,0:T(8,128)(2,1)} %bitcast.23), calls=%async_computation.3 | async-start | bytes 2457600 | tf_op jit(solution)/shard_map/all_to_all | solution.py:296
  41.9 9.4 %collective-permute-done.8.refs_2_ = bf16[256,1792]{1,0:T(8,128)(2,1)S(1)} collective-permute-done((bf16[256,1792]{1,0:T(8,128)(2,1)S(1)}, bf16[256,1792]{1,0:T(8,128)(2,1)S(1)}, u32[]{:S(2)}, u32[]{:S(2)}) %collective-permute-start.8) | collective-permute-done | bytes 917536 | tf_op jit(solution)/shard_map/ppermute | solution.py:284
  51.3 3.6 %collective-permute-done.7.refs_1_ = bf16[256,1792]{1,0:T(8,128)(2,1)} collective-permute-done((bf16[256,1792]{1,0:T(8,128)(2,1)S(1)}, bf16[256,1792]{1,0:T(8,128)(2,1)}, u32[]{:S(2)}, u32[]{:S(2)}) %collective-permute-start.7) | collective-permute-done | bytes 917536 | tf_op jit(solution)/shard_map/ppermute | solution.py:284
  54.9 3.9 %collective-permute-start.9 = (bf16[256,1792]{1,0:T(8,128)(2,1)}, bf16[256,1792]{1,0:T(8,128)(2,1)S(1)}, u32[]{:S(2)}, u32[]{:S(2)}) collective-permute-start(bf16[256,1792]{1,0:T(8,128)(2,1)} %collective-permute-done.7.refs_1_), channel_id=1, source_target_pairs={{0,8},{1,57},{8,16},{9,1},{16,24},{17,9},{24,32},{25,17},{32,40},{... | collective-permute-start | bytes 2752520 | tf_op jit(solution)/shard_map/ppermute | solution.py:284
  58.9 3.6 %shard_map.69 = (bf16[320,3712]{1,0:T(8,128)(2,1)}, f32[8,128]{1,0:T(8,128)S(1)}) custom-call(s32[2]{0:T(128)S(1)} %pad_add_fusion.1.place_ref, f32[8,128]{1,0:T(8,128)S(1)} %get-tuple-element.37.token_ref, f32[16,256]{1,0:T(8,128)S(1)} %collective-permute-done.2.refs_0_, bf16[256,1792]{1,0:T(8,128)(2,1)} %collective-permute-done.7.refs_1_, ...), custom_call_target="tpu_custom_call" | custom-call | flops 3300000000 | bytes 4128768 | tf_op jit(solution)/shard_map/pallas_call | solution.py:109
  62.5 4.4 %all-to-all-start.2 = ((bf16[8,40,3712]{2,1,0:T(8,128)(2,1)}), bf16[8,40,3712]{2,1,0:T(8,128)(2,1)}, u32[]{:S(2)}, u32[]{:S(2)}) async-start(bf16[8,40,3712]{2,1,0:T(8,128)(2,1)} %bitcast.20), calls=%async_computation.2 | async-start | bytes 4751360 | tf_op jit(solution)/shard_map/all_to_all | solution.py:296
  66.9 2.6 %collective-permute-done.9.refs_1_ = bf16[256,1792]{1,0:T(8,128)(2,1)S(1)} collective-permute-done((bf16[256,1792]{1,0:T(8,128)(2,1)}, bf16[256,1792]{1,0:T(8,128)(2,1)S(1)}, u32[]{:S(2)}, u32[]{:S(2)}) %collective-permute-start.9) | collective-permute-done | bytes 917536 | tf_op jit(solution)/shard_map/ppermute | solution.py:284
  69.5 9.7 %collective-permute-done.10.refs_2_ = bf16[256,1792]{1,0:T(8,128)(2,1)S(1)} collective-permute-done((bf16[256,1792]{1,0:T(8,128)(2,1)S(1)}, bf16[256,1792]{1,0:T(8,128)(2,1)S(1)}, u32[]{:S(2)}, u32[]{:S(2)}) %collective-permute-start.10) | collective-permute-done | bytes 917536 | tf_op jit(solution)/shard_map/ppermute | solution.py:284
  79.2 3.5 %collective-permute-start.11 = (bf16[256,1792]{1,0:T(8,128)(2,1)S(1)}, bf16[256,1792]{1,0:T(8,128)(2,1)S(1)}, u32[]{:S(2)}, u32[]{:S(2)}) collective-permute-start(bf16[256,1792]{1,0:T(8,128)(2,1)S(1)} %collective-permute-done.9.refs_1_), channel_id=1, source_target_pairs={{0,8},{1,57},{8,16},{9,1},{16,24},{17,9},{24,32},{25,17},{32,40},{... | collective-permute-start | bytes 2752520 | tf_op jit(solution)/shard_map/ppermute | solution.py:284
  82.8 2.5 %shard_map.70 = (bf16[320,3712]{1,0:T(8,128)(2,1)}, f32[8,128]{1,0:T(8,128)S(1)}) custom-call(s32[2]{0:T(128)S(1)} %pad_add_fusion.1.place_ref, f32[8,128]{1,0:T(8,128)S(1)} %get-tuple-element.42.token_ref, f32[16,256]{1,0:T(8,128)S(1)} %collective-permute-done.3.refs_0_, bf16[256,1792]{1,0:T(8,128)(2,1)S(1)} %collective-permute-done.9.refs_1_, ...), custom_call_target="tpu_custom_call" | custom-call | flops 15399999488 | bytes 4128768 | tf_op jit(solution)/shard_map/pallas_call | solution.py:109
  85.3 11.3 %all-to-all-done.2 = bf16[8,40,3712]{2,1,0:T(8,128)(2,1)} async-done(((bf16[8,40,3712]{2,1,0:T(8,128)(2,1)}), bf16[8,40,3712]{2,1,0:T(8,128)(2,1)}, u32[]{:S(2)}, u32[]{:S(2)}) %all-to-all-start.2) | async-done | bytes 2375712 | tf_op jit(solution)/shard_map/all_to_all | solution.py:296
  96.5 4.3 %all-to-all-start.1 = ((bf16[8,40,3712]{2,1,0:T(8,128)(2,1)}), bf16[8,40,3712]{2,1,0:T(8,128)(2,1)}, u32[]{:S(2)}, u32[]{:S(2)}) async-start(bf16[8,40,3712]{2,1,0:T(8,128)(2,1)} %bitcast.16), calls=%async_computation.1 | async-start | bytes 4751360 | tf_op jit(solution)/shard_map/all_to_all | solution.py:296
  100.9 2.0 %collective-permute-done.12.refs_3_ = bf16[256,1792]{1,0:T(8,128)(2,1)} collective-permute-done((bf16[256,1792]{1,0:T(8,128)(2,1)S(1)}, bf16[256,1792]{1,0:T(8,128)(2,1)}, u32[]{:S(2)}, u32[]{:S(2)}) %collective-permute-start.12) | collective-permute-done | bytes 917536 | tf_op jit(solution)/shard_map/ppermute | solution.py:284
  102.9 3.2 %collective-permute-start.13 = (bf16[256,1792]{1,0:T(8,128)(2,1)S(1)}, bf16[256,1792]{1,0:T(8,128)(2,1)S(1)}, u32[]{:S(2)}, u32[]{:S(2)}) collective-permute-start(bf16[256,1792]{1,0:T(8,128)(2,1)S(1)} %collective-permute-done.11.refs_2_), channel_id=1, source_target_pairs={{0,8},{1,57},{8,16},{9,1},{16,24},{17,9},{24,32},{25,17},{32,40},{... | collective-permute-start | bytes 2752520 | tf_op jit(solution)/shard_map/ppermute | solution.py:284
  106.1 10.3 %collective-permute-done.13.refs_4_ = bf16[256,1792]{1,0:T(8,128)(2,1)S(1)} collective-permute-done((bf16[256,1792]{1,0:T(8,128)(2,1)S(1)}, bf16[256,1792]{1,0:T(8,128)(2,1)S(1)}, u32[]{:S(2)}, u32[]{:S(2)}) %collective-permute-start.13) | collective-permute-done | bytes 917536 | tf_op jit(solution)/shard_map/ppermute | solution.py:284
  116.5 4.7 %shard_map.71 = (bf16[320,5504]{1,0:T(8,128)(2,1)}, f32[8,128]{1,0:T(8,128)}) custom-call(s32[2]{0:T(128)S(1)} %pad_add_fusion.1.place_ref, f32[8,128]{1,0:T(8,128)S(1)} %get-tuple-element.45.token_ref, f32[16,256]{1,0:T(8,128)S(1)} %collective-permute-done.4.refs_0_, f32[16,256]{1,0:T(8,128)S(1)} %collective-permute-done.5.refs_1_, ...), custom_call_target="tpu_custom_call" | custom-call | flops 8800000000 | bytes 6193152 | tf_op jit(solution)/shard_map/pallas_call | solution.py:109
  121.1 9.0 %all-to-all-done.1 = bf16[8,40,3712]{2,1,0:T(8,128)(2,1)} async-done(((bf16[8,40,3712]{2,1,0:T(8,128)(2,1)}), bf16[8,40,3712]{2,1,0:T(8,128)(2,1)}, u32[]{:S(2)}, u32[]{:S(2)}) %all-to-all-start.1) | async-done | bytes 2375712 | tf_op jit(solution)/shard_map/all_to_all | solution.py:296
  130.2 4.7 %all-to-all-start = ((bf16[8,40,5504]{2,1,0:T(8,128)(2,1)}), bf16[8,40,5504]{2,1,0:T(8,128)(2,1)}, u32[]{:S(2)}, u32[]{:S(2)}) async-start(bf16[8,40,5504]{2,1,0:T(8,128)(2,1)} %bitcast.10), calls=%async_computation | async-start | bytes 7045120 | tf_op jit(solution)/shard_map/all_to_all | solution.py:296
  136.7 6.5 %shard_map.72 = (bf16[8,160,1024]{2,1,0:T(8,128)(2,1)}, f32[64,128]{1,0:T(8,128)}) custom-call(s32[1]{0:T(128)} %bitcast.22.zs_ref, bf16[320,1920]{1,0:T(8,128)(2,1)} %bitcast.24.x_ref, bf16[1024,3584]{1,0:T(8,128)(2,1)} %bitcast.51, bf16[8,160,1024]{2,1,0:T(8,128)(2,1)} %bitcast.37, f32[64,128]{1,0:T(8,128)} %broadcast_in_dim.10.refs_1_), custom_call_target="tpu_custom_call" | custom-call | flops 1258291200 | bytes 9224192 | tf_op jit(solution)/shard_map/pallas_call | solution.py:212
  143.2 7.8 %shard_map.73 = (bf16[8,160,1024]{2,1,0:T(8,128)(2,1)}, f32[64,128]{1,0:T(8,128)}) custom-call(s32[2]{0:T(128)} %pad_add_fusion.3.zs_ref, bf16[320,3712]{1,0:T(8,128)(2,1)} %bitcast.21.x_ref, bf16[1024,3584]{1,0:T(8,128)(2,1)} %bitcast.52, bf16[8,160,1024]{2,1,0:T(8,128)(2,1)} %bitcast.38, ...), custom_call_target="tpu_custom_call", output_to_operand_aliasing={{0}: (6, {})} | custom-call | flops 2432696320 | bytes 11026432 | tf_op jit(solution)/shard_map/pallas_call | solution.py:212
  151.1 8.0 %shard_map.74 = (bf16[8,160,1024]{2,1,0:T(8,128)(2,1)}, f32[64,128]{1,0:T(8,128)}) custom-call(s32[2]{0:T(128)} %pad_add_fusion.2.zs_ref, bf16[320,3712]{1,0:T(8,128)(2,1)} %bitcast.17.x_ref, bf16[1024,3584]{1,0:T(8,128)(2,1)} %bitcast.53, bf16[8,160,1024]{2,1,0:T(8,128)(2,1)} %bitcast.40, ...), custom_call_target="tpu_custom_call", output_to_operand_aliasing={{0}: (6, {})} | custom-call | flops 2432696320 | bytes 11026432 | tf_op jit(solution)/shard_map/pallas_call | solution.py:212
  159.0 17.5 %all-to-all-done = bf16[8,40,5504]{2,1,0:T(8,128)(2,1)} async-done(((bf16[8,40,5504]{2,1,0:T(8,128)(2,1)}), bf16[8,40,5504]{2,1,0:T(8,128)(2,1)}, u32[]{:S(2)}, u32[]{:S(2)}) %all-to-all-start) | async-done | bytes 3522592 | tf_op jit(solution)/shard_map/all_to_all | solution.py:296
  177.3 9.6 %shard_map.75 = (bf16[8,160,1024]{2,1,0:T(8,128)(2,1)}, f32[64,128]{1,0:T(8,128)S(1)}) custom-call(s32[3]{0:T(128)S(1)} %pad_add_fusion.zs_ref, bf16[320,5504]{1,0:T(8,128)(2,1)} %bitcast.11.x_ref, bf16[1024,3584]{1,0:T(8,128)(2,1)} %bitcast.54, bf16[8,160,1024]{2,1,0:T(8,128)(2,1)S(1)} %bitcast.42, ...), custom_call_target="tpu_custom_call", output_to_operand_aliasing={{0}: (7, {})} | custom-call | flops 3607101440 | bytes 12828672 | tf_op jit(solution)/shard_map/pallas_call | solution.py:212
  186.9 15.8 %all_to_all.25 = f32[64,1,128]{2,1,0:T(1,128)S(1)} all-to-all(f32[64,1,128]{2,1,0:T(1,128)S(1)} %bitcast.49), channel_id=1, replica_groups=mesh['pipe'=4,'z'=8,'x'=4,'core'=2] {'z','x','core'}, dimensions={0} | all-to-all | bytes 65536 | tf_op jit(solution)/shard_map/all_to_all | solution.py:296
  (34 shorter events, 13.7 us)
Async XLA Ops:
  0.6 22.0 %collective-permute-start = (bf16[128,3584]{1,0:T(8,128)(2,1)}, bf16[128,3584]{1,0:T(8,128)(2,1)S(1)}, u32[]{:S(2)}, u32[]{:S(2)}) collective-permute-start(bf16[128,3584]{1,0:T(8,128)(2,1)} %bitcast.56), channel_id=1, source_target_pairs={{64,0},{128,64},{192,128},{65,1},{129,65},{193,129},{66,2},{130,66... | collective-permute-start | bytes 2752520 | tf_op jit(solution)/shard_map/ppermute | solution.py:269
  3.3 4.1 %collective-permute-start.1 = (f32[16,128]{1,0:T(8,128)S(1)}, f32[16,128]{1,0:T(8,128)S(1)}, u32[]{:S(2)}, u32[]{:S(2)}) collective-permute-start(f32[16,128]{1,0:T(8,128)S(1)} %pad_maximum_fusion), channel_id=1, source_target_pairs={{0,1},{1,0},{2,3},{3,2},{4,5},{5,4},{6,7},{7,6},{8,9},{9,8},{10,11... | collective-permute-start | bytes 24584 | tf_op jit(solution)/shard_map/ppermute | solution.py:274
  8.1 9.9 %collective-permute-start.5 = (f32[16,256]{1,0:T(8,128)S(1)}, f32[16,256]{1,0:T(8,128)S(1)}, u32[]{:S(2)}, u32[]{:S(2)}) collective-permute-start(f32[16,256]{1,0:T(8,128)S(1)} %maximum_select_fusion.1.refs_0_), channel_id=1, source_target_pairs={{0,32},{1,33},{8,40},{9,41},{16,48},{17,49},{24,56},{25,57},{32,0}... | collective-permute-start | bytes 49160 | tf_op jit(solution)/shard_map/ppermute | solution.py:284
  13.3 4.8 %collective-permute-start.4 = (f32[16,256]{1,0:T(8,128)S(1)}, f32[16,256]{1,0:T(8,128)S(1)}, u32[]{:S(2)}, u32[]{:S(2)}) collective-permute-start(f32[16,256]{1,0:T(8,128)S(1)} %maximum_select_fusion.1.refs_0_), channel_id=1, source_target_pairs={{0,24},{1,41},{8,32},{9,49},{16,40},{17,57},{24,48},{25,1},{32,56}... | collective-permute-start | bytes 49160 | tf_op jit(solution)/shard_map/ppermute | solution.py:284
  13.3 4.9 %collective-permute-start.3 = (f32[16,256]{1,0:T(8,128)S(1)}, f32[16,256]{1,0:T(8,128)S(1)}, u32[]{:S(2)}, u32[]{:S(2)}) collective-permute-start(f32[16,256]{1,0:T(8,128)S(1)} %maximum_select_fusion.1.refs_0_), channel_id=1, source_target_pairs={{0,16},{1,49},{8,24},{9,57},{16,32},{17,1},{24,40},{25,9},{32,48},... | collective-permute-start | bytes 49160 | tf_op jit(solution)/shard_map/ppermute | solution.py:284
  17.4 2.9 %collective-permute-start.2 = (f32[16,256]{1,0:T(8,128)S(1)}, f32[16,256]{1,0:T(8,128)S(1)}, u32[]{:S(2)}, u32[]{:S(2)}) collective-permute-start(f32[16,256]{1,0:T(8,128)S(1)} %maximum_select_fusion.1.refs_0_), channel_id=1, source_target_pairs={{0,8},{1,57},{8,16},{9,1},{16,24},{17,9},{24,32},{25,17},{32,40},{... | collective-permute-start | bytes 49160 | tf_op jit(solution)/shard_map/ppermute | solution.py:284
  24.0 5.0 %collective-permute-start.6 = (bf16[128,1792]{1,0:T(8,128)(2,1)S(1)}, bf16[128,1792]{1,0:T(8,128)(2,1)S(1)}, u32[]{:S(2)}, u32[]{:S(2)}) collective-permute-start(bf16[128,1792]{1,0:T(8,128)(2,1)S(1)} %get-tuple-element.63), channel_id=1, source_target_pairs={{0,1},{1,0},{2,3},{3,2},{4,5},{5,4},{6,7},{7,6},{8,9},{9,8},{10,11... | collective-permute-start | bytes 1376264 | tf_op jit(solution)/shard_map/ppermute | solution.py:302
  29.2 22.1 %collective-permute-start.8 = (bf16[256,1792]{1,0:T(8,128)(2,1)S(1)}, bf16[256,1792]{1,0:T(8,128)(2,1)S(1)}, u32[]{:S(2)}, u32[]{:S(2)}) collective-permute-start(bf16[256,1792]{1,0:T(8,128)(2,1)S(1)} %maximum_select_fusion.refs_1_), channel_id=1, source_target_pairs={{1,8},{0,57},{9,16},{8,1},{17,24},{16,9},{25,32},{24,17},{33,40},{... | collective-permute-start | bytes 2752520 | tf_op jit(solution)/shard_map/ppermute | solution.py:284
  31.4 23.5 %collective-permute-start.7 = (bf16[256,1792]{1,0:T(8,128)(2,1)S(1)}, bf16[256,1792]{1,0:T(8,128)(2,1)}, u32[]{:S(2)}, u32[]{:S(2)}) collective-permute-start(bf16[256,1792]{1,0:T(8,128)(2,1)S(1)} %maximum_select_fusion.refs_1_), channel_id=1, source_target_pairs={{0,8},{1,57},{8,16},{9,1},{16,24},{17,9},{24,32},{25,17},{32,40},{... | collective-permute-start | bytes 2752520 | tf_op jit(solution)/shard_map/ppermute | solution.py:284
  37.3 25.2 %all-to-all-start.3 = ((bf16[8,40,1920]{2,1,0:T(8,128)(2,1)}), bf16[8,40,1920]{2,1,0:T(8,128)(2,1)}, u32[]{:S(2)}, u32[]{:S(2)}) async-start(bf16[8,40,1920]{2,1,0:T(8,128)(2,1)} %bitcast.23), calls=%async_computation.3 | async-start | bytes 2457600 | tf_op jit(solution)/shard_map/all_to_all | solution.py:296
  54.9 14.6 %collective-permute-start.9 = (bf16[256,1792]{1,0:T(8,128)(2,1)}, bf16[256,1792]{1,0:T(8,128)(2,1)S(1)}, u32[]{:S(2)}, u32[]{:S(2)}) collective-permute-start(bf16[256,1792]{1,0:T(8,128)(2,1)} %collective-permute-done.7.refs_1_), channel_id=1, source_target_pairs={{0,8},{1,57},{8,16},{9,1},{16,24},{17,9},{24,32},{25,17},{32,40},{... | collective-permute-start | bytes 2752520 | tf_op jit(solution)/shard_map/ppermute | solution.py:284
  58.8 20.4 %collective-permute-start.10 = (bf16[256,1792]{1,0:T(8,128)(2,1)S(1)}, bf16[256,1792]{1,0:T(8,128)(2,1)S(1)}, u32[]{:S(2)}, u32[]{:S(2)}) collective-permute-start(bf16[256,1792]{1,0:T(8,128)(2,1)S(1)} %collective-permute-done.8.refs_2_), channel_id=1, source_target_pairs={{0,8},{1,57},{8,16},{9,1},{16,24},{17,9},{24,32},{25,17},{32,40},{... | collective-permute-start | bytes 2752520 | tf_op jit(solution)/shard_map/ppermute | solution.py:284
  62.5 34.0 %all-to-all-start.2 = ((bf16[8,40,3712]{2,1,0:T(8,128)(2,1)}), bf16[8,40,3712]{2,1,0:T(8,128)(2,1)}, u32[]{:S(2)}, u32[]{:S(2)}) async-start(bf16[8,40,3712]{2,1,0:T(8,128)(2,1)} %bitcast.20), calls=%async_computation.2 | async-start | bytes 4751360 | tf_op jit(solution)/shard_map/all_to_all | solution.py:296
  79.2 21.6 %collective-permute-start.11 = (bf16[256,1792]{1,0:T(8,128)(2,1)S(1)}, bf16[256,1792]{1,0:T(8,128)(2,1)S(1)}, u32[]{:S(2)}, u32[]{:S(2)}) collective-permute-start(bf16[256,1792]{1,0:T(8,128)(2,1)S(1)} %collective-permute-done.9.refs_1_), channel_id=1, source_target_pairs={{0,8},{1,57},{8,16},{9,1},{16,24},{17,9},{24,32},{25,17},{32,40},{... | collective-permute-start | bytes 2752520 | tf_op jit(solution)/shard_map/ppermute | solution.py:284
  82.7 20.2 %collective-permute-start.12 = (bf16[256,1792]{1,0:T(8,128)(2,1)S(1)}, bf16[256,1792]{1,0:T(8,128)(2,1)}, u32[]{:S(2)}, u32[]{:S(2)}) collective-permute-start(bf16[256,1792]{1,0:T(8,128)(2,1)S(1)} %collective-permute-done.10.refs_2_), channel_id=1, source_target_pairs={{0,8},{1,57},{8,16},{9,1},{16,24},{17,9},{24,32},{25,17},{32,40},{... | collective-permute-start | bytes 2752520 | tf_op jit(solution)/shard_map/ppermute | solution.py:284
  96.5 33.6 %all-to-all-start.1 = ((bf16[8,40,3712]{2,1,0:T(8,128)(2,1)}), bf16[8,40,3712]{2,1,0:T(8,128)(2,1)}, u32[]{:S(2)}, u32[]{:S(2)}) async-start(bf16[8,40,3712]{2,1,0:T(8,128)(2,1)} %bitcast.16), calls=%async_computation.1 | async-start | bytes 4751360 | tf_op jit(solution)/shard_map/all_to_all | solution.py:296
  102.9 13.6 %collective-permute-start.13 = (bf16[256,1792]{1,0:T(8,128)(2,1)S(1)}, bf16[256,1792]{1,0:T(8,128)(2,1)S(1)}, u32[]{:S(2)}, u32[]{:S(2)}) collective-permute-start(bf16[256,1792]{1,0:T(8,128)(2,1)S(1)} %collective-permute-done.11.refs_2_), channel_id=1, source_target_pairs={{0,8},{1,57},{8,16},{9,1},{16,24},{17,9},{24,32},{25,17},{32,40},{... | collective-permute-start | bytes 2752520 | tf_op jit(solution)/shard_map/ppermute | solution.py:284
  130.2 46.3 %all-to-all-start = ((bf16[8,40,5504]{2,1,0:T(8,128)(2,1)}), bf16[8,40,5504]{2,1,0:T(8,128)(2,1)}, u32[]{:S(2)}, u32[]{:S(2)}) async-start(bf16[8,40,5504]{2,1,0:T(8,128)(2,1)} %bitcast.10), calls=%async_computation | async-start | bytes 7045120 | tf_op jit(solution)/shard_map/all_to_all | solution.py:296
  151.1 25.5 %copy-start = (bf16[1,1,1280,1024]{3,2,1,0:T(8,128)(2,1)S(1)}, bf16[1,1,1280,1024]{3,2,1,0:T(8,128)(2,1)}, u32[]{:S(2)}) copy-start(bf16[1,1,1280,1024]{3,2,1,0:T(8,128)(2,1)} %param.9) | copy-start | bytes 7864324
  176.5 0.8 copy-start.2
  177.3 25.4 %copy-start.1 = (f32[1,128,8]{1,2,0:T(8,128)S(1)}, f32[1,128,8]{1,2,0:T(8,128)}, u32[]{:S(2)}) copy-start(f32[1,128,8]{1,2,0:T(8,128)} %param.7) | copy-start | bytes 12292
  177.3 25.4 %copy-start.3 = (s32[1,128,8]{1,2,0:T(8,128)S(1)}, s32[1,128,8]{1,2,0:T(8,128)}, u32[]{:S(2)}) copy-start(s32[1,128,8]{1,2,0:T(8,128)} %param.6) | copy-start | bytes 12292
